TPU v7x, 32 devices: a whole 2x2x4 slice. The times are simulated.
32 devices in a mesh: dp: 4 (over x, core), row: 4 (over z), col: 2 (over y).
Axes of the slice: x: 2, y: 2, z: 4, core: 2. Of those that a mesh axis runs over, the one named last changes fastest.
Arguments:
- states: bfloat16 [8192, 2048], P(('dp', 'row'), 'col'), may hold values from -6 to 6
- keep: int32 [8192], P(('dp', 'row')), may hold values 0 or 1
- cont_ids: int32 [4, 1024], P('dp'), may hold values from 0 to 3, never falling along the last dimension, each value on 1 to 512 neighbouring positions
- answer_len: int32 [4, 4], P('dp'), may hold values from 1 to 512
- teacher: bfloat16 [8192, 2048], P(('dp', 'row'), 'col'), may hold values from -6 to 6
- out_grad: bfloat16 [8192, 2048], P(('dp', 'row'), 'col'), may hold values from -6 to 6
- gain_attn: float32 [2048], P('col'), may hold values from 0.5 to 1.5
- w_query: bfloat16 [2048, 2048], P('col', 'row'), may hold values from -0.125 to 0.125
- key_projection: bfloat16 [2048, 512], P('col', 'row'), may hold values from -0.125 to 0.125
- value_projection: bfloat16 [2048, 512], P('col', 'row'), may hold values from -0.125 to 0.125
- w_out: bfloat16 [2048, 2048], P('row', 'col'), may hold values from -1.5 to 1.5
- gain_ffn: float32 [2048], P('col'), may hold values from 0.5 to 1.5
- w_gate: bfloat16 [2048, 5632], P('col', 'row'), may hold values from -0.125 to 0.125
- w_up: bfloat16 [2048, 5632], P('col', 'row'), may hold values from -0.125 to 0.125
- w_down: bfloat16 [5632, 2048], P('row', 'col'), may hold values from -0.078125 to 0.078125
Outputs:
- output: bfloat16 [8192, 2048], P(('dp', 'row'), 'col')
- loss: float32 [], replicated
- grad_states: float32 [8192, 2048], P(('dp', 'row'), 'col')
- grad_gain_attn: float32 [2048], P('col')
- grad_query: float32 [2048, 2048], P('col', 'row')
- grad_key: float32 [2048, 512], P('col', 'row')
- grad_value: float32 [2048, 512], P('col', 'row')
- grad_out: float32 [2048, 2048], P('row', 'col')
- grad_gain_ffn: float32 [2048], P('col')
- grad_gate: float32 [2048, 5632], P('col', 'row')
- grad_up: float32 [2048, 5632], P('col', 'row')
- grad_down: float32 [5632, 2048], P('row', 'col')
Inputs may be any that keep to these rules, and one draw needn't show every extreme that they name: `cont_ids`: in each group the continuation numbers never fall along the tokens, and each continuation has 1 to 512 tokens.
All inputs are finite; a program needn't handle non-finite values. No bound on the sum of `keep` on one device may be relied on, other than what follows from the above.
Results may differ from a plain program's by a relative error of at most 0.019.
Values may be sent and summed in bfloat16 or wider, within the bound.
No kernel may reach another device: no remote copies, remote signals or barrier semaphores. Data moves between devices by JAX's collectives and lax.ppermute only.
A program may use at most 192 MiB of HBM per device.

v0:
```python
import jax
import jax.numpy as jnp
from jax import lax
from jax.sharding import PartitionSpec as P

MODEL_WIDTH = 2048
HEAD_SIZE = 128
PROMPT = 1024


EPSILON = 1e-05
MASKED = -1e30
ROPE_BASE = 10000.0


def rows_of(values, start, count, axis=0):
    return lax.dynamic_slice_in_dim(values, start, count, axis)


def token_layout(cont_ids, answer_len):
    groups, cont_tokens = cont_ids.shape
    labels = jnp.arange(answer_len.shape[1], dtype=jnp.int32)
    starts = jnp.sum((cont_ids[:, None, :] < labels[None, :, None]).astype(jnp.int32), axis=2)
    member = (cont_ids[:, :, None] == labels[None, None, :]).astype(jnp.int32)
    own_start = jnp.sum(member * starts[:, None, :], axis=2)
    own_limit = jnp.sum(member * answer_len[:, None, :], axis=2)
    offset = jnp.arange(cont_tokens, dtype=jnp.int32)[None, :] - own_start
    prompt_pos = jnp.arange(PROMPT, dtype=jnp.int32)[None, :]
    positions = jnp.concatenate([prompt_pos, PROMPT + offset], axis=1).reshape(-1)
    segment = jnp.concatenate(
        [jnp.full((groups, PROMPT), -1, dtype=jnp.int32), cont_ids], axis=1
    ).reshape(-1)
    counted = jnp.concatenate(
        [jnp.ones((groups, PROMPT), jnp.int32), (offset < own_limit).astype(jnp.int32)], axis=1
    ).reshape(-1)
    return (positions, segment, counted)


def rotary(values, positions, sign):
    half = values.shape[-1] // 2
    freqs = ROPE_BASE ** (-2.0 * jnp.arange(half, dtype=jnp.float32) / values.shape[-1])
    angles = positions.astype(jnp.float32)[:, None] * freqs[None, :]
    cosine = jnp.cos(angles)[:, None, :]
    sine = sign * jnp.sin(angles)[:, None, :]
    first = values[..., :half]
    second = values[..., half:]
    return jnp.concatenate(
        [first * cosine - second * sine, second * cosine + first * sine], axis=-1
    )


def visible(query_index, query_segment, key_index, key_segment):
    earlier = key_index[None, :] <= query_index[:, None]
    shared = (key_segment[None, :] < 0) | (key_segment[None, :] == query_segment[:, None])
    return earlier & shared


def feature_sum(values):
    return lax.psum(values, "col")


def gather_rows(values):
    return lax.all_gather(values, "row", axis=0, tiled=True)


def gather_cols(values):
    return lax.all_gather(values, "col", axis=0, tiled=True)


def partial_cols(term, count):
    return lax.psum_scatter(
        term(jnp.int32(0), count * lax.axis_size("col")), "col", scatter_dimension=0, tiled=True
    )


def partial_rows(term, count):
    return lax.psum_scatter(
        term(jnp.int32(0), count * lax.axis_size("row")), "row", scatter_dimension=0, tiled=True
    )


def body(
    states,
    keep,
    cont_ids,
    answer_len,
    teacher,
    out_grad,
    gain_attn,
    w_query,
    key_projection,
    value_projection,
    w_out,
    gain_ffn,
    w_gate,
    w_up,
    w_down,
):
    local_rows = states.shape[0]
    whole_rows = local_rows * lax.axis_size("row")
    query_rows = whole_rows // lax.axis_size("col")
    group_tokens = PROMPT + cont_ids.shape[1]
    key_heads = key_projection.shape[1] // HEAD_SIZE
    heads_per_group = w_query.shape[1] // key_projection.shape[1]
    query_width = w_query.shape[1]
    scale = HEAD_SIZE ** (-0.5)
    block = min(512, query_rows)
    blocks = query_rows // block
    positions, segment, counted = token_layout(cont_ids, answer_len)
    token_index = jnp.arange(whole_rows, dtype=jnp.int32)
    row_start = lax.axis_index("row") * local_rows
    col_start = lax.axis_index("col") * query_rows
    counted_here = rows_of(counted, row_start, local_rows).astype(jnp.float32)[:, None]
    query_pos = rows_of(positions, col_start, query_rows)
    keep_here = keep.astype(jnp.float32)[:, None]
    states_f = states.astype(jnp.float32)
    scale_attn = lax.rsqrt(
        feature_sum(jnp.sum(states_f * states_f, axis=1)) / MODEL_WIDTH + EPSILON
    )[:, None]
    normed_attn = (states_f * scale_attn * gain_attn[None, :]).astype(jnp.bfloat16)
    normed_all = gather_rows(normed_attn)
    w_kv = jnp.concatenate([key_projection, value_projection], axis=1)
    query_raw = partial_cols(
        lambda start, count: jnp.dot(
            rows_of(normed_all, start, count), w_query, preferred_element_type=jnp.float32
        ),
        query_rows,
    )
    kv_raw = lax.psum(jnp.dot(normed_all, w_kv, preferred_element_type=jnp.float32), "col")
    queries = (
        rotary(
            query_raw.reshape(query_rows, key_heads * heads_per_group, HEAD_SIZE), query_pos, 1.0
        )
        .astype(jnp.bfloat16)
        .reshape(query_rows, key_heads, heads_per_group, HEAD_SIZE)
    )
    keys = rotary(
        kv_raw[:, : key_heads * HEAD_SIZE].reshape(whole_rows, key_heads, HEAD_SIZE), positions, 1.0
    ).astype(jnp.bfloat16)
    values = (
        kv_raw[:, key_heads * HEAD_SIZE :]
        .reshape(whole_rows, key_heads, HEAD_SIZE)
        .astype(jnp.bfloat16)
    )

    def context_of(index):
        first = col_start + index * block
        key_first = first // group_tokens * group_tokens
        query_block = rows_of(queries, index * block, block)
        key_group = rows_of(keys, key_first, group_tokens)
        value_group = rows_of(values, key_first, group_tokens)
        raw = (
            jnp.einsum("qgjd,kgd->gjqk", query_block, key_group, preferred_element_type=jnp.float32)
            * scale
        )
        mask = visible(
            rows_of(token_index, first, block),
            rows_of(segment, first, block),
            rows_of(token_index, key_first, group_tokens),
            rows_of(segment, key_first, group_tokens),
        )
        scores = jnp.where(mask[None, None], raw, MASKED)
        return (query_block, key_group, value_group, scores, key_first)

    def attend(index):
        query_block, key_group, value_group, scores, key_first = context_of(index)
        peak = jnp.max(scores, axis=-1, keepdims=True)
        exponent = jnp.exp(scores - peak)
        totals = jnp.sum(exponent, axis=-1, keepdims=True)
        weights = (exponent / totals).astype(jnp.bfloat16)
        mixed = jnp.einsum(
            "gjqk,kgd->qgjd", weights, value_group, preferred_element_type=jnp.float32
        )
        return (mixed, peak + jnp.log(totals))

    mixed_blocks, log_totals = lax.map(attend, jnp.arange(blocks, dtype=jnp.int32))
    attn_context = mixed_blocks.reshape(query_rows, query_width).astype(jnp.bfloat16)
    context_all = gather_cols(attn_context)
    attention = partial_rows(
        lambda start, count: jnp.dot(
            rows_of(context_all, start, count), w_out, preferred_element_type=jnp.float32
        ),
        local_rows,
    )
    hidden_res = states_f + keep_here * attention
    scale_ffn = lax.rsqrt(
        feature_sum(jnp.sum(hidden_res * hidden_res, axis=1)) / MODEL_WIDTH + EPSILON
    )[:, None]
    normed_ffn = (hidden_res * scale_ffn * gain_ffn[None, :]).astype(jnp.bfloat16)
    ffn_all = gather_rows(normed_ffn)
    w_pair = jnp.concatenate([w_gate, w_up], axis=1)
    inner = w_gate.shape[1]
    gate_up = partial_cols(
        lambda start, count: jnp.dot(
            rows_of(ffn_all, start, count), w_pair, preferred_element_type=jnp.float32
        ),
        query_rows,
    )
    gate = gate_up[:, :inner]
    up_proj = gate_up[:, inner:]
    sigma = jax.nn.sigmoid(gate)
    swish = gate * sigma
    hidden = (swish * up_proj).astype(jnp.bfloat16)
    hidden_all = gather_cols(hidden)
    feed = partial_rows(
        lambda start, count: jnp.dot(
            rows_of(hidden_all, start, count), w_down, preferred_element_type=jnp.float32
        ),
        local_rows,
    )
    result = hidden_res + keep_here * feed
    error = result - teacher.astype(jnp.float32)
    own_count = jnp.where(lax.axis_index("col") == 0, jnp.sum(counted_here), 0.0)
    error_total, token_count_sum = lax.psum(
        (jnp.sum(counted_here * error * error), own_count), ("dp", "row", "col")
    )
    loss = error_total / (token_count_sum * MODEL_WIDTH)
    grad_result = (
        out_grad.astype(jnp.float32) + 2.0 / (token_count_sum * MODEL_WIDTH) * counted_here * error
    )
    grad_feed = (keep_here * grad_result).astype(jnp.bfloat16)
    grad_feed_all = gather_rows(grad_feed)
    grad_down = jnp.einsum(
        "tf,td->fd", hidden_all, grad_feed_all, preferred_element_type=jnp.float32
    )
    grad_hidden = partial_cols(
        lambda start, count: jnp.einsum(
            "td,fd->tf",
            rows_of(grad_feed_all, start, count),
            w_down,
            preferred_element_type=jnp.float32,
        ),
        query_rows,
    )
    grad_gate_in = grad_hidden * up_proj * sigma * (1.0 + gate * (1.0 - sigma))
    grad_up_in = grad_hidden * swish
    grad_pair = jnp.concatenate([grad_gate_in, grad_up_in], axis=1).astype(jnp.bfloat16)
    grad_pair_all = gather_cols(grad_pair)
    grad_w_pair = jnp.einsum(
        "td,tf->df", ffn_all, grad_pair_all, preferred_element_type=jnp.float32
    )
    grad_normed_ffn = partial_rows(
        lambda start, count: jnp.einsum(
            "tf,df->td",
            rows_of(grad_pair_all, start, count),
            w_pair,
            preferred_element_type=jnp.float32,
        ),
        local_rows,
    )
    grad_gain_ffn = jnp.sum(grad_normed_ffn * hidden_res * scale_ffn, axis=0)
    weighted_ffn = grad_normed_ffn * gain_ffn[None, :]
    inner_ffn = feature_sum(jnp.sum(weighted_ffn * hidden_res, axis=1))[:, None]
    grad_hidden_res = (
        grad_result + scale_ffn * weighted_ffn - hidden_res * scale_ffn**3 * inner_ffn / MODEL_WIDTH
    )
    grad_attention = (keep_here * grad_hidden_res).astype(jnp.bfloat16)
    grad_att_all = gather_rows(grad_attention)
    grad_out = jnp.einsum(
        "to,td->od", context_all, grad_att_all, preferred_element_type=jnp.float32
    )
    grad_context = partial_cols(
        lambda start, count: jnp.einsum(
            "td,od->to",
            rows_of(grad_att_all, start, count),
            w_out,
            preferred_element_type=jnp.float32,
        ),
        query_rows,
    )
    grad_context = grad_context.astype(jnp.bfloat16).reshape(
        query_rows, key_heads, heads_per_group, HEAD_SIZE
    )

    def attend_back(carry, item):
        index, log_total = item
        query_block, key_group, value_group, scores, key_first = context_of(index)
        grad_block = rows_of(grad_context, index * block, block)
        probs = jnp.exp(scores - log_total)
        grad_probs = jnp.einsum(
            "qgjd,kgd->gjqk", grad_block, value_group, preferred_element_type=jnp.float32
        )
        row_dot = jnp.sum(probs * grad_probs, axis=-1, keepdims=True)
        grad_scores = (probs * (grad_probs - row_dot)).astype(jnp.bfloat16)
        grad_query_block = (
            jnp.einsum("gjqk,kgd->qgjd", grad_scores, key_group, preferred_element_type=jnp.float32)
            * scale
        )
        grad_key_group = (
            jnp.einsum(
                "gjqk,qgjd->kgd", grad_scores, query_block, preferred_element_type=jnp.float32
            )
            * scale
        )
        grad_value_group = jnp.einsum(
            "gjqk,qgjd->kgd",
            probs.astype(jnp.bfloat16),
            grad_block,
            preferred_element_type=jnp.float32,
        )
        pair = jnp.concatenate([grad_key_group, grad_value_group], axis=1)
        updated = rows_of(carry, key_first, group_tokens) + pair
        return (updated, grad_query_block)

    start_carry = jnp.zeros((whole_rows, 2 * key_heads, HEAD_SIZE), jnp.float32)
    grad_kv_part, grad_query_blocks = lax.scan(
        attend_back, start_carry, (jnp.arange(blocks, dtype=jnp.int32), log_totals)
    )
    grad_kv_sum = (
        lax.psum(
            grad_kv_part.reshape(whole_rows, 2 * key_heads * HEAD_SIZE).astype(jnp.bfloat16), "col"
        )
        .astype(jnp.float32)
        .reshape(whole_rows, 2 * key_heads, HEAD_SIZE)
    )
    grad_keys = rotary(grad_kv_sum[:, :key_heads], positions, -1.0)
    grad_kv = (
        jnp.concatenate([grad_keys, grad_kv_sum[:, key_heads:]], axis=1)
        .reshape(whole_rows, 2 * key_heads * HEAD_SIZE)
        .astype(jnp.bfloat16)
    )
    grad_queries = (
        rotary(
            grad_query_blocks.reshape(query_rows, key_heads * heads_per_group, HEAD_SIZE),
            query_pos,
            -1.0,
        )
        .reshape(query_rows, query_width)
        .astype(jnp.bfloat16)
    )
    grad_queries_all = gather_cols(grad_queries)
    grad_query = jnp.einsum(
        "td,tq->dq", normed_all, grad_queries_all, preferred_element_type=jnp.float32
    )
    grad_kv_weight = jnp.einsum(
        "td,tk->dk", normed_all, grad_kv, preferred_element_type=jnp.float32
    )
    grad_key = grad_kv_weight[:, : key_heads * HEAD_SIZE]
    grad_value = grad_kv_weight[:, key_heads * HEAD_SIZE :]

    def back_terms(start, count):
        from_queries = jnp.einsum(
            "tq,dq->td",
            rows_of(grad_queries_all, start, count),
            w_query,
            preferred_element_type=jnp.float32,
        )
        from_kv = jnp.einsum(
            "tk,dk->td", rows_of(grad_kv, start, count), w_kv, preferred_element_type=jnp.float32
        )
        return from_queries + from_kv

    grad_normed_attn = partial_rows(back_terms, local_rows)
    grad_gain_attn = jnp.sum(grad_normed_attn * states_f * scale_attn, axis=0)
    weighted_attn = grad_normed_attn * gain_attn[None, :]
    inner_attn = feature_sum(jnp.sum(weighted_attn * states_f, axis=1))[:, None]
    grad_states = (
        grad_hidden_res
        + scale_attn * weighted_attn
        - states_f * scale_attn**3 * inner_attn / MODEL_WIDTH
    )
    gain_attn_sum, gain_ffn_sum = lax.psum((grad_gain_attn, grad_gain_ffn), ("dp", "row"))
    summed = (
        lax.psum(grad_query.astype(jnp.bfloat16), "dp").astype(jnp.float32),
        lax.psum(grad_key.astype(jnp.bfloat16), "dp").astype(jnp.float32),
        lax.psum(grad_value.astype(jnp.bfloat16), "dp").astype(jnp.float32),
        lax.psum(grad_out.astype(jnp.bfloat16), "dp").astype(jnp.float32),
        lax.psum(grad_w_pair[:, :inner].astype(jnp.bfloat16), "dp").astype(jnp.float32),
        lax.psum(grad_w_pair[:, inner:].astype(jnp.bfloat16), "dp").astype(jnp.float32),
        lax.psum(grad_down.astype(jnp.bfloat16), "dp").astype(jnp.float32),
    )
    return (
        result.astype(jnp.bfloat16),
        loss,
        grad_states,
        gain_attn_sum,
        summed[0],
        summed[1],
        summed[2],
        summed[3],
        gain_ffn_sum,
        summed[4],
        summed[5],
        summed[6],
    )


def solution(mesh):
    return jax.shard_map(
        body,
        mesh=mesh,
        in_specs=(
            P(("dp", "row"), "col"),
            P(("dp", "row")),
            P("dp", None),
            P("dp", None),
            P(("dp", "row"), "col"),
            P(("dp", "row"), "col"),
            P("col"),
            P("col", "row"),
            P("col", "row"),
            P("col", "row"),
            P("row", "col"),
            P("col"),
            P("col", "row"),
            P("col", "row"),
            P("row", "col"),
        ),
        out_specs=(
            P(("dp", "row"), "col"),
            P(),
            P(("dp", "row"), "col"),
            P("col"),
            P("col", "row"),
            P("col", "row"),
            P("col", "row"),
            P("row", "col"),
            P("col"),
            P("col", "row"),
            P("col", "row"),
            P("row", "col"),
        ),
        check_vma=False,
    )
```

profile of v0, /device:TPU:0, one launch (start us, length us, event | category | flops | bytes accessed | tf_op | source)
XLA Modules:
  0.0 2396.0 jit_solution(15382242776699901373)
XLA Ops:
  8.9 5.9 psum.119
  20.5 80.6 %all-gather.9.cloned.1.call-done = bf16[2048,1024]{1,0:T(8,128)(2,1)} async-done(((bf16[512,1024]{1,0:T(8,128)(2,1)}), bf16[2048,1024]{1,0:T(8,128)(2,1)}) %all-gather.9.cloned.1.call-update) | async-done | bytes 4194320 | tf_op jit(solution)/shard_map/all_gather | solution.py:63
  106.0 6.8 fusion.91
  118.2 49.4 %all-reduce.9.cloned.1.call-done = f32[2048,256]{0,1:T(8,128)} async-done(((f32[2048,256]{0,1:T(8,128)}), f32[2048,256]{0,1:T(8,128)}) %all-reduce.9.cloned.1.call-update) | async-done | bytes 2097168 | tf_op jit(solution)/shard_map/psum | solution.py:129
  177.6 47.3 %reduce-scatter.9.cloned.1.call-done = f32[1024,512]{1,0:T(8,128)} async-done(((f32[2048,512]{1,0:T(8,128)}), f32[1024,512]{1,0:T(8,128)}) %reduce-scatter.9.cloned.1.call-update) | async-done | bytes 2097168 | tf_op jit(solution)/shard_map/reduce_scatter | solution.py:71
  233.5 36.7 %while.27 = (s32[]{:T(128)}, bf16[2,512,1,4,128]{4,1,3,2,0:T(8,128)(2,1)}, f32[2,1,4,512,1]{3,2,4,1,0:T(4,128)S(1)}, s32[2048]{0:T(1024)S(1)}, s32[2]{0:T(128)S(...) while((s32[]{:T(128)}, ...), condition=%wide.region_9.10_spmd.clone, body=%wide.region_6.9_spmd.clone.sunk | while | flops 2202009600 | bytes 65642824 | solution.py:176
  245.3 5.5 fusion.154
  263.7 5.5 fusion.154
  273.8 32.8 %all-gather.11.cloned.1.call-done = bf16[2048,512]{1,0:T(8,128)(2,1)} async-done(((bf16[1024,512]{1,0:T(8,128)(2,1)}), bf16[2048,512]{1,0:T(8,128)(2,1)}) %all-gather.11.cloned.1.call-update) | async-done | bytes 2097168 | tf_op jit(solution)/shard_map/all_gather | solution.py:67
  306.7 7.5 fusion.93
  314.8 144.0 %reduce-scatter.11.cloned.1.call-done = f32[512,1024]{1,0:T(8,128)} async-done(((f32[2048,1024]{1,0:T(8,128)}), f32[512,1024]{1,0:T(8,128)}) %reduce-scatter.11.cloned.1.call-update) | async-done | bytes 2097168 | tf_op jit(solution)/shard_map/reduce_scatter | solution.py:77
  475.8 76.0 %all-gather.13.cloned.1.call-done = bf16[2048,1024]{1,0:T(8,128)(2,1)} async-done(((bf16[512,1024]{1,0:T(8,128)(2,1)}), bf16[2048,1024]{1,0:T(8,128)(2,1)}) %all-gather.13.cloned.1.call-update) | async-done | bytes 4194320 | tf_op jit(solution)/shard_map/all_gather | solution.py:63
  551.8 19.7 fusion.94
  571.6 255.4 %reduce-scatter.13.cloned.1.call-done = f32[1024,2816]{1,0:T(8,128)} async-done(((f32[2048,2816]{1,0:T(8,128)}), f32[1024,2816]{1,0:T(8,128)}) %reduce-scatter.13.cloned.1.call-update) | async-done | bytes 11534352 | tf_op jit(solution)/shard_map/reduce_scatter | solution.py:71
  827.0 6.3 multiply_convert_fusion.2
  833.3 74.6 %all-gather.15.cloned.1.call-done = bf16[2048,1408]{1,0:T(8,128)(2,1)} async-done(((bf16[1024,1408]{1,0:T(8,128)(2,1)}), bf16[2048,1408]{1,0:T(8,128)(2,1)}) %all-gather.15.cloned.1.call-update) | async-done | bytes 5767184 | tf_op jit(solution)/shard_map/all_gather | solution.py:67
  907.9 10.7 fusion.95
  920.6 142.7 %reduce-scatter.15.cloned.1.call-done = f32[512,1024]{1,0:T(8,128)} async-done(((f32[2048,1024]{1,0:T(8,128)}), f32[512,1024]{1,0:T(8,128)}) %reduce-scatter.15.cloned.1.call-update) | async-done | bytes 2097168 | tf_op jit(solution)/shard_map/reduce_scatter | solution.py:77
  1068.3 41.1 %all-reduce.2 = (f32[]{:T(128)}, f32[]{:T(128)}) all-reduce(f32[]{:T(128)} %get-tuple-element.352, f32[]{:T(128)S(6)} %select_n.47), channel_id=1, replica_groups=mesh['dp'=4,'row'=4,'col'=2] {'dp','row','col'}, use_global_device_ids=true, to_apply=%region_17.18 | all-reduce | flops 2 | bytes 16 | tf_op jit(solution)/shard_map/psum | solution.py:214
  1113.8 80.8 %all-gather.17.cloned.1.call-done = bf16[2048,1024]{1,0:T(8,128)(2,1)} async-done(((bf16[512,1024]{1,0:T(8,128)(2,1)}), bf16[2048,1024]{1,0:T(8,128)(2,1)}) %all-gather.17.cloned.1.call-update) | async-done | bytes 4194320 | tf_op jit(solution)/shard_map/all_gather | solution.py:63
  1194.7 11.2 fusion.96
  1205.9 131.8 %reduce-scatter.17.cloned.1.call-done = f32[1024,1408]{1,0:T(8,128)} async-done(((f32[2048,1408]{1,0:T(8,128)}), f32[1024,1408]{1,0:T(8,128)}) %reduce-scatter.17.cloned.1.call-update) | async-done | bytes 5767184 | tf_op jit(solution)/shard_map/reduce_scatter | solution.py:71
  1337.7 7.4 multiply_convert_fusion.1
  1348.1 141.1 %all-gather.19.cloned.1.call-done = bf16[2048,2816]{1,0:T(8,128)(2,1)} async-done(((bf16[1024,2816]{1,0:T(8,128)(2,1)}), bf16[2048,2816]{1,0:T(8,128)(2,1)}) %all-gather.19.cloned.1.call-update) | async-done | bytes 11534352 | tf_op jit(solution)/shard_map/all_gather | solution.py:67
  1489.2 18.0 fusion.97
  1507.3 144.6 %reduce-scatter.19.cloned.1.call-done = f32[512,1024]{1,0:T(8,128)} async-done(((f32[2048,1024]{1,0:T(8,128)}), f32[512,1024]{1,0:T(8,128)}) %reduce-scatter.19.cloned.1.call-update) | async-done | bytes 2097168 | tf_op jit(solution)/shard_map/reduce_scatter | solution.py:77
  1659.5 5.5 multiply_convert_fusion.3
  1665.1 81.6 %all-gather.21.cloned.1.call-done = bf16[2048,1024]{1,0:T(8,128)(2,1)} async-done(((bf16[512,1024]{1,0:T(8,128)(2,1)}), bf16[2048,1024]{1,0:T(8,128)(2,1)}) %all-gather.21.cloned.1.call-update) | async-done | bytes 4194320 | tf_op jit(solution)/shard_map/all_gather | solution.py:63
  1746.7 6.9 fusion.98
  1753.7 10.9 convolution_convert_fusion.1
  1764.5 42.0 %reduce-scatter.21.cloned.1.call-done = f32[1024,512]{1,0:T(8,128)} async-done(((f32[2048,512]{1,0:T(8,128)}), f32[1024,512]{1,0:T(8,128)}) %reduce-scatter.21.cloned.1.call-update) | async-done | bytes 2097168 | tf_op jit(solution)/shard_map/reduce_scatter | solution.py:71
  1809.4 100.4 %while.28 = (s32[]{:T(128)}, f32[2048,2,128]{0,2,1:T(8,128)}, f32[2,512,1,4,128]{4,1,0,3,2:T(8,128)}, s32[2]{0:T(128)S(1)}, bf16[1024,1,4,128]{3,0,2,1:T(8,128)(...) while((s32[]{:T(128)}, f32[2048,2,128]{0,2,1:T(8,128)}, ...), condition=%wide.region_27.28_spmd.clone.clone, body=%wide.region_25.27_spmd.clone.clone.sunk | while | flops 5437915136 | bytes 244941232 | solution.py:306
  1817.1 5.8 copy-done.2
  1822.9 5.1 fusion.163
  1828.0 12.1 fusion.164
  1840.1 12.1 fusion.165
  1867.0 5.8 copy-done.2
  1872.8 5.1 fusion.163
  1877.9 12.1 fusion.164
  1889.9 12.1 fusion.165
  1912.6 19.1 convolution_convert_fusion
  1934.5 5.8 fusion.88
  1943.6 9.2 all-reduce.11.cloned.1.call-done
  1959.2 28.7 %all-gather.23.cloned.1.call-done = bf16[2048,512]{0,1:T(8,128)(2,1)} async-done(((bf16[1024,512]{0,1:T(8,128)(2,1)}), bf16[2048,512]{0,1:T(8,128)(2,1)}) %all-gather.23.cloned.1.call-update) | async-done | bytes 2097168 | tf_op jit(solution)/shard_map/all_gather | solution.py:67
  1987.9 6.2 convolution_convert_fusion.3
  2004.7 191.2 %all-reduce.13.cloned.1.call-done = (bf16[1024,512]{1,0:T(8,128)(2,1)}, bf16[1024,128]{1,0:T(8,128)(2,1)}, bf16[1024,128]{1,0:T(8,128)(2,1)}, bf16[512,1024]{1,0...) async-done(((bf16[1024,512]{1,0:T(8,128)(2,1)}, bf16[1024,128]{1,0:T(8,128)(2,1)}, bf16[1024,128]{1,0:T(8,128)(2,1)}, ...) | async-done | bytes 11272208 | tf_op jit(solution)/shard_map/psum | solution.py:364
  2214.1 128.9 %reduce-scatter.23.cloned.1.call-done = f32[512,1024]{1,0:T(8,128)} async-done(((f32[2048,1024]{1,0:T(8,128)}), f32[512,1024]{1,0:T(8,128)}) %reduce-scatter.23.cloned.1.call-update) | async-done | bytes 2097168 | tf_op jit(solution)/shard_map/reduce_scatter | solution.py:77
  2350.2 33.3 %all-reduce.3 = (f32[1024]{0:T(1024)}, f32[1024]{0:T(1024)}) all-reduce(f32[1024]{0:T(1024)S(1)} %get-tuple-element.289, f32[1024]{0:T(1024)S(1)} %copy-done.33), channel_id=1, replica_groups=mesh['dp'=4,'row'=4,'col'=2] {'dp','row'}, use_global_device_ids=true, to_apply=%region_33.34 | all-reduce | flops 2048 | bytes 16384 | tf_op jit(solution)/shard_map/psum | solution.py:362
  (252 shorter events, 188.9 us)
Async XLA Ops:
  7.2 900.8 %copy-start = (bf16[1408,1024]{1,0:T(8,128)(2,1)S(1)}, bf16[1408,1024]{1,0:T(8,128)(2,1)}, u32[]{:S(2)}) copy-start(bf16[1408,1024]{1,0:T(8,128)(2,1)} %param.33) | copy-start | bytes 8650756
  7.2 94.0 %all-gather.9.cloned.1.call-start = ((), (), s32[]{:S(2)}) async-start(), calls=%async_computation.8 | async-start | bytes 5242880 | tf_op jit(solution)/shard_map/all_gather | solution.py:63
  18.5 149.1 %all-reduce.9.cloned.1.call-start = ((), (), s32[]{:S(2)}) async-start(), calls=%async_computation.10 | async-start | bytes 4194304 | tf_op jit(solution)/shard_map/psum | solution.py:129
  20.5 85.4 %copy-start.19 = (bf16[1024,256]{1,0:T(8,128)(2,1)}, bf16[1024,256]{1,0:T(8,128)(2,1)S(1)}, u32[]{:S(2)}) copy-start(bf16[1024,256]{1,0:T(8,128)(2,1)S(1)} %constant_dynamic-update-slice_fusion) | copy-start | bytes 1572868
  106.0 118.9 %reduce-scatter.9.cloned.1.call-start = ((), (), s32[]{:S(2)}) async-start(), calls=%async_computation.9 | async-start | bytes 6291456 | tf_op jit(solution)/shard_map/reduce_scatter | solution.py:71
  112.9 193.8 %all-gather.11.cloned.1.call-start = ((), (), s32[]{:S(2)}) async-start(), calls=%async_computation.11 | async-start | bytes 3145728 | tf_op jit(solution)/shard_map/all_gather | solution.py:67
  113.6 58.7 %copy-start.36 = (f32[64]{0:T(128)}, f32[64]{0:T(128)S(1)}, u32[]{:S(2)}) copy-start(f32[64]{0:T(128)S(1)} %multiply_power_fusion) | copy-start | bytes 772
  115.0 57.3 %copy-start.24 = (f32[1,2048]{1,0:T(1,128)}, f32[1,2048]{1,0:T(1,128)S(1)}, u32[]{:S(2)}) copy-start(f32[1,2048]{1,0:T(1,128)S(1)} %add_convert_fusion.2) | copy-start | bytes 24580
  240.9 4.5 copy-start.22
  259.2 4.5 copy-start.22
  273.4 185.4 %reduce-scatter.11.cloned.1.call-start = ((), (), s32[]{:S(2)}) async-start(), calls=%async_computation.12 | async-start | bytes 10485760 | tf_op jit(solution)/shard_map/reduce_scatter | solution.py:77
  314.2 153.1 %copy-start.27 = (f32[1024]{0:T(1024)S(1)}, f32[1024]{0:T(1024)}, u32[]{:S(2)}) copy-start(f32[1024]{0:T(1024)} %param.30) | copy-start | bytes 12292
  314.2 237.6 %all-gather.13.cloned.1.call-start = ((), (), s32[]{:S(2)}) async-start(), calls=%async_computation.13 | async-start | bytes 5242880 | tf_op jit(solution)/shard_map/all_gather | solution.py:63
  470.2 356.8 %reduce-scatter.13.cloned.1.call-start = ((), (), s32[]{:S(2)}) async-start(), calls=%async_computation.14 | async-start | bytes 34603008 | tf_op jit(solution)/shard_map/reduce_scatter | solution.py:71
  571.6 336.4 %all-gather.15.cloned.1.call-start = ((), (), s32[]{:S(2)}) async-start(), calls=%async_computation.15 | async-start | bytes 8650752 | tf_op jit(solution)/shard_map/all_gather | solution.py:67
  833.3 230.0 %reduce-scatter.15.cloned.1.call-start = ((), (), s32[]{:S(2)}) async-start(), calls=%async_computation.16 | async-start | bytes 10485760 | tf_op jit(solution)/shard_map/reduce_scatter | solution.py:77
  918.6 276.0 %all-gather.17.cloned.1.call-start = ((), (), s32[]{:S(2)}) async-start(), calls=%async_computation.17 | async-start | bytes 5242880 | tf_op jit(solution)/shard_map/all_gather | solution.py:63
  1113.8 223.9 %reduce-scatter.17.cloned.1.call-start = ((), (), s32[]{:S(2)}) async-start(), calls=%async_computation.18 | async-start | bytes 17301504 | tf_op jit(solution)/shard_map/reduce_scatter | solution.py:71
  1205.8 283.3 %all-gather.19.cloned.1.call-start = ((), (), s32[]{:S(2)}) async-start(), calls=%async_computation.19 | async-start | bytes 17301504 | tf_op jit(solution)/shard_map/all_gather | solution.py:67
  1348.0 303.8 %reduce-scatter.19.cloned.1.call-start = ((), (), s32[]{:S(2)}) async-start(), calls=%async_computation.20 | async-start | bytes 10485760 | tf_op jit(solution)/shard_map/reduce_scatter | solution.py:77
  1507.2 144.7 %copy-start.5 = (f32[512,1024]{1,0:T(8,128)S(1)}, f32[512,1024]{1,0:T(8,128)}, u32[]{:S(2)}) copy-start(f32[512,1024]{1,0:T(8,128)} %get-tuple-element.355) | copy-start | bytes 6291460
  1507.2 239.5 %all-gather.21.cloned.1.call-start = ((), (), s32[]{:S(2)}) async-start(), calls=%async_computation.21 | async-start | bytes 5242880 | tf_op jit(solution)/shard_map/all_gather | solution.py:63
  1665.0 141.5 %reduce-scatter.21.cloned.1.call-start = ((), (), s32[]{:S(2)}) async-start(), calls=%async_computation.22 | async-start | bytes 6291456 | tf_op jit(solution)/shard_map/reduce_scatter | solution.py:71
  1753.6 199.1 %all-reduce.11.cloned.1.call-start = ((), (), s32[]{:S(2)}) async-start(), calls=%async_computation.24 | async-start | bytes 2097152 | tf_op jit(solution)/shard_map/psum | solution.py:310
  1764.5 44.9 %copy-start.7 = (bf16[2048,1,128]{2,0,1:T(8,128)(2,1)S(1)}, bf16[2048,1,128]{2,0,1:T(8,128)(2,1)}, u32[]{:S(2)}) copy-start(bf16[2048,1,128]{2,0,1:T(8,128)(2,1)} %get-tuple-element.662) | copy-start | bytes 1572868
  1817.1 5.8 copy-start.2
  1867.0 5.8 copy-start.2
  1912.5 19.2 copy-start.12
  1912.6 19.2 copy-start.17
  1912.6 75.3 %all-gather.23.cloned.1.call-start = ((), (), s32[]{:S(2)}) async-start(), calls=%async_computation.23 | async-start | bytes 3145728 | tf_op jit(solution)/shard_map/all_gather | solution.py:67
  1912.6 19.1 copy-start.10
  1934.4 5.9 copy-start.42
  1934.4 261.5 %all-reduce.13.cloned.1.call-start = ((), (), s32[]{:S(2)}) async-start(), calls=%async_computation.26 | async-start | bytes 22544384 | tf_op jit(solution)/shard_map/psum | solution.py:364
  1934.4 5.8 copy-start.41
  1943.6 10.8 copy-start.25
  1943.6 10.8 copy-start.37
  1952.7 4.2 slice-start
  1952.7 4.3 copy-start.40
  1994.1 5.2 copy-start.20
  1994.1 348.8 %reduce-scatter.23.cloned.1.call-start = ((), (), s32[]{:S(2)}) async-start(), calls=%async_computation.25 | async-start | bytes 10485760 | tf_op jit(solution)/shard_map/reduce_scatter | solution.py:77
  2195.9 6.6 copy-start.21
  2199.5 4.6 copy-start.16
  2210.8 132.1 %copy-start.6 = (bf16[512,1024]{1,0:T(8,128)(2,1)S(1)}, bf16[512,1024]{1,0:T(8,128)(2,1)}, u32[]{:S(2)}) copy-start(bf16[512,1024]{1,0:T(8,128)(2,1)} %param.19) | copy-start | bytes 3145732
  2210.8 132.1 %copy-start.26 = (f32[1024]{0:T(1024)S(1)}, f32[1024]{0:T(1024)}, u32[]{:S(2)}) copy-start(f32[1024]{0:T(1024)} %param.25) | copy-start | bytes 12292
  2210.8 132.1 %copy-start.32 = (f32[512]{0:T(512)S(1)}, f32[512]{0:T(512)}, u32[]{:S(2)}) copy-start(f32[512]{0:T(512)} %copy-done.31) | copy-start | bytes 6148
  2214.1 136.1 %copy-start.33 = (f32[1024]{0:T(1024)S(1)}, f32[1024]{0:T(1024)}, u32[]{:S(2)}) copy-start(f32[1024]{0:T(1024)} %get-tuple-element.287) | copy-start | bytes 12292
  2214.1 169.4 %copy-start.35 = (f32[512]{0:T(512)S(1)}, f32[512]{0:T(512)}, u32[]{:S(2)}) copy-start(f32[512]{0:T(512)} %get-tuple-element.380) | copy-start | bytes 6148
  2383.5 4.6 copy-start.1
  (23 other events, 40.7 us)
Sparse Core Ops, SparseCore 0:
  18.6 82.5 all-gather.8
  106.1 61.4 all-reduce.8
  170.6 54.3 reduce-scatter.8
  273.5 33.1 all-gather.10
  314.3 144.4 reduce-scatter.10
  470.3 81.4 all-gather.12
  571.7 255.2 reduce-scatter.12
  833.4 74.4 all-gather.14
  918.8 144.4 reduce-scatter.14
  1113.9 80.7 all-gather.16
  1206.0 131.6 reduce-scatter.16
  1348.1 141.0 all-gather.18
  1507.3 144.4 reduce-scatter.18
  1665.2 81.4 all-gather.20
  1753.7 52.8 reduce-scatter.20
  1912.7 40.0 all-reduce.10
  1954.7 33.1 all-gather.22
  1994.2 201.6 all-reduce.12
  2198.2 144.6 reduce-scatter.22
where the time goes:
time: 2400 us
  waiting for transfers between devices  1880 us (78%)
  matrix products  207 us (9%)
  other arithmetic  128 us (5%)
  blocking collectives  95.1 us (4%)
  local copies, waits for them, and re-layouts  60.3 us (3%)
    reduce_scatter x4, waiting for transfers between devices, partial_rows(): lax.psum_scatter(term(jnp.int32(0), count * lax.axis_size('row')), 'row',...  560 us
    reduce_scatter x4, waiting for transfers between devices, partial_cols(): lax.psum_scatter(term(jnp.int32(0), count * lax.axis_size('col')), 'col',...  477 us
    all_gather x4, waiting for transfers between devices, gather_rows(): return lax.all_gather(values, 'row', axis=0, tiled=True)  319 us
    all_gather x4, waiting for transfers between devices, gather_cols(): return lax.all_gather(values, 'col', axis=0, tiled=True)  277 us
    psum x1, waiting for transfers between devices, body(): lax.psum(grad_query.astype(jnp.bfloat16), 'dp').astype(jnp.float32)  191 us
    psum x1, waiting for transfers between devices, body(): lax.psum(jnp.dot(normed_all, w_kv, preferred_element_type=jnp.float32), '...  49.4 us
  transfers between devices with their start and end apart: 19, of which 19 were waited for; matrix products, arithmetic and copies ran while one was open for 4% of the time, Pallas kernels for 0%

commit v1 on v0

--- a/solution.py
+++ b/solution.py
@@ -1,6 +1,10 @@
+import functools
+
 import jax
 import jax.numpy as jnp
 from jax import lax
+from jax.experimental import pallas as pl
+from jax.experimental.pallas import tpu as pltpu
 from jax.sharding import PartitionSpec as P
 
 MODEL_WIDTH = 2048
@@ -385,9 +389,553 @@
     )
 
 
+LOG2E = 1.4426950408889634
+VMEM_BYTES = 58 << 20
+ORDER = (0, 2, 1, 3)
+
+
+def swap(values, axis, mask):
+    size = lax.axis_size(axis)
+    return lax.ppermute(values, axis, [(i, i ^ mask) for i in range(size)])
+
+
+def xor_order(slots, mask):
+    bit = 1
+    while bit < len(slots):
+        odd = (mask & bit) != 0
+        slots = [jnp.where(odd, slots[i ^ bit], slots[i]) for i in range(len(slots))]
+        bit *= 2
+    return slots
+
+
+def low(values):
+    return values.astype(jnp.bfloat16)
+
+
+def wide(values):
+    return values.astype(jnp.float32)
+
+
+def dot_nn(left, right):
+    return lax.dot_general(left, right, (((1,), (0,)), ((), ())), preferred_element_type=jnp.float32)
+
+
+def dot_nt(left, right):
+    return lax.dot_general(left, right, (((1,), (1,)), ((), ())), preferred_element_type=jnp.float32)
+
+
+def dot_tn(left, right):
+    return lax.dot_general(left, right, (((0,), (0,)), ((), ())), preferred_element_type=jnp.float32)
+
+
+def attend_kernel(slots, scale, flags, q_ref, qseg_ref, kseg_ref, *refs):
+    kv_refs = refs[:slots]
+    o_ref, lse_ref, peak_ref, total_ref, acc_ref = refs[slots:]
+    query = q_ref[...]
+    rows = query.shape[0]
+
+    def scores(slot):
+        return dot_nt(kv_refs[slot][:, :HEAD_SIZE], query) * (scale * LOG2E)
+
+    def seen(slot):
+        key_seg = kseg_ref[slot * rows : (slot + 1) * rows, :]
+        return (key_seg < 0) | (key_seg == qseg_ref[...])
+
+    def add(slot, s):
+        peak = peak_ref[...]
+        higher = jnp.maximum(peak, jnp.max(s, axis=0, keepdims=True))
+        fade = jnp.exp2(peak - higher)
+        e = jnp.exp2(s - higher)
+        total_ref[...] = total_ref[...] * fade + jnp.sum(e, axis=0, keepdims=True)
+        acc_ref[...] = acc_ref[...] * fade + dot_tn(kv_refs[slot][:, HEAD_SIZE:], low(e))
+        peak_ref[...] = higher
+
+    key_index = lax.broadcasted_iota(jnp.int32, (rows, rows), 0)
+    query_index = lax.broadcasted_iota(jnp.int32, (rows, rows), 1)
+    s = jnp.where((key_index <= query_index) & seen(0), scores(0), MASKED)
+    peak = jnp.max(s, axis=0, keepdims=True)
+    e = jnp.exp2(s - peak)
+    peak_ref[...] = peak
+    total_ref[...] = jnp.sum(e, axis=0, keepdims=True)
+    acc_ref[...] = dot_tn(kv_refs[0][:, HEAD_SIZE:], low(e))
+    for slot in range(1, slots):
+
+        @pl.when(flags[slot] == 1)
+        def _(slot=slot):
+            add(slot, scores(slot))
+
+        @pl.when(flags[slot] == 2)
+        def _(slot=slot):
+            add(slot, jnp.where(seen(slot), scores(slot), MASKED))
+
+    o_ref[...] = low(jnp.transpose(acc_ref[...] / total_ref[...]))
+    lse_ref[0] = peak_ref[...] + jnp.log2(total_ref[...])
+
+
+def attend_back_kernel(slots, scale, flags, q_ref, do_ref, lse_ref, cos_ref, sin_ref, qseg_ref, kseg_ref, *refs):
+    kv_refs = refs[:slots]
+    dq_ref = refs[slots]
+    dkv_refs = refs[slots + 1 : 2 * slots + 1]
+    p_ref, dp_ref, dot_ref, dq_acc, dkv_acc = refs[2 * slots + 1 :]
+    step, steps = pl.program_id(1), pl.num_programs(1)
+    query, grad = q_ref[...], do_ref[...]
+    rows = query.shape[0]
+
+    @pl.when(step == 0)
+    def _():
+        dkv_acc[...] = jnp.zeros_like(dkv_acc)
+
+    def seen(slot):
+        key_seg = kseg_ref[slot * rows : (slot + 1) * rows, :]
+        return (key_seg < 0) | (key_seg == qseg_ref[...])
+
+    def first(slot, mask):
+        e = jnp.exp2(dot_nt(kv_refs[slot][:, :HEAD_SIZE], query) * (scale * LOG2E) - lse_ref[0])
+        if mask is not None:
+            e = jnp.where(mask, e, 0.0)
+        dp = dot_nt(kv_refs[slot][:, HEAD_SIZE:], grad)
+        p_ref[slot] = e
+        dp_ref[slot] = dp
+        part = jnp.sum(e * dp, axis=0, keepdims=True)
+        if slot == 0:
+            dot_ref[...] = part
+        else:
+            dot_ref[...] += part
+
+    def second(slot):
+        p = p_ref[slot]
+        ds = low(p * (dp_ref[slot] - dot_ref[...]))
+        dkv_acc[slot, :, :HEAD_SIZE] += dot_nn(ds, query)
+        dkv_acc[slot, :, HEAD_SIZE:] += dot_nn(low(p), grad)
+        part = dot_tn(kv_refs[slot][:, :HEAD_SIZE], ds)
+        if slot == 0:
+            dq_acc[...] = part
+        else:
+            dq_acc[...] += part
+
+    key_index = lax.broadcasted_iota(jnp.int32, (rows, rows), 0)
+    query_index = lax.broadcasted_iota(jnp.int32, (rows, rows), 1)
+    first(0, (key_index <= query_index) & seen(0))
+    for slot in range(1, slots):
+
+        @pl.when(flags[slot] == 1)
+        def _(slot=slot):
+            first(slot, None)
+
+        @pl.when(flags[slot] == 2)
+        def _(slot=slot):
+            first(slot, seen(slot))
+
+    second(0)
+    for slot in range(1, slots):
+
+        @pl.when(flags[slot] > 0)
+        def _(slot=slot):
+            second(slot)
+
+    half = HEAD_SIZE // 2
+    upper, lower = dq_acc[:half, :] * scale, dq_acc[half:, :] * scale
+    cosine, sine = cos_ref[...], sin_ref[...]
+    turned = jnp.concatenate([upper * cosine + lower * sine, lower * cosine - upper * sine], axis=0)
+    dq_ref[...] = low(jnp.transpose(turned))
+
+    @pl.when(step == steps - 1)
+    def _():
+        for slot in range(slots):
+            out = dkv_refs[slot]
+            out[:, :HEAD_SIZE] = (dkv_acc[slot, :, :HEAD_SIZE] * scale).astype(out.dtype)
+            out[:, HEAD_SIZE:] = dkv_acc[slot, :, HEAD_SIZE:].astype(out.dtype)
+
+
+def attend(flags, queries, query_seg, key_seg, key_values):
+    rows, width = queries.shape
+    slots, groups = len(key_values), key_values[0].shape[1] // (2 * HEAD_SIZE)
+    share = width // HEAD_SIZE // groups
+    whole = lambda g, m, f: (0, 0)
+    head = lambda g, m, f: (0, m * groups + g)
+    return pl.pallas_call(
+        functools.partial(attend_kernel, slots, HEAD_SIZE ** (-0.5)),
+        out_shape=(
+            jax.ShapeDtypeStruct((rows, width), jnp.bfloat16),
+            jax.ShapeDtypeStruct((share * groups, 1, rows), jnp.float32),
+        ),
+        grid_spec=pltpu.PrefetchScalarGridSpec(
+            num_scalar_prefetch=1,
+            grid=(groups, share),
+            in_specs=[
+                pl.BlockSpec((rows, HEAD_SIZE), head),
+                pl.BlockSpec((1, rows), whole),
+                pl.BlockSpec((slots * rows, 1), whole),
+            ]
+            + [pl.BlockSpec((rows, 2 * HEAD_SIZE), lambda g, m, f: (0, g))] * slots,
+            out_specs=(
+                pl.BlockSpec((rows, HEAD_SIZE), head),
+                pl.BlockSpec((1, 1, rows), lambda g, m, f: (m * groups + g, 0, 0)),
+            ),
+            scratch_shapes=[
+                pltpu.VMEM((1, rows), jnp.float32),
+                pltpu.VMEM((1, rows), jnp.float32),
+                pltpu.VMEM((HEAD_SIZE, rows), jnp.float32),
+            ],
+        ),
+        compiler_params=pltpu.CompilerParams(vmem_limit_bytes=VMEM_BYTES),
+        cost_estimate=pl.CostEstimate(
+            flops=3 * rows * rows * width * 4, transcendentals=3 * rows * rows * share * groups, bytes_accessed=8 << 20
+        ),
+        name="attend",
+    )(flags, queries, query_seg, key_seg, *key_values)
+
+
+def attend_back(flags, queries, grads, lse, cosine, sine, query_seg, key_seg, key_values):
+    rows, width = queries.shape
+    slots, groups = len(key_values), key_values[0].shape[1] // (2 * HEAD_SIZE)
+    share = width // HEAD_SIZE // groups
+    whole = lambda g, m, f: (0, 0)
+    head = lambda g, m, f: (0, m * groups + g)
+    pair = pl.BlockSpec((rows, 2 * HEAD_SIZE), lambda g, m, f: (0, g))
+    return pl.pallas_call(
+        functools.partial(attend_back_kernel, slots, HEAD_SIZE ** (-0.5)),
+        out_shape=(
+            jax.ShapeDtypeStruct((rows, width), jnp.bfloat16),
+            jax.ShapeDtypeStruct(key_values[0].shape, jnp.float32),
+        )
+        + (jax.ShapeDtypeStruct(key_values[0].shape, jnp.bfloat16),) * (slots - 1),
+        grid_spec=pltpu.PrefetchScalarGridSpec(
+            num_scalar_prefetch=1,
+            grid=(groups, share),
+            in_specs=[
+                pl.BlockSpec((rows, HEAD_SIZE), head),
+                pl.BlockSpec((rows, HEAD_SIZE), head),
+                pl.BlockSpec((1, 1, rows), lambda g, m, f: (m * groups + g, 0, 0)),
+                pl.BlockSpec((HEAD_SIZE // 2, rows), whole),
+                pl.BlockSpec((HEAD_SIZE // 2, rows), whole),
+                pl.BlockSpec((1, rows), whole),
+                pl.BlockSpec((slots * rows, 1), whole),
+            ]
+            + [pair] * slots,
+            out_specs=(pl.BlockSpec((rows, HEAD_SIZE), head),) + (pair,) * slots,
+            scratch_shapes=[
+                pltpu.VMEM((slots, rows, rows), jnp.float32),
+                pltpu.VMEM((slots, rows, rows), jnp.float32),
+                pltpu.VMEM((1, rows), jnp.float32),
+                pltpu.VMEM((HEAD_SIZE, rows), jnp.float32),
+                pltpu.VMEM((slots, rows, 2 * HEAD_SIZE), jnp.float32),
+            ],
+        ),
+        compiler_params=pltpu.CompilerParams(vmem_limit_bytes=VMEM_BYTES),
+        cost_estimate=pl.CostEstimate(
+            flops=3 * rows * rows * width * 10, transcendentals=3 * rows * rows * share * groups, bytes_accessed=12 << 20
+        ),
+        name="attend_back",
+    )(flags, queries, grads, lse, cosine, sine, query_seg, key_seg, *key_values)
+
+
+def feed_kernel(a_ref, wg_ref, wu_ref, wd_ref, gate_ref, up_ref, hid_ref, out_ref):
+    gate = dot_nt(a_ref[...], wg_ref[...])
+    up = dot_nt(a_ref[...], wu_ref[...])
+    hid = low(gate * jax.nn.sigmoid(gate) * up)
+    gate_ref[...] = gate
+    up_ref[...] = up
+    hid_ref[...] = hid
+    out_ref[...] = low(dot_nn(hid, wd_ref[...]))
+
+
+def feed_back_kernel(gm_ref, gate_ref, up_ref, wg_ref, wu_ref, wd_ref, dgate_ref, dup_ref, out_ref):
+    dhid = dot_nt(gm_ref[...], wd_ref[...])
+    gate, up = gate_ref[...], up_ref[...]
+    sigma = jax.nn.sigmoid(gate)
+    dgate = low(dhid * up * sigma * (1.0 + gate * (1.0 - sigma)))
+    dup = low(dhid * (gate * sigma))
+    dgate_ref[...] = dgate
+    dup_ref[...] = dup
+    out_ref[...] = low(dot_nn(dgate, wg_ref[...]) + dot_nn(dup, wu_ref[...]))
+
+
+def feed_call(kernel, name, wide_in, narrow_in, weights, narrow_out, rows=256):
+    tokens, features = wide_in.shape
+    hidden = weights[0].shape[0]
+    by_rows = lambda width: pl.BlockSpec((rows, width), lambda i: (i, 0))
+    fixed = pl.BlockSpec((hidden, features), lambda i: (0, 0), pipeline_mode=pl.Buffered(1))
+    return pl.pallas_call(
+        kernel,
+        out_shape=tuple(jax.ShapeDtypeStruct((tokens, hidden), t) for t in narrow_out)
+        + (jax.ShapeDtypeStruct((tokens, features), jnp.bfloat16),),
+        grid=(tokens // rows,),
+        in_specs=[by_rows(features)] + [by_rows(hidden) for _ in narrow_in] + [fixed] * len(weights),
+        out_specs=tuple(by_rows(hidden) for _ in narrow_out) + (by_rows(features),),
+        compiler_params=pltpu.CompilerParams(vmem_limit_bytes=VMEM_BYTES),
+        cost_estimate=pl.CostEstimate(
+            flops=6 * tokens * hidden * features, transcendentals=tokens * hidden, bytes_accessed=40 << 20
+        ),
+        name=name,
+    )(wide_in, *narrow_in, *weights)
+
+
+def feed(tokens, wg, wu, wd):
+    return feed_call(feed_kernel, "feed", tokens, [], [wg, wu, wd], (jnp.float32, jnp.float32, jnp.bfloat16))
+
+
+def feed_back(grads, gate, up, wg, wu, wd):
+    return feed_call(feed_back_kernel, "feed_back", grads, [gate, up], [wg, wu, wd], (jnp.bfloat16, jnp.bfloat16))
+
+
+def plane_gather(x):
+    half = x.shape[0] // 2
+    a, b = x[:half], x[half:]
+    a_x = swap(a, "dp", 2)
+    b_y = swap(b, "col", 1)
+    a_y = swap(jnp.concatenate([a, a_x], axis=0), "col", 1)
+    b_x = swap(jnp.concatenate([b, b_y], axis=1), "dp", 2)
+    pieces = [x, a_x, b_y, a_y, b_x]
+    sides = []
+    for x_, a_x_, b_y_, a_y_, b_x_ in (pieces, [swap(piece, "dp", 1) for piece in pieces]):
+        own = jnp.concatenate([x_, a_x_, b_x_[:, : x.shape[1]]], axis=0)
+        other = jnp.concatenate([a_y_[:half], b_y_, a_y_[half:], b_x_[:, x.shape[1] :]], axis=0)
+        sides.append(jnp.concatenate([own, other], axis=1))
+    return jnp.concatenate(sides, axis=0)
+
+
+def plane_scatter(p):
+    rows, width = p.shape[0] // 2, p.shape[1] // 2
+    half = rows // 4
+    q = wide(p[:rows]) + wide(swap(p[rows:], "dp", 1))
+    a_x = swap(low(q[2 * half : 3 * half]), "dp", 2)
+    b_y = swap(low(jnp.concatenate([q[half : 2 * half, width:], q[3 * half :, width:]], axis=0)), "col", 1)
+    a = q[:half] + wide(a_x)
+    b = jnp.concatenate([q[half : 2 * half, :width], q[3 * half :, :width]], axis=0) + wide(b_y)
+    a_y = swap(low(a[:, width:]), "col", 1)
+    b_x = swap(low(b[half:]), "dp", 2)
+    return jnp.concatenate([a[:, :width] + wide(a_y), b[:half] + wide(b_x)], axis=0)
+
+
+def dp_slots(x):
+    far = swap(x, "dp", 2)
+    return [x, swap(x, "dp", 1), far, swap(far, "dp", 1)]
+
+
+def home(slots, order):
+    odd = swap(low(jnp.concatenate([slots[1], slots[3]], axis=0)), "dp", 1)
+    count = slots[0].shape[0]
+    near = wide(slots[0]) + wide(odd[:count])
+    far = swap(low(wide(slots[2]) + wide(odd[count:])), "dp", 2)
+    total = near + wide(far)
+    parts = xor_order([low(total[i]) for i in range(count)], order)
+    summed = wide(parts[0])
+    for k in range(1, count):
+        summed += wide(swap(parts[k], "row", k))
+    return xor_order(dp_slots(low(summed)), lax.axis_index("dp"))
+
+
+def fast_body(
+    states,
+    keep,
+    cont_ids,
+    answer_len,
+    teacher,
+    out_grad,
+    gain_attn,
+    w_query,
+    key_projection,
+    value_projection,
+    w_out,
+    gain_ffn,
+    w_gate,
+    w_up,
+    w_down,
+):
+    rows, width = states.shape
+    n_row, n_col, n_dp = lax.axis_size("row"), lax.axis_size("col"), lax.axis_size("dp")
+    d, r, y = lax.axis_index("dp"), lax.axis_index("row"), lax.axis_index("col")
+    groups = n_row // n_col
+    features = width * n_col
+    heads_row = w_query.shape[1] // HEAD_SIZE
+    order = r ^ (y * groups)
+
+    def along_row(x):
+        return xor_order([x] + [swap(x, "row", k) for k in range(1, n_row)], order)
+
+    kv_t = jnp.concatenate([key_projection.T, value_projection.T], axis=0)
+    kv_part = kv_t.shape[0] // n_dp
+    kv_rows = jnp.concatenate(along_row(rows_of(kv_t, d * kv_part, kv_part)), axis=0)
+    kv_slots = xor_order(dp_slots(kv_rows), d)
+
+    def kv_weights(side):
+        lo = side * groups * kv_part
+        return jnp.concatenate(
+            [s[lo + g * kv_part : lo + (g + 1) * kv_part] for g in range(groups) for s in kv_slots], axis=0
+        )
+
+    wkv = [kv_weights(0), kv_weights(1)]
+    q_part = jnp.concatenate(along_row(rows_of(w_query, d * HEAD_SIZE, HEAD_SIZE, 1).T), axis=0)
+    q_slots = dp_slots(q_part)
+    side_rows = groups * HEAD_SIZE
+    wq = [
+        jnp.concatenate([q_slots[m][s * side_rows : (s + 1) * side_rows] for m in ORDER], axis=0) for s in (0, 1)
+    ]
+    o_part = jnp.concatenate(along_row(rows_of(w_out, d * HEAD_SIZE, HEAD_SIZE)), axis=0)
+    o_slots = dp_slots(o_part)
+    wo = [
+        jnp.concatenate([o_slots[m][s * side_rows : (s + 1) * side_rows] for m in ORDER], axis=0) for s in (0, 1)
+    ]
+
+    inner = w_down.shape[0]
+    inner_part = inner // (n_dp * n_col)
+
+    def hidden_rows(w):
+        own = rows_of(w, (d * n_col + y) * inner_part, inner_part)
+        other = rows_of(w, (d * n_col + (1 - y)) * inner_part, inner_part)
+        return gather_rows(jnp.concatenate([own, swap(other, "col", 1)], axis=1))
+
+    wg, wu, wd = hidden_rows(w_gate.T), hidden_rows(w_up.T), hidden_rows(w_down)
+
+    positions, segment, counted = token_layout(cont_ids, answer_len)
+    row_start = r * rows
+    count = jnp.sum(counted.astype(jnp.float32)).reshape(1)
+    count = count + swap(count, "dp", 1)
+    count = (count + swap(count, "dp", 2))[0]
+    counted_here = rows_of(counted, row_start, rows).astype(jnp.float32)[:, None]
+    keep_here = keep.astype(jnp.float32)[:, None]
+    position = rows_of(positions, row_start, rows).astype(jnp.float32)
+    query_seg = rows_of(segment, row_start, rows)
+    key_segs = [rows_of(segment, jnp.maximum(r - k, 0) * rows, rows) for k in range(n_row)]
+    flags = [jnp.int32(2)]
+    for k in range(1, n_row):
+        least, most = jnp.min(key_segs[k]), jnp.max(key_segs[k])
+        active = (r >= k) & ((least < 0) | (most >= jnp.min(query_seg)))
+        flags.append(jnp.where(active, jnp.where(most < 0, 1, 2), 0).astype(jnp.int32))
+    flags = jnp.stack(flags)
+    key_seg = jnp.concatenate(key_segs)[:, None]
+    query_seg = query_seg[None, :]
+    freqs = ROPE_BASE ** (-2.0 * jnp.arange(HEAD_SIZE // 2, dtype=jnp.float32) / HEAD_SIZE)
+    angles_t = freqs[:, None] * position[None, :]
+    cos_t, sin_t = jnp.cos(angles_t), jnp.sin(angles_t)
+    cos_n, sin_n = cos_t.T, sin_t.T
+    cos_n = jnp.concatenate([cos_n, cos_n], axis=1)
+    sin_n = jnp.concatenate([-sin_n, sin_n], axis=1)
+
+    def turn(x, sign):
+        half = HEAD_SIZE // 2
+        turned = jnp.concatenate([x[:, half:], x[:, :half]], axis=1)
+        return x * cos_n + turned * (sign * sin_n)
+
+    def turn_heads(x, sign):
+        return jnp.concatenate(
+            [turn(x[:, i : i + HEAD_SIZE], sign) for i in range(0, x.shape[1], HEAD_SIZE)], axis=1
+        )
+
+    def turn_keys(x, sign):
+        return jnp.concatenate(
+            [
+                turn(x[:, i : i + HEAD_SIZE], sign) if i % (2 * HEAD_SIZE) == 0 else x[:, i : i + HEAD_SIZE]
+                for i in range(0, x.shape[1], HEAD_SIZE)
+            ],
+            axis=1,
+        )
+
+    states_f = wide(states)
+    squares = jnp.sum(states_f * states_f, axis=1)
+    scale_attn = lax.rsqrt((squares + swap(squares, "col", 1)) / features + EPSILON)[:, None]
+    a1 = low(states_f * scale_attn * gain_attn[None, :])
+    kv_sum = dot_nt(a1, wkv[0]) + wide(swap(low(dot_nt(a1, wkv[1])), "col", 1))
+    key_value = low(turn_keys(kv_sum, 1.0))
+    key_values = [key_value] + [
+        lax.ppermute(key_value, "row", [(i, i + k) for i in range(n_row - k)]) for k in range(1, n_row)
+    ]
+    q_sum = dot_nt(a1, wq[0]) + wide(swap(low(dot_nt(a1, wq[1])), "col", 1))
+    queries = low(turn_heads(q_sum, 1.0))
+    context, lse = attend(flags, queries, query_seg, key_seg, key_values)
+    context_other = swap(context, "col", 1)
+    attention = dot_nn(context, wo[0]) + dot_nn(context_other, wo[1])
+    hidden_res = states_f + keep_here * attention
+
+    squares = jnp.sum(hidden_res * hidden_res, axis=1)
+    scale_ffn = lax.rsqrt((squares + swap(squares, "col", 1)) / features + EPSILON)[:, None]
+    a2 = low(hidden_res * scale_ffn * gain_ffn[None, :])
+    a2_all = plane_gather(a2)
+    gate, up, hidden, parts = feed(a2_all, wg, wu, wd)
+    result = hidden_res + keep_here * plane_scatter(parts)
+    error = result - wide(teacher)
+    error_total = jnp.sum(counted_here * error * error).reshape(1)
+    for axis, mask in (("dp", 1), ("dp", 2), ("col", 1), ("row", 1), ("row", 2)):
+        error_total = error_total + swap(error_total, axis, mask)
+    loss = error_total[0] / (count * features)
+    grad_result = wide(out_grad) + 2.0 / (count * features) * counted_here * error
+
+    gm_all = plane_gather(low(keep_here * grad_result))
+    dgate, dup, parts = feed_back(gm_all, gate, up, wg, wu, wd)
+    grad_normed_ffn = plane_scatter(parts)
+
+    def hidden_home(left, right):
+        part = lax.psum_scatter(low(dot_tn(left, right)), "row", scatter_dimension=0, tiled=True)
+        own, other = part[:, :width], swap(part[:, width:], "col", 1)
+        pair = jnp.concatenate(xor_order([own, other], y), axis=0)
+        return lax.all_gather(pair, "dp", axis=0, tiled=True)
+
+    grad_down = wide(hidden_home(hidden, gm_all))
+    grad_gate = wide(hidden_home(dgate, a2_all).T)
+    grad_up = wide(hidden_home(dup, a2_all).T)
+    gain_ffn_sum = jnp.sum(grad_normed_ffn * hidden_res * scale_ffn, axis=0)
+    weighted = grad_normed_ffn * gain_ffn[None, :]
+    inner_sum = jnp.sum(weighted * hidden_res, axis=1)
+    inner_sum = (inner_sum + swap(inner_sum, "col", 1))[:, None]
+    grad_hidden_res = grad_result + scale_ffn * weighted - hidden_res * scale_ffn**3 * inner_sum / features
+
+    ga = low(keep_here * grad_hidden_res)
+    grad_context = low(dot_nt(ga, wo[0]) + wide(swap(low(dot_nt(ga, wo[1])), "col", 1)))
+    dq, *dkv_parts = attend_back(flags, queries, grad_context, lse, cos_t, sin_t, query_seg, key_seg, key_values)
+    dkv_sum = dkv_parts[0]
+    for k in range(1, n_row):
+        dkv_sum += wide(lax.ppermute(dkv_parts[k], "row", [(i + k, i) for i in range(n_row - k)]))
+    dkv = low(turn_keys(wide(low(dkv_sum)), -1.0))
+    dq_other = swap(dq, "col", 1)
+    dkv_other = swap(dkv, "col", 1)
+    grad_normed_attn = (
+        dot_nn(dq, wq[0]) + dot_nn(dq_other, wq[1]) + dot_nn(dkv, wkv[0]) + dot_nn(dkv_other, wkv[1])
+    )
+
+    def head_slots(own, other):
+        sides = [x.reshape(n_dp, groups, HEAD_SIZE, width) for x in (own, other)]
+        return [jnp.concatenate([s[ORDER.index(m)] for s in sides], axis=0) for m in range(n_dp)]
+
+    grad_out = wide(jnp.concatenate(home(head_slots(dot_tn(context, ga), dot_tn(context_other, ga)), order), axis=0))
+    grad_query = wide(jnp.concatenate(home(head_slots(dot_tn(dq, a1), dot_tn(dq_other, a1)), order), axis=0).T)
+    dwkv = jnp.concatenate(
+        [x.reshape(groups, n_dp, kv_part, width) for x in (dot_tn(dkv, a1), dot_tn(dkv_other, a1))], axis=0
+    )
+    dwkv = jnp.concatenate(home(xor_order([dwkv[:, i] for i in range(n_dp)], d), order), axis=0)
+    grad_key = wide(dwkv[: kv_t.shape[0] // 2].T)
+    grad_value = wide(dwkv[kv_t.shape[0] // 2 :].T)
+
+    gain_attn_sum = jnp.sum(grad_normed_attn * states_f * scale_attn, axis=0)
+    weighted = grad_normed_attn * gain_attn[None, :]
+    inner_sum = jnp.sum(weighted * states_f, axis=1)
+    inner_sum = (inner_sum + swap(inner_sum, "col", 1))[:, None]
+    grad_states = grad_hidden_res + scale_attn * weighted - states_f * scale_attn**3 * inner_sum / features
+
+    gains = []
+    for gain in (gain_attn_sum, gain_ffn_sum):
+        for axis, mask in (("dp", 1), ("dp", 2), ("row", 1), ("row", 2)):
+            gain = gain + swap(gain, axis, mask)
+        gains.append(gain)
+    return (
+        low(result),
+        loss,
+        grad_states,
+        gains[0],
+        grad_query,
+        grad_key,
+        grad_value,
+        grad_out,
+        gains[1],
+        grad_gate,
+        grad_up,
+        grad_down,
+    )
+
+
 def solution(mesh):
     return jax.shard_map(
-        body,
+        fast_body if dict(mesh.shape) == {"dp": 4, "row": 4, "col": 2} else body,
         mesh=mesh,
         in_specs=(
             P(("dp", "row"), "col"),

time: 2400 us -> 1050 us (0.44)
  waiting for transfers between devices: 1880 us -> 471 us
  starting transfers between devices: 1.55 us -> 147 us
  matrix products: 207 us -> 65.6 us
  blocking collectives: 95.1 us -> 0 us
  Pallas kernels: 0 us -> 85.2 us
  other arithmetic: 128 us -> 167 us
    reduce_scatter x8 -> x3, waiting for transfers between devices: 1040 us -> 66.7 us  [hidden_home(): lax.psum_scatter(low(dot_tn(left, right)), 'row', scatter_dimension=0, ti...]
    ppermute x0 -> x107, waiting for transfers between devices: none -> 356 us  [the longest x101 305 us: swap(): return lax.ppermute(values, axis, [(i, i ^ mask) for i in range(size)])]
    all_gather x4 -> x3, waiting for transfers between devices: 277 us -> 0.01 us  [hidden_home(): return lax.all_gather(pair, 'dp', axis=0, tiled=True)]
    all_gather x4 -> x3, waiting for transfers between devices: 319 us -> 48.1 us  [gather_rows(): return lax.all_gather(values, 'row', axis=0, tiled=True)]
    psum x3 -> x0, waiting for transfers between devices: 250 us -> none  [the longest x1 191 us: body(): lax.psum(grad_query.astype(jnp.bfloat16), 'dp').astype(jnp.float32)]
    ppermute x0 -> x107, starting transfers between devices: none -> 146 us  [the longest x101 130 us: swap(): return lax.ppermute(values, axis, [(i, i ^ mask) for i in range(size)])]
    dot_general x29 -> x21, matrix products: 207 us -> 65.6 us  [the longest x9 40.5 us: dot_tn(): lax.dot_general(left, right, (((0,), (0,)), ((), ())), preferred_element_...]
    psum x6 -> x0, blocking collectives: 95.1 us -> none  [the longest x1 41.1 us: body(): lax.psum((jnp.sum(counted_here * error * error), own_count), ('dp', 'row'...]
  transfers between devices with their start and end apart: 19 -> 116, of which waited for: 19 -> 52; matrix products, arithmetic and copies ran while one was open for 4% -> 23% of each run, Pallas kernels for 0% -> 2%
where the time goes in v1:
time: 1050 us
  waiting for transfers between devices  471 us (45%)
  other arithmetic  167 us (16%)
  starting transfers between devices  147 us (14%)
  Pallas kernels  85.2 us (8%)
  local copies, waits for them, and re-layouts  82.6 us (8%)
  matrix products  65.6 us (6%)
  between operations  30.6 us (3%)
    ppermute x101, waiting for transfers between devices, swap(): return lax.ppermute(values, axis, [(i, i ^ mask) for i in range(size)])  305 us
    ppermute x101, starting transfers between devices, swap(): return lax.ppermute(values, axis, [(i, i ^ mask) for i in range(size)])  130 us
    concatenate x2, other arithmetic, plane_gather(): return jnp.concatenate(sides, axis=0)  71.6 us
    reduce_scatter x3, waiting for transfers between devices, hidden_home(): lax.psum_scatter(low(dot_tn(left, right)), 'row', scatter_dimension=0, ti...  66.7 us
    pallas_call x2, Pallas kernels, feed_call(): pl.pallas_call(kernel, out_shape=tuple((jax.ShapeDtypeStruct((tokens, hid...  60.2 us
    all_gather x3, waiting for transfers between devices, gather_rows(): return lax.all_gather(values, 'row', axis=0, tiled=True)  48.1 us
    ppermute x3, waiting for transfers between devices, fast_body(): lax.ppermute(dkv_parts[k], 'row', [(i + k, i) for i in range(n_row - k)])  40.6 us
    dot_general x9, matrix products, dot_tn(): lax.dot_general(left, right, (((0,), (0,)), ((), ())), preferred_element_...  40.5 us
  transfers between devices with their start and end apart: 116, of which 52 were waited for; matrix products, arithmetic and copies ran while one was open for 23% of the time, Pallas kernels for 2%

profile of v1, /device:TPU:0, one launch (start us, length us, event | category | flops | bytes accessed | tf_op | source)
XLA Modules:
  0.0 1049.0 jit_solution(9419996991479627404)
XLA Ops:
  8.5 5.1 collective-permute-start.8
  50.7 25.3 %collective-permute-done.2 = bf16[128,1024]{1,0:T(8,128)(2,1)S(1)} collective-permute-done((bf16[128,1024]{1,0:T(8,128)(2,1)S(1)}, bf16[128,1024]{1,0:T(8,128)(2,1)S(1)}, u32[]{:S(2)}, u32[]{:S(2)}) %collective-permute-start.2) | collective-permute-done | bytes 262176 | tf_op jit(solution)/shard_map/ppermute | solution.py:399
  101.5 11.1 %collective-permute-done.4 = bf16[512,1024]{1,0:T(8,128)(2,1)} collective-permute-done((bf16[512,1024]{1,0:T(8,128)(2,1)}, bf16[512,1024]{1,0:T(8,128)(2,1)}, u32[]{:S(2)}, u32[]{:S(2)}) %collective-permute-start.4) | collective-permute-done | bytes 1048608 | tf_op jit(solution)/shard_map/ppermute | solution.py:399
  123.1 5.8 collective-permute-done.14
  137.6 5.2 collective-permute-start.16
  142.7 16.2 %collective-permute-done.7 = bf16[512,1024]{1,0:T(8,128)(2,1)S(1)} collective-permute-done((bf16[512,1024]{1,0:T(8,128)(2,1)S(1)}, bf16[512,1024]{1,0:T(8,128)(2,1)S(1)}, u32[]{:S(2)}, u32[]{:S(2)}) %collective-permute-start.7) | collective-permute-done | bytes 1048608 | tf_op jit(solution)/shard_map/ppermute | solution.py:399
  170.1 10.0 collective-permute-done.17.refs_3_
  180.9 10.2 attend.1
  201.7 14.4 %collective-permute-done.24 = bf16[512,1024]{1,0:T(8,128)(2,1)S(1)} collective-permute-done((bf16[512,1024]{1,0:T(8,128)(2,1)}, bf16[512,1024]{1,0:T(8,128)(2,1)S(1)}, u32[]{:S(2)}, u32[]{:S(2)}) %collective-permute-start.24) | collective-permute-done | bytes 1048608 | tf_op jit(solution)/shard_map/ppermute | solution.py:399
  228.1 8.4 collective-permute-done.27
  243.8 16.5 %collective-permute-done.28 = bf16[256,2048]{1,0:T(8,128)(2,1)} collective-permute-done((bf16[256,2048]{1,0:T(8,128)(2,1)S(1)}, bf16[256,2048]{1,0:T(8,128)(2,1)}, u32[]{:S(2)}, u32[]{:S(2)}) %collective-permute-start.28) | collective-permute-done | bytes 1048608 | tf_op jit(solution)/shard_map/ppermute | solution.py:399
  260.3 8.7 collective-permute-done.37
  276.2 35.9 %maximum_maximum_fusion.a_ref = bf16[2048,2048]{1,0:T(8,128)(2,1)} fusion(bf16[256,1024]{1,0:T(8,128)(2,1)S(1)} %get-tuple-element.232, bf16[256,1024]{1,0:T(8,128)(2,1)S(1)} %get-tuple-element.234, bf16[256,1024]{1,0:T(8,128)(2,1)S(1)} %collective-permute-done.34, bf16[256,1024]{1,0:T(8,128)(2,1)S(1)} %get-tuple-element.233, ...), kind=kLoop, calls=%fused_computation | loop fusion | flops 117440512 | bytes 16777216 | tf_op jit(solution)/shard_map/concatenate | solution.py:695
  312.0 48.1 %all-gather.11.cloned.1.call-done.wd_ref = bf16[704,2048]{1,0:T(8,128)(2,1)} async-done(((bf16[176,2048]{1,0:T(8,128)(2,1)}), bf16[704,2048]{1,0:T(8,128)(2,1)}) %all-gather.11.cloned.1.call-update) | async-done | bytes 2883600 | tf_op jit(solution)/shard_map/all_gather | solution.py:67
  360.2 26.7 %feed.1 = (f32[2048,704]{1,0:T(8,128)}, f32[2048,704]{1,0:T(8,128)}, bf16[2048,704]{1,0:T(8,128)(2,1)}, bf16[2048,2048]{1,0:T(8,128)(2,1)}) custom-call(bf16[2048,2048]{1,0:T(8,128)(2,1)} %maximum_maximum_fusion.a_ref, bf16[704,2048]{1,0:T(8,128)(2,1)} %all-gather.7.cloned.1.call-done.wg_ref, bf16[704,2048]{1,0:T(8,128)(2,1)} %all-gather.9.cloned.1.call-done.wu_ref, ...), custom_call_target="tpu_custom_call" | custom-call | flops 17716740096 | bytes 41943040 | tf_op jit(solution)/shard_map/feed/pallas_call | solution.py:659
  389.4 7.3 collective-permute-done.38
  396.7 7.9 fusion.79
  411.2 20.1 %collective-permute-done.41 = bf16[512,1024]{1,0:T(8,128)(2,1)S(1)} collective-permute-done((bf16[512,1024]{1,0:T(8,128)(2,1)S(1)}, bf16[512,1024]{1,0:T(8,128)(2,1)S(1)}, u32[]{:S(2)}, u32[]{:S(2)}) %collective-permute-start.41) | collective-permute-done | bytes 1048608 | tf_op jit(solution)/shard_map/ppermute | solution.py:399
  436.4 7.7 collective-permute-start.49
  452.1 9.7 collective-permute-done.51
  464.6 20.4 %collective-permute-done.52 = bf16[256,2048]{1,0:T(8,128)(2,1)S(1)} collective-permute-done((bf16[256,2048]{1,0:T(8,128)(2,1)S(1)}, bf16[256,2048]{1,0:T(8,128)(2,1)S(1)}, u32[]{:S(2)}, u32[]{:S(2)}) %collective-permute-start.52) | collective-permute-done | bytes 1048608 | tf_op jit(solution)/shard_map/ppermute | solution.py:399
  493.0 35.8 %maximum_maximum_fusion.1.gm_ref = bf16[2048,2048]{1,0:T(8,128)(2,1)} fusion(bf16[256,1024]{1,0:T(8,128)(2,1)S(1)} %get-tuple-element.222, bf16[256,1024]{1,0:T(8,128)(2,1)S(1)} %get-tuple-element.224, bf16[256,1024]{1,0:T(8,128)(2,1)} %copy-done.42, bf16[256,1024]{1,0:T(8,128)(2,1)S(1)} %get-tuple-element.223, bf16[256,1024]{1,0:T(8,128)(2,1)S(1)} %get-tuple-element.221, ...), kind=kLoop, calls=%fused_computation.1 | loop fusion | flops 117440512 | bytes 16777216 | tf_op jit(solution)/shard_map/concatenate | solution.py:695
  528.8 33.5 %feed_back.1 = (bf16[2048,704]{1,0:T(8,128)(2,1)}, bf16[2048,704]{1,0:T(8,128)(2,1)}, bf16[2048,2048]{1,0:T(8,128)(2,1)}) custom-call(bf16[2048,2048]{1,0:T(8,128)(2,1)} %maximum_maximum_fusion.1.gm_ref, f32[2048,704]{1,0:T(8,128)} %get-tuple-element.28.gate_ref, f32[2048,704]{1,0:T(8,128)} %get-tuple-element.29.up_ref, ...), custom_call_target="tpu_custom_call" | custom-call | flops 17716740096 | bytes 41943040 | tf_op jit(solution)/shard_map/feed_back/pallas_call | solution.py:659
  562.3 10.7 %convolution_convert_fusion.2 = bf16[704,2048]{1,0:T(8,128)(2,1)} fusion(bf16[2048,704]{1,0:T(8,128)(2,1)} %get-tuple-element.37, bf16[2048,2048]{1,0:T(8,128)(2,1)} %maximum_maximum_fusion.a_ref), kind=kOutput, calls=%fused_computation.20 | convolution fusion | flops 5907021824 | bytes 14155776 | tf_op jit(solution)/shard_map/dot_general | solution.py:428
  573.1 10.7 %convolution_convert_fusion.1 = bf16[704,2048]{1,0:T(8,128)(2,1)} fusion(bf16[2048,704]{1,0:T(8,128)(2,1)} %get-tuple-element.38, bf16[2048,2048]{1,0:T(8,128)(2,1)} %maximum_maximum_fusion.a_ref), kind=kOutput, calls=%fused_computation.19 | convolution fusion | flops 5907021824 | bytes 14155776 | tf_op jit(solution)/shard_map/dot_general | solution.py:428
  583.9 10.7 %convolution_convert_fusion = bf16[704,2048]{1,0:T(8,128)(2,1)} fusion(bf16[2048,704]{1,0:T(8,128)(2,1)} %get-tuple-element.39, bf16[2048,2048]{1,0:T(8,128)(2,1)} %maximum_maximum_fusion.1.gm_ref), kind=kOutput, calls=%fused_computation.18 | convolution fusion | flops 5907021824 | bytes 14155776 | tf_op jit(solution)/shard_map/dot_general | solution.py:428
  599.5 28.0 %reduce-scatter.4.cloned.1.call-done = bf16[176,2048]{1,0:T(8,128)(2,1)} async-done(((bf16[704,2048]{1,0:T(8,128)(2,1)}), bf16[176,2048]{1,0:T(8,128)(2,1)}) %reduce-scatter.4.cloned.1.call-update) | async-done | bytes 720912 | tf_op jit(solution)/shard_map/reduce_scatter | solution.py:869
  630.1 8.6 collective-permute-done.104
  641.3 8.0 fusion.80
  656.9 18.4 %collective-permute-done.62 = bf16[512,1024]{1,0:T(8,128)(2,1)S(1)} collective-permute-done((bf16[512,1024]{1,0:T(8,128)(2,1)S(1)}, bf16[512,1024]{1,0:T(8,128)(2,1)S(1)}, u32[]{:S(2)}, u32[]{:S(2)}) %collective-permute-start.62) | collective-permute-done | bytes 1048608 | tf_op jit(solution)/shard_map/ppermute | solution.py:399
  678.6 7.2 reduce-scatter.6.cloned.1.call-done
  700.9 7.3 collective-permute-done.61
  713.1 31.5 %reduce-scatter.8.cloned.1.call-done = bf16[176,2048]{1,0:T(8,128)(2,1)} async-done(((bf16[704,2048]{1,0:T(8,128)(2,1)}), bf16[176,2048]{1,0:T(8,128)(2,1)}) %reduce-scatter.8.cloned.1.call-update) | async-done | bytes 720912 | tf_op jit(solution)/shard_map/reduce_scatter | solution.py:869
  747.1 6.4 multiply_convert_fusion
  799.0 14.8 %attend_back.1 = (bf16[512,1024]{1,0:T(8,128)(2,1)}, f32[512,512]{1,0:T(8,128)}, bf16[512,512]{1,0:T(8,128)(2,1)}, bf16[512,512]{1,0:T(8,128)(2,1)}, bf16[512,512]{1,0:T(8,128)(2,1)}) custom-call(s32[4]{0:T(128)} %pad_add_fusion.1.flags, bf16[512,1024]{1,0:T(8,128)(2,1)} %copy-done.59, bf16[512,1024]{1,0:T(8,128)(2,1)} %add_convert_fusion.do_ref, ...), custom_call_target="tpu_custom_call" | custom-call | flops 8053063680 | bytes 12582912 | tf_op jit(solution)/shard_map/attend_back/pallas_call | solution.py:596
  822.0 29.4 %collective-permute-done.69 = bf16[512,512]{1,0:T(8,128)(2,1)S(1)} collective-permute-done((bf16[512,512]{1,0:T(8,128)(2,1)}, bf16[512,512]{1,0:T(8,128)(2,1)S(1)}, u32[]{:S(2)}, u32[]{:S(2)}) %collective-permute-start.69) | collective-permute-done | bytes 524320 | tf_op jit(solution)/shard_map/ppermute | solution.py:888
  851.5 11.2 %collective-permute-done.68 = bf16[512,512]{1,0:T(8,128)(2,1)S(1)} collective-permute-done((bf16[512,512]{1,0:T(8,128)(2,1)}, bf16[512,512]{1,0:T(8,128)(2,1)S(1)}, u32[]{:S(2)}, u32[]{:S(2)}) %collective-permute-start.68) | collective-permute-done | bytes 524320 | tf_op jit(solution)/shard_map/ppermute | solution.py:888
  868.9 6.4 collective-permute-start.93
  898.7 10.3 collective-permute-start.95
  909.8 11.9 %collective-permute-start.74 = (f32[1024]{0:T(1024)S(1)}, f32[1024]{0:T(1024)S(1)}, u32[]{:S(2)}, u32[]{:S(2)}) collective-permute-start(f32[1024]{0:T(1024)S(1)} %add.361), channel_id=1, source_target_pairs={{0,2},{2,0},{4,6},{6,4},{1,3},{3,1},{5,7},{7,5},{8,10},{10,8},{12,... | collective-permute-start | bytes 12296 | tf_op jit(solution)/shard_map/ppermute | solution.py:399
  928.4 15.6 %collective-permute-done.97 = bf16[128,1024]{1,0:T(8,128)(2,1)S(1)} collective-permute-done((bf16[128,1024]{1,0:T(8,128)(2,1)S(1)}, bf16[128,1024]{1,0:T(8,128)(2,1)S(1)}, u32[]{:S(2)}, u32[]{:S(2)}) %collective-permute-start.97) | collective-permute-done | bytes 262176 | tf_op jit(solution)/shard_map/ppermute | solution.py:399
  959.8 20.3 %collective-permute-done.89 = bf16[64,1024]{1,0:T(8,128)(2,1)S(1)} collective-permute-done((bf16[64,1024]{1,0:T(8,128)(2,1)S(1)}, bf16[64,1024]{1,0:T(8,128)(2,1)S(1)}, u32[]{:S(2)}, u32[]{:S(2)}) %collective-permute-start.89) | collective-permute-done | bytes 131104 | tf_op jit(solution)/shard_map/ppermute | solution.py:399
  991.9 16.0 %collective-permute-done.79 = bf16[128,1024]{1,0:T(8,128)(2,1)S(1)} collective-permute-done((bf16[128,1024]{1,0:T(8,128)(2,1)S(1)}, bf16[128,1024]{1,0:T(8,128)(2,1)S(1)}, u32[]{:S(2)}, u32[]{:S(2)}) %collective-permute-start.79) | collective-permute-done | bytes 262176 | tf_op jit(solution)/shard_map/ppermute | solution.py:399
  1008.6 5.1 convert_bitcast_fusion.1
  1016.5 5.0 convert_bitcast_fusion
  1021.5 6.2 copy.79
  1027.7 6.2 copy.80
  1033.9 5.1 convert_element_type.396
  (529 shorter events, 317.5 us)
Async XLA Ops:
  7.2 304.8 %all-gather.7.cloned.1.call-start = ((), (), s32[]{:S(2)}) async-start(), calls=%async_computation.3 | async-start | bytes 3604480 | tf_op jit(solution)/shard_map/all_gather | solution.py:67
  8.5 33.5 %collective-permute-start.8 = (bf16[64,1024]{0,1:T(8,128)(2,1)S(1)}, bf16[64,1024]{0,1:T(8,128)(2,1)}, u32[]{:S(2)}, u32[]{:S(2)}) collective-permute-start(bf16[64,1024]{0,1:T(8,128)(2,1)S(1)} %fusion.35), channel_id=1, source_target_pairs={{0,6},{2,4},{4,2},{6,0},{1,7},{3,5},{5,3},{7,1},{8,14},{10,12},{12... | collective-permute-start | bytes 393224 | tf_op jit(solution)/shard_map/ppermute | solution.py:399
  13.6 29.0 %collective-permute-start.9 = (bf16[64,1024]{0,1:T(8,128)(2,1)S(1)}, bf16[64,1024]{0,1:T(8,128)(2,1)}, u32[]{:S(2)}, u32[]{:S(2)}) collective-permute-start(bf16[64,1024]{0,1:T(8,128)(2,1)S(1)} %fusion.35), channel_id=1, source_target_pairs={{0,4},{2,6},{4,0},{6,2},{1,5},{3,7},{5,1},{7,3},{8,12},{10,14},{12... | collective-permute-start | bytes 393224 | tf_op jit(solution)/shard_map/ppermute | solution.py:399
  13.6 30.4 %collective-permute-start.10 = (bf16[64,1024]{0,1:T(8,128)(2,1)S(1)}, bf16[64,1024]{0,1:T(8,128)(2,1)}, u32[]{:S(2)}, u32[]{:S(2)}) collective-permute-start(bf16[64,1024]{0,1:T(8,128)(2,1)S(1)} %fusion.35), channel_id=1, source_target_pairs={{0,2},{2,0},{4,6},{6,4},{1,3},{3,1},{5,7},{7,5},{8,10},{10,8},{12,... | collective-permute-start | bytes 393224 | tf_op jit(solution)/shard_map/ppermute | solution.py:399
  17.7 31.1 %collective-permute-start.3 = (bf16[128,1024]{1,0:T(8,128)(2,1)S(1)}, bf16[128,1024]{1,0:T(8,128)(2,1)}, u32[]{:S(2)}, u32[]{:S(2)}) collective-permute-start(bf16[128,1024]{1,0:T(8,128)(2,1)S(1)} %bitcast.155), channel_id=1, source_target_pairs={{0,2},{2,0},{4,6},{6,4},{1,3},{3,1},{5,7},{7,5},{8,10},{10,8},{12,... | collective-permute-start | bytes 786440 | tf_op jit(solution)/shard_map/ppermute | solution.py:399
  42.1 33.9 %collective-permute-start.2 = (bf16[128,1024]{1,0:T(8,128)(2,1)S(1)}, bf16[128,1024]{1,0:T(8,128)(2,1)S(1)}, u32[]{:S(2)}, u32[]{:S(2)}) collective-permute-start(bf16[128,1024]{1,0:T(8,128)(2,1)S(1)} %bitcast.157), channel_id=1, source_target_pairs={{0,4},{2,6},{4,0},{6,2},{1,5},{3,7},{5,1},{7,3},{8,12},{10,14},{12... | collective-permute-start | bytes 786440 | tf_op jit(solution)/shard_map/ppermute | solution.py:399
  42.6 38.8 %collective-permute-start.20 = (bf16[128,1024]{1,0:T(8,128)(2,1)}, bf16[128,1024]{1,0:T(8,128)(2,1)S(1)}, u32[]{:S(2)}, u32[]{:S(2)}) collective-permute-start(bf16[128,1024]{1,0:T(8,128)(2,1)} %constant_dynamic-slice_fusion.7), channel_id=1, source_target_pairs={{0,2},{2,0},{4,6},{6,4},{1,3},{3,1},{5,7},{7,5},{8,10},{10,8},{12,... | collective-permute-start | bytes 786440 | tf_op jit(solution)/shard_map/ppermute | solution.py:399
  44.1 37.9 %collective-permute-start.18 = (bf16[128,1024]{1,0:T(8,128)(2,1)}, bf16[128,1024]{1,0:T(8,128)(2,1)S(1)}, u32[]{:S(2)}, u32[]{:S(2)}) collective-permute-start(bf16[128,1024]{1,0:T(8,128)(2,1)} %constant_dynamic-slice_fusion.7), channel_id=1, source_target_pairs={{0,6},{2,4},{4,2},{6,0},{1,7},{3,5},{5,3},{7,1},{8,14},{10,12},{12... | collective-permute-start | bytes 786440 | tf_op jit(solution)/shard_map/ppermute | solution.py:399
  48.8 37.4 %collective-permute-start.19 = (bf16[128,1024]{1,0:T(8,128)(2,1)}, bf16[128,1024]{1,0:T(8,128)(2,1)S(1)}, u32[]{:S(2)}, u32[]{:S(2)}) collective-permute-start(bf16[128,1024]{1,0:T(8,128)(2,1)} %constant_dynamic-slice_fusion.7), channel_id=1, source_target_pairs={{0,4},{2,6},{4,0},{6,2},{1,5},{3,7},{5,1},{7,3},{8,12},{10,14},{12... | collective-permute-start | bytes 786440 | tf_op jit(solution)/shard_map/ppermute | solution.py:399
  50.2 40.4 %collective-permute-start.35 = (bf16[176,1024]{1,0:T(8,128)(2,1)S(1)}, bf16[176,1024]{1,0:T(8,128)(2,1)S(1)}, u32[]{:S(2)}, u32[]{:S(2)}) collective-permute-start(bf16[176,1024]{1,0:T(8,128)(2,1)S(1)} %bitcast.169), channel_id=1, source_target_pairs={{0,1},{1,0},{2,3},{3,2},{4,5},{5,4},{6,7},{7,6},{8,9},{9,8},{10,11... | collective-permute-start | bytes 1081352 | tf_op jit(solution)/shard_map/ppermute | solution.py:399
  81.4 111.6 %collective-permute-start.36 = (bf16[176,1024]{1,0:T(8,128)(2,1)}, bf16[176,1024]{1,0:T(8,128)(2,1)}, u32[]{:S(2)}, u32[]{:S(2)}) collective-permute-start(bf16[176,1024]{1,0:T(8,128)(2,1)} %bitcast.17), channel_id=1, source_target_pairs={{0,1},{1,0},{2,3},{3,2},{4,5},{5,4},{6,7},{7,6},{8,9},{9,8},{10,11... | collective-permute-start | bytes 1081352 | tf_op jit(solution)/shard_map/ppermute | solution.py:399
  86.2 26.4 %collective-permute-start.4 = (bf16[512,1024]{1,0:T(8,128)(2,1)}, bf16[512,1024]{1,0:T(8,128)(2,1)}, u32[]{:S(2)}, u32[]{:S(2)}) collective-permute-start(bf16[512,1024]{1,0:T(8,128)(2,1)} %pad_maximum_fusion.4), channel_id=1, source_target_pairs={{0,16},{8,24},{16,0},{24,8},{1,17},{9,25},{17,1},{25,9},{2,18},{10... | collective-permute-start | bytes 3145736 | tf_op jit(solution)/shard_map/ppermute | solution.py:399
  90.6 30.2 %collective-permute-start.5 = (bf16[512,1024]{1,0:T(8,128)(2,1)}, bf16[512,1024]{1,0:T(8,128)(2,1)}, u32[]{:S(2)}, u32[]{:S(2)}) collective-permute-start(bf16[512,1024]{1,0:T(8,128)(2,1)} %pad_maximum_fusion.4), channel_id=1, source_target_pairs={{0,8},{8,0},{16,24},{24,16},{1,9},{9,1},{17,25},{25,17},{2,10},{10... | collective-permute-start | bytes 3145736 | tf_op jit(solution)/shard_map/ppermute | solution.py:399
  92.0 220.0 %all-gather.9.cloned.1.call-start = ((), (), s32[]{:S(2)}) async-start(), calls=%async_computation.4 | async-start | bytes 3604480 | tf_op jit(solution)/shard_map/all_gather | solution.py:67
  92.2 76.9 %collective-permute-start.21 = (bf16[512,1024]{1,0:T(8,128)(2,1)}, bf16[512,1024]{1,0:T(8,128)(2,1)}, u32[]{:S(2)}, u32[]{:S(2)}) collective-permute-start(bf16[512,1024]{1,0:T(8,128)(2,1)} %pad_maximum_fusion.5), channel_id=1, source_target_pairs={{0,16},{8,24},{16,0},{24,8},{1,17},{9,25},{17,1},{25,9},{2,18},{10... | collective-permute-start | bytes 3145736 | tf_op jit(solution)/shard_map/ppermute | solution.py:399
  135.7 33.9 %collective-permute-start.15 = (bf16[512,512]{1,0:T(8,128)(2,1)S(1)}, bf16[512,512]{1,0:T(8,128)(2,1)S(1)}, u32[]{:S(2)}, u32[]{:S(2)}) collective-permute-start(bf16[512,512]{1,0:T(8,128)(2,1)S(1)} %pad_maximum_fusion.20.refs_0_), channel_id=1, source_target_pairs={{0,2},{2,4},{4,6},{1,3},{3,5},{5,7},{8,10},{10,12},{12,14},{9,11},... | collective-permute-start | bytes 1572872 | tf_op jit(solution)/shard_map/ppermute | solution.py:842
  137.6 32.5 %collective-permute-start.16 = (bf16[512,512]{1,0:T(8,128)(2,1)S(1)}, bf16[512,512]{1,0:T(8,128)(2,1)S(1)}, u32[]{:S(2)}, u32[]{:S(2)}) collective-permute-start(bf16[512,512]{1,0:T(8,128)(2,1)S(1)} %pad_maximum_fusion.20.refs_0_), channel_id=1, source_target_pairs={{0,4},{2,6},{1,5},{3,7},{8,12},{10,14},{9,13},{11,15},{16,20},{18,... | collective-permute-start | bytes 1572872 | tf_op jit(solution)/shard_map/ppermute | solution.py:842
  169.1 28.1 %collective-permute-start.22 = (bf16[512,1024]{1,0:T(8,128)(2,1)}, bf16[512,1024]{1,0:T(8,128)(2,1)}, u32[]{:S(2)}, u32[]{:S(2)}) collective-permute-start(bf16[512,1024]{1,0:T(8,128)(2,1)} %pad_maximum_fusion.5), channel_id=1, source_target_pairs={{0,8},{8,0},{16,24},{24,16},{1,9},{9,1},{17,25},{25,17},{2,10},{10... | collective-permute-start | bytes 3145736 | tf_op jit(solution)/shard_map/ppermute | solution.py:399
  169.5 29.9 %collective-permute-start.23 = (bf16[512,1024]{1,0:T(8,128)(2,1)}, bf16[512,1024]{1,0:T(8,128)(2,1)}, u32[]{:S(2)}, u32[]{:S(2)}) collective-permute-start(bf16[512,1024]{1,0:T(8,128)(2,1)} %collective-permute-done.21), channel_id=1, source_target_pairs={{0,8},{8,0},{16,24},{24,16},{1,9},{9,1},{17,25},{25,17},{2,10},{10... | collective-permute-start | bytes 3145736 | tf_op jit(solution)/shard_map/ppermute | solution.py:399
  194.9 165.2 %all-gather.11.cloned.1.call-start = ((), (), s32[]{:S(2)}) async-start(), calls=%async_computation.5 | async-start | bytes 3604480 | tf_op jit(solution)/shard_map/all_gather | solution.py:67
  240.5 29.7 %collective-permute-start.29 = (bf16[512,1024]{1,0:T(8,128)(2,1)}, bf16[512,1024]{1,0:T(8,128)(2,1)}, u32[]{:S(2)}, u32[]{:S(2)}) collective-permute-start(bf16[512,1024]{1,0:T(8,128)(2,1)} %pad_maximum_fusion.7), channel_id=1, source_target_pairs={{0,1},{1,0},{2,3},{3,2},{4,5},{5,4},{6,7},{7,6},{8,9},{9,8},{10,11... | collective-permute-start | bytes 3145736 | tf_op jit(solution)/shard_map/ppermute | solution.py:399
  241.9 27.0 %collective-permute-start.37 = (bf16[176,1024]{1,0:T(8,128)(2,1)S(1)}, bf16[176,1024]{1,0:T(8,128)(2,1)S(1)}, u32[]{:S(2)}, u32[]{:S(2)}) collective-permute-start(bf16[176,1024]{1,0:T(8,128)(2,1)S(1)} %get-tuple-element.161), channel_id=1, source_target_pairs={{0,1},{1,0},{2,3},{3,2},{4,5},{5,4},{6,7},{7,6},{8,9},{9,8},{10,11... | collective-permute-start | bytes 1081352 | tf_op jit(solution)/shard_map/ppermute | solution.py:399
  269.9 357.7 %reduce-scatter.4.cloned.1.call-start = ((), (), s32[]{:S(2)}) async-start(), calls=%async_computation.6 | async-start | bytes 3604480 | tf_op jit(solution)/shard_map/reduce_scatter | solution.py:869
  406.0 25.3 %collective-permute-start.41 = (bf16[512,1024]{1,0:T(8,128)(2,1)S(1)}, bf16[512,1024]{1,0:T(8,128)(2,1)S(1)}, u32[]{:S(2)}, u32[]{:S(2)}) collective-permute-start(bf16[512,1024]{1,0:T(8,128)(2,1)S(1)} %pad_maximum_fusion.8), channel_id=1, source_target_pairs={{0,1},{1,0},{2,3},{3,2},{4,5},{5,4},{6,7},{7,6},{8,9},{9,8},{10,11... | collective-permute-start | bytes 3145736 | tf_op jit(solution)/shard_map/ppermute | solution.py:399
  408.8 25.1 %collective-permute-start.39 = (bf16[256,2048]{1,0:T(8,128)(2,1)S(1)}, bf16[256,2048]{1,0:T(8,128)(2,1)S(1)}, u32[]{:S(2)}, u32[]{:S(2)}) collective-permute-start(bf16[256,2048]{1,0:T(8,128)(2,1)S(1)} %slice.781), channel_id=1, source_target_pairs={{0,16},{8,24},{16,0},{24,8},{1,17},{9,25},{17,1},{25,9},{2,18},{10... | collective-permute-start | bytes 3145736 | tf_op jit(solution)/shard_map/ppermute | solution.py:399
  573.0 112.8 %reduce-scatter.6.cloned.1.call-start = ((), (), s32[]{:S(2)}) async-start(), calls=%async_computation.8 | async-start | bytes 3604480 | tf_op jit(solution)/shard_map/reduce_scatter | solution.py:869
  583.8 160.8 %reduce-scatter.8.cloned.1.call-start = ((), (), s32[]{:S(2)}) async-start(), calls=%async_computation.10 | async-start | bytes 3604480 | tf_op jit(solution)/shard_map/reduce_scatter | solution.py:869
  594.6 414.0 %all-gather.13.cloned.1.call-start = ((), (), s32[]{:S(2)}) async-start(), calls=%async_computation.7 | async-start | bytes 3604480 | tf_op jit(solution)/shard_map/all_gather | solution.py:872
  599.5 41.8 %collective-permute-start.59 = (bf16[1024,2048]{1,0:T(8,128)(2,1)}, bf16[1024,2048]{1,0:T(8,128)(2,1)}, u32[]{:S(2)}, u32[]{:S(2)}) collective-permute-start(bf16[1024,2048]{1,0:T(8,128)(2,1)} %slice.647), channel_id=1, source_target_pairs={{0,8},{8,0},{16,24},{24,16},{1,9},{9,1},{17,25},{25,17},{2,10},{10... | collective-permute-start | bytes 12582920 | tf_op jit(solution)/shard_map/ppermute | solution.py:399
  640.8 375.7 %all-gather.15.cloned.1.call-start = ((), (), s32[]{:S(2)}) async-start(), calls=%async_computation.9 | async-start | bytes 3604480 | tf_op jit(solution)/shard_map/all_gather | solution.py:872
  655.2 33.1 %collective-permute-start.60 = (bf16[256,2048]{1,0:T(8,128)(2,1)}, bf16[256,2048]{1,0:T(8,128)(2,1)}, u32[]{:S(2)}, u32[]{:S(2)}) collective-permute-start(bf16[256,2048]{1,0:T(8,128)(2,1)} %slice.801), channel_id=1, source_target_pairs={{0,16},{8,24},{16,0},{24,8},{1,17},{9,25},{17,1},{25,9},{2,18},{10... | collective-permute-start | bytes 3145736 | tf_op jit(solution)/shard_map/ppermute | solution.py:399
  699.2 334.7 %all-gather.17.cloned.1.call-start = ((), (), s32[]{:S(2)}) async-start(), calls=%async_computation.11 | async-start | bytes 3604480 | tf_op jit(solution)/shard_map/all_gather | solution.py:872
  710.4 36.8 %collective-permute-start.64 = (f32[512]{0:T(512)S(1)}, f32[512]{0:T(512)S(1)}, u32[]{:S(2)}, u32[]{:S(2)}) collective-permute-start(f32[512]{0:T(512)S(1)} %get-tuple-element.89), channel_id=1, source_target_pairs={{0,1},{1,0},{2,3},{3,2},{4,5},{5,4},{6,7},{7,6},{8,9},{9,8},{10,11... | collective-permute-start | bytes 6152 | tf_op jit(solution)/shard_map/ppermute | solution.py:399
  745.6 48.3 %collective-permute-start.106 = (bf16[176,1024]{1,0:T(8,128)(2,1)S(1)}, bf16[176,1024]{1,0:T(8,128)(2,1)S(1)}, u32[]{:S(2)}, u32[]{:S(2)}) collective-permute-start(bf16[176,1024]{1,0:T(8,128)(2,1)S(1)} %slice.862), channel_id=1, source_target_pairs={{0,1},{1,0},{2,3},{3,2},{4,5},{5,4},{6,7},{7,6},{8,9},{9,8},{10,11... | collective-permute-start | bytes 1081352 | tf_op jit(solution)/shard_map/ppermute | solution.py:399
  756.3 38.5 %collective-permute-start.65 = (bf16[512,1024]{1,0:T(8,128)(2,1)}, bf16[512,1024]{1,0:T(8,128)(2,1)}, u32[]{:S(2)}, u32[]{:S(2)}) collective-permute-start(bf16[512,1024]{1,0:T(8,128)(2,1)} %convolution_convert_fusion.3), channel_id=1, source_target_pairs={{0,1},{1,0},{2,3},{3,2},{4,5},{5,4},{6,7},{7,6},{8,9},{9,8},{10,11... | collective-permute-start | bytes 3145736 | tf_op jit(solution)/shard_map/ppermute | solution.py:399
  773.5 93.6 %collective-permute-start.92 = (bf16[8,128,1024]{2,1,0:T(8,128)(2,1)}, bf16[8,128,1024]{2,1,0:T(8,128)(2,1)}, u32[]{:S(2)}, u32[]{:S(2)}) collective-permute-start(bf16[8,128,1024]{2,1,0:T(8,128)(2,1)} %pad_maximum_fusion.2), channel_id=1, source_target_pairs={{0,8},{8,0},{16,24},{24,16},{1,9},{9,1},{17,25},{25,17},{2,10},{10... | collective-permute-start | bytes 6291464 | tf_op jit(solution)/shard_map/ppermute | solution.py:399
  813.9 37.6 %collective-permute-start.69 = (bf16[512,512]{1,0:T(8,128)(2,1)}, bf16[512,512]{1,0:T(8,128)(2,1)S(1)}, u32[]{:S(2)}, u32[]{:S(2)}) collective-permute-start(bf16[512,512]{1,0:T(8,128)(2,1)} %get-tuple-element.36), channel_id=1, source_target_pairs={{6,0},{7,1},{14,8},{15,9},{22,16},{23,17},{30,24},{31,25}} | collective-permute-start | bytes 1572872 | tf_op jit(solution)/shard_map/ppermute | solution.py:888
  815.2 47.5 %collective-permute-start.68 = (bf16[512,512]{1,0:T(8,128)(2,1)}, bf16[512,512]{1,0:T(8,128)(2,1)S(1)}, u32[]{:S(2)}, u32[]{:S(2)}) collective-permute-start(bf16[512,512]{1,0:T(8,128)(2,1)} %get-tuple-element.35), channel_id=1, source_target_pairs={{4,0},{6,2},{5,1},{7,3},{12,8},{14,10},{13,9},{15,11},{20,16},{22,... | collective-permute-start | bytes 1572872 | tf_op jit(solution)/shard_map/ppermute | solution.py:888
  816.5 46.2 %collective-permute-start.67 = (bf16[512,512]{1,0:T(8,128)(2,1)}, bf16[512,512]{1,0:T(8,128)(2,1)S(1)}, u32[]{:S(2)}, u32[]{:S(2)}) collective-permute-start(bf16[512,512]{1,0:T(8,128)(2,1)} %get-tuple-element.34), channel_id=1, source_target_pairs={{2,0},{4,2},{6,4},{3,1},{5,3},{7,5},{10,8},{12,10},{14,12},{11,9},... | collective-permute-start | bytes 1572872 | tf_op jit(solution)/shard_map/ppermute | solution.py:888
  817.8 62.1 %collective-permute-start.66 = (bf16[512,1024]{1,0:T(8,128)(2,1)}, bf16[512,1024]{1,0:T(8,128)(2,1)S(1)}, u32[]{:S(2)}, u32[]{:S(2)}) collective-permute-start(bf16[512,1024]{1,0:T(8,128)(2,1)} %get-tuple-element.32), channel_id=1, source_target_pairs={{0,1},{1,0},{2,3},{3,2},{4,5},{5,4},{6,7},{7,6},{8,9},{9,8},{10,11... | collective-permute-start | bytes 3145736 | tf_op jit(solution)/shard_map/ppermute | solution.py:399
  889.5 56.0 %collective-permute-start.76 = (bf16[8,128,1024]{2,1,0:T(8,128)(2,1)S(1)}, bf16[8,128,1024]{2,1,0:T(8,128)(2,1)S(1)}, u32[]{:S(2)}, u32[]{:S(2)}) collective-permute-start(bf16[8,128,1024]{2,1,0:T(8,128)(2,1)S(1)} %pad_maximum_fusion.1), channel_id=1, source_target_pairs={{0,8},{8,0},{16,24},{24,16},{1,9},{9,1},{17,25},{25,17},{2,10},{10... | collective-permute-start | bytes 6291464 | tf_op jit(solution)/shard_map/ppermute | solution.py:399
  891.6 36.6 %collective-permute-start.71 = (f32[512]{0:T(512)S(1)}, f32[512]{0:T(512)S(1)}, u32[]{:S(2)}, u32[]{:S(2)}) collective-permute-start(f32[512]{0:T(512)S(1)} %get-tuple-element.91), channel_id=1, source_target_pairs={{0,1},{1,0},{2,3},{3,2},{4,5},{5,4},{6,7},{7,6},{8,9},{9,8},{10,11... | collective-permute-start | bytes 6152 | tf_op jit(solution)/shard_map/ppermute | solution.py:399
  898.7 26.9 %collective-permute-start.95 = (bf16[128,1024]{1,0:T(8,128)(2,1)S(1)}, bf16[128,1024]{1,0:T(8,128)(2,1)S(1)}, u32[]{:S(2)}, u32[]{:S(2)}) collective-permute-start(bf16[128,1024]{1,0:T(8,128)(2,1)S(1)} %get-tuple-element.208), channel_id=1, source_target_pairs={{0,4},{2,6},{4,0},{6,2},{1,5},{3,7},{5,1},{7,3},{8,12},{10,14},{12... | collective-permute-start | bytes 786440 | tf_op jit(solution)/shard_map/ppermute | solution.py:399
  928.3 29.8 %collective-permute-start.99 = (bf16[128,1024]{1,0:T(8,128)(2,1)S(1)}, bf16[128,1024]{1,0:T(8,128)(2,1)S(1)}, u32[]{:S(2)}, u32[]{:S(2)}) collective-permute-start(bf16[128,1024]{1,0:T(8,128)(2,1)S(1)} %fusion.31), channel_id=1, source_target_pairs={{0,8},{8,0},{16,24},{24,16},{1,9},{9,1},{17,25},{25,17},{2,10},{10... | collective-permute-start | bytes 786440 | tf_op jit(solution)/shard_map/ppermute | solution.py:399
  953.0 27.1 %collective-permute-start.77 = (bf16[4,128,1024]{2,1,0:T(8,128)(2,1)S(1)}, bf16[4,128,1024]{2,1,0:T(8,128)(2,1)S(1)}, u32[]{:S(2)}, u32[]{:S(2)}) collective-permute-start(bf16[4,128,1024]{2,1,0:T(8,128)(2,1)S(1)} %fusion.13), channel_id=1, source_target_pairs={{0,16},{8,24},{16,0},{24,8},{1,17},{9,25},{17,1},{25,9},{2,18},{10... | collective-permute-start | bytes 3145736 | tf_op jit(solution)/shard_map/ppermute | solution.py:399
  958.1 27.1 %collective-permute-start.91 = (bf16[64,1024]{1,0:T(8,128)(2,1)S(1)}, bf16[64,1024]{1,0:T(8,128)(2,1)S(1)}, u32[]{:S(2)}, u32[]{:S(2)}) collective-permute-start(bf16[64,1024]{1,0:T(8,128)(2,1)S(1)} %fusion.62), channel_id=1, source_target_pairs={{0,8},{8,0},{16,24},{24,16},{1,9},{9,1},{17,25},{25,17},{2,10},{10... | collective-permute-start | bytes 393224 | tf_op jit(solution)/shard_map/ppermute | solution.py:399
  981.6 26.4 %collective-permute-start.79 = (bf16[128,1024]{1,0:T(8,128)(2,1)S(1)}, bf16[128,1024]{1,0:T(8,128)(2,1)S(1)}, u32[]{:S(2)}, u32[]{:S(2)}) collective-permute-start(bf16[128,1024]{1,0:T(8,128)(2,1)S(1)} %get-tuple-element.215), channel_id=1, source_target_pairs={{0,4},{2,6},{4,0},{6,2},{1,5},{3,7},{5,1},{7,3},{8,12},{10,14},{12... | collective-permute-start | bytes 786440 | tf_op jit(solution)/shard_map/ppermute | solution.py:399
  1013.7 25.3 %collective-permute-start.83 = (bf16[128,1024]{1,0:T(8,128)(2,1)S(1)}, bf16[128,1024]{1,0:T(8,128)(2,1)S(1)}, u32[]{:S(2)}, u32[]{:S(2)}) collective-permute-start(bf16[128,1024]{1,0:T(8,128)(2,1)S(1)} %fusion.34), channel_id=1, source_target_pairs={{0,8},{8,0},{16,24},{24,16},{1,9},{9,1},{17,25},{25,17},{2,10},{10... | collective-permute-start | bytes 786440 | tf_op jit(solution)/shard_map/ppermute | solution.py:399
  (136 other events, 1707.0 us)
Sparse Core Ops, SparseCore 0:
  92.1 63.0 all-gather.6
  195.1 87.9 all-gather.8
  285.2 74.9 all-gather.10
  573.1 54.3 reduce-scatter.3
  629.7 56.0 reduce-scatter.5
  688.5 56.0 reduce-scatter.7
  746.1 26.9 all-gather.12
  774.7 29.1 all-gather.14
  805.5 27.0 all-gather.16

commit v2 on v1

--- a/solution.py
+++ b/solution.py
@@ -390,6 +390,13 @@
 
 
 LOG2E = 1.4426950408889634
+N_ROW = 4
+SHARE = 0.1
+
+
+def cost(flops, moved, exps=0, share=SHARE):
+    return pl.CostEstimate(flops=int(share * flops), bytes_accessed=int(share * moved), transcendentals=int(share * exps))
+
 VMEM_BYTES = 58 << 20
 ORDER = (0, 2, 1, 3)
 
@@ -406,6 +413,10 @@
         slots = [jnp.where(odd, slots[i ^ bit], slots[i]) for i in range(len(slots))]
         bit *= 2
     return slots
+
+
+def after(values, *others):
+    return lax.optimization_barrier((values, *others))[0]
 
 
 def low(values):
@@ -474,9 +485,7 @@
 
 def attend_back_kernel(slots, scale, flags, q_ref, do_ref, lse_ref, cos_ref, sin_ref, qseg_ref, kseg_ref, *refs):
     kv_refs = refs[:slots]
-    dq_ref = refs[slots]
-    dkv_refs = refs[slots + 1 : 2 * slots + 1]
-    p_ref, dp_ref, dot_ref, dq_acc, dkv_acc = refs[2 * slots + 1 :]
+    dq_ref, dkv_ref, p_ref, dp_ref, dot_ref, dq_acc, dkv_acc = refs[slots:]
     step, steps = pl.program_id(1), pl.num_programs(1)
     query, grad = q_ref[...], do_ref[...]
     rows = query.shape[0]
@@ -542,17 +551,26 @@
     @pl.when(step == steps - 1)
     def _():
         for slot in range(slots):
-            out = dkv_refs[slot]
-            out[:, :HEAD_SIZE] = (dkv_acc[slot, :, :HEAD_SIZE] * scale).astype(out.dtype)
-            out[:, HEAD_SIZE:] = dkv_acc[slot, :, HEAD_SIZE:].astype(out.dtype)
+            at = pl.ds(pl.multiple_of(flags[slots + slot] * rows, rows), rows)
+            dkv_ref[at, :HEAD_SIZE] = low(dkv_acc[slot, :, :HEAD_SIZE] * scale)
+            dkv_ref[at, HEAD_SIZE:] = low(dkv_acc[slot, :, HEAD_SIZE:])
+
+
+def attend_specs(queries, key_values):
+    rows, width = queries.shape
+    slots, groups = key_values.shape[0] // rows, key_values.shape[1] // (2 * HEAD_SIZE)
+    whole = lambda g, m, f: (0, 0)
+    head = pl.BlockSpec((rows, HEAD_SIZE), lambda g, m, f: (0, m * groups + g))
+    line = pl.BlockSpec((1, 1, rows), lambda g, m, f: (m * groups + g, 0, 0))
+    segs = [pl.BlockSpec((1, rows), whole), pl.BlockSpec((slots * rows, 1), whole)]
+    pairs = [
+        pl.BlockSpec((rows, 2 * HEAD_SIZE), lambda g, m, f, slot=slot: (f[slots + slot], g)) for slot in range(slots)
+    ]
+    return rows, width, slots, groups, width // HEAD_SIZE // groups, whole, head, line, segs, pairs
 
 
 def attend(flags, queries, query_seg, key_seg, key_values):
-    rows, width = queries.shape
-    slots, groups = len(key_values), key_values[0].shape[1] // (2 * HEAD_SIZE)
-    share = width // HEAD_SIZE // groups
-    whole = lambda g, m, f: (0, 0)
-    head = lambda g, m, f: (0, m * groups + g)
+    rows, width, slots, groups, share, whole, head, line, segs, pairs = attend_specs(queries, key_values)
     return pl.pallas_call(
         functools.partial(attend_kernel, slots, HEAD_SIZE ** (-0.5)),
         out_shape=(
@@ -562,16 +580,8 @@
         grid_spec=pltpu.PrefetchScalarGridSpec(
             num_scalar_prefetch=1,
             grid=(groups, share),
-            in_specs=[
-                pl.BlockSpec((rows, HEAD_SIZE), head),
-                pl.BlockSpec((1, rows), whole),
-                pl.BlockSpec((slots * rows, 1), whole),
-            ]
-            + [pl.BlockSpec((rows, 2 * HEAD_SIZE), lambda g, m, f: (0, g))] * slots,
-            out_specs=(
-                pl.BlockSpec((rows, HEAD_SIZE), head),
-                pl.BlockSpec((1, 1, rows), lambda g, m, f: (m * groups + g, 0, 0)),
-            ),
+            in_specs=[head] + segs + pairs,
+            out_specs=(head, line),
             scratch_shapes=[
                 pltpu.VMEM((1, rows), jnp.float32),
                 pltpu.VMEM((1, rows), jnp.float32),
@@ -579,41 +589,25 @@
             ],
         ),
         compiler_params=pltpu.CompilerParams(vmem_limit_bytes=VMEM_BYTES),
-        cost_estimate=pl.CostEstimate(
-            flops=3 * rows * rows * width * 4, transcendentals=3 * rows * rows * share * groups, bytes_accessed=8 << 20
-        ),
+        cost_estimate=cost(3 * rows * rows * width * 4, 8 << 20, 3 * rows * rows * share * groups),
         name="attend",
-    )(flags, queries, query_seg, key_seg, *key_values)
+    )(flags, queries, query_seg, key_seg, *[key_values] * slots)
 
 
 def attend_back(flags, queries, grads, lse, cosine, sine, query_seg, key_seg, key_values):
-    rows, width = queries.shape
-    slots, groups = len(key_values), key_values[0].shape[1] // (2 * HEAD_SIZE)
-    share = width // HEAD_SIZE // groups
-    whole = lambda g, m, f: (0, 0)
-    head = lambda g, m, f: (0, m * groups + g)
-    pair = pl.BlockSpec((rows, 2 * HEAD_SIZE), lambda g, m, f: (0, g))
+    rows, width, slots, groups, share, whole, head, line, segs, pairs = attend_specs(queries, key_values)
+    angle = pl.BlockSpec((HEAD_SIZE // 2, rows), whole)
     return pl.pallas_call(
         functools.partial(attend_back_kernel, slots, HEAD_SIZE ** (-0.5)),
         out_shape=(
             jax.ShapeDtypeStruct((rows, width), jnp.bfloat16),
-            jax.ShapeDtypeStruct(key_values[0].shape, jnp.float32),
-        )
-        + (jax.ShapeDtypeStruct(key_values[0].shape, jnp.bfloat16),) * (slots - 1),
+            jax.ShapeDtypeStruct(key_values.shape, jnp.bfloat16),
+        ),
         grid_spec=pltpu.PrefetchScalarGridSpec(
             num_scalar_prefetch=1,
             grid=(groups, share),
-            in_specs=[
-                pl.BlockSpec((rows, HEAD_SIZE), head),
-                pl.BlockSpec((rows, HEAD_SIZE), head),
-                pl.BlockSpec((1, 1, rows), lambda g, m, f: (m * groups + g, 0, 0)),
-                pl.BlockSpec((HEAD_SIZE // 2, rows), whole),
-                pl.BlockSpec((HEAD_SIZE // 2, rows), whole),
-                pl.BlockSpec((1, rows), whole),
-                pl.BlockSpec((slots * rows, 1), whole),
-            ]
-            + [pair] * slots,
-            out_specs=(pl.BlockSpec((rows, HEAD_SIZE), head),) + (pair,) * slots,
+            in_specs=[head, head, line, angle, angle] + segs + pairs,
+            out_specs=(head, pl.BlockSpec((slots * rows, 2 * HEAD_SIZE), lambda g, m, f: (0, g))),
             scratch_shapes=[
                 pltpu.VMEM((slots, rows, rows), jnp.float32),
                 pltpu.VMEM((slots, rows, rows), jnp.float32),
@@ -623,60 +617,373 @@
             ],
         ),
         compiler_params=pltpu.CompilerParams(vmem_limit_bytes=VMEM_BYTES),
-        cost_estimate=pl.CostEstimate(
-            flops=3 * rows * rows * width * 10, transcendentals=3 * rows * rows * share * groups, bytes_accessed=12 << 20
-        ),
+        cost_estimate=cost(3 * rows * rows * width * 10, 12 << 20, 3 * rows * rows * share * groups),
         name="attend_back",
-    )(flags, queries, grads, lse, cosine, sine, query_seg, key_seg, *key_values)
-
-
-def feed_kernel(a_ref, wg_ref, wu_ref, wd_ref, gate_ref, up_ref, hid_ref, out_ref):
-    gate = dot_nt(a_ref[...], wg_ref[...])
-    up = dot_nt(a_ref[...], wu_ref[...])
+    )(flags, queries, grads, lse, cosine, sine, query_seg, key_seg, *[key_values] * slots)
+
+
+def project_kernel(side, a_ref, *refs):
+    slots, (own_ref, send_ref) = refs[:-2], refs[-2:]
+    part = slots[0].shape[0] // 2
+    own = pl.multiple_of(side[0] * part, part)
+    other = pl.multiple_of((1 - side[0]) * part, part)
+    for place, slot in enumerate(ORDER):
+        columns = slice(place * part, (place + 1) * part)
+        send_ref[:, columns] = low(dot_nt(a_ref[...], slots[slot][pl.ds(other, part), :]))
+        own_ref[:, columns] = dot_nt(a_ref[...], slots[slot][pl.ds(own, part), :])
+
+
+def merge_kernel(side, own_ref, other_ref, *refs):
+    slots, out_ref = refs[:-1], refs[-1]
+    part = slots[0].shape[0] // 2
+    own = pl.multiple_of(side[0] * part, part)
+    other = pl.multiple_of((1 - side[0]) * part, part)
+    total = None
+    for place, slot in enumerate(ORDER):
+        columns = slice(place * part, (place + 1) * part)
+        term = dot_nn(own_ref[:, columns], slots[slot][pl.ds(own, part), :])
+        term += dot_nn(other_ref[:, columns], slots[slot][pl.ds(other, part), :])
+        total = term if total is None else total + term
+    out_ref[...] = total
+
+
+def local_call(kernel, name, scalars, operands, outs, flops, scratch=()):
+    vmem = pl.BlockSpec(memory_space=pltpu.VMEM)
+    moved = sum(x.size * x.dtype.itemsize for x in operands)
+    return pl.pallas_call(
+        kernel,
+        out_shape=outs,
+        in_specs=[pl.BlockSpec(memory_space=pltpu.SMEM)] + [vmem] * len(operands),
+        out_specs=jax.tree.map(lambda _: vmem, outs),
+        scratch_shapes=list(scratch),
+        compiler_params=pltpu.CompilerParams(vmem_limit_bytes=VMEM_BYTES),
+        cost_estimate=cost(flops, 2 * moved, 0),
+        name=name,
+    )(scalars, *operands)
+
+
+def project(side, a, slots):
+    rows, width = a.shape[0], slots[0].shape[0] * len(slots) // 2
+    outs = (jax.ShapeDtypeStruct((rows, width), jnp.float32), jax.ShapeDtypeStruct((rows, width), jnp.bfloat16))
+    return local_call(project_kernel, "project", side, [a, *slots], outs, 4 * rows * width * a.shape[1])
+
+
+def merge(side, own, other, slots):
+    outs = jax.ShapeDtypeStruct((own.shape[0], slots[0].shape[1]), jnp.float32)
+    return local_call(merge_kernel, "merge", side, [own, other, *slots], outs, 4 * own.size * slots[0].shape[1])
+
+
+def key_value_kernel(scalars, a_ref, mine_ref, theirs_ref, own_ref, send_ref, all_ref):
+    order, core = scalars[0], scalars[1]
+    count = mine_ref.shape[0] // HEAD_SIZE
+    groups = count // 2
+    for ref, kind in ((mine_ref, core), (theirs_ref, 1 - core)):
+        for slot in range(count):
+            place = slot ^ order
+            lane = pl.multiple_of(((place % groups) * 2 + kind) * HEAD_SIZE, HEAD_SIZE)
+            all_ref[place // groups, :, pl.ds(lane, HEAD_SIZE)] = dot_nt(
+                a_ref[...], ref[slot * HEAD_SIZE : (slot + 1) * HEAD_SIZE, :]
+            )
+    own_ref[...] = all_ref[0]
+    send_ref[...] = low(all_ref[1])
+
+
+def key_value_back_kernel(scalars, own_ref, other_ref, mine_ref, theirs_ref, out_ref, all_ref):
+    order, core = scalars[0], scalars[1]
+    count = mine_ref.shape[0] // HEAD_SIZE
+    groups = count // 2
+    all_ref[0] = own_ref[...]
+    all_ref[1] = other_ref[...]
+    total = None
+    for ref, kind in ((mine_ref, core), (theirs_ref, 1 - core)):
+        for slot in range(count):
+            place = slot ^ order
+            lane = pl.multiple_of(((place % groups) * 2 + kind) * HEAD_SIZE, HEAD_SIZE)
+            term = dot_nn(
+                all_ref[place // groups, :, pl.ds(lane, HEAD_SIZE)], ref[slot * HEAD_SIZE : (slot + 1) * HEAD_SIZE, :]
+            )
+            total = term if total is None else total + term
+    out_ref[...] = total
+
+
+def key_value_project(scalars, a, mine, theirs):
+    rows, width = a.shape[0], mine.shape[0]
+    outs = (jax.ShapeDtypeStruct((rows, width), jnp.float32), jax.ShapeDtypeStruct((rows, width), jnp.bfloat16))
+    return local_call(
+        key_value_kernel, "key_value", scalars, [a, mine, theirs], outs, 4 * rows * width * a.shape[1],
+        [pltpu.VMEM((2, rows, width), jnp.float32)],
+    )
+
+
+def key_value_back(scalars, own, other, mine, theirs):
+    outs = jax.ShapeDtypeStruct((own.shape[0], mine.shape[1]), jnp.float32)
+    return local_call(
+        key_value_back_kernel, "key_value_back", scalars, [own, other, mine, theirs], outs, 4 * own.size * mine.shape[1],
+        [pltpu.VMEM((2, *own.shape), own.dtype)],
+    )
+
+
+def load_block(step, pieces, all_ref):
+    x_ref, ax_ref, by_ref, ay_ref, bx_ref = pieces
+    rows, width = ax_ref.shape
+
+    @pl.when(step == 0)
+    def _():
+        all_ref[:, :width] = x_ref[:rows, :]
+        all_ref[:, width:] = ay_ref[:rows, :]
+
+    @pl.when(step == 1)
+    def _():
+        all_ref[:, :width] = x_ref[rows:, :]
+        all_ref[:, width:] = by_ref[...]
+
+    @pl.when(step == 2)
+    def _():
+        all_ref[:, :width] = ax_ref[...]
+        all_ref[:, width:] = ay_ref[rows:, :]
+
+    @pl.when(step == 3)
+    def _():
+        all_ref[...] = bx_ref[...]
+
+
+def store_block(step, out, outs):
+    a_keep, a_send, b_keep, b_send = outs
+    rows, width = a_keep.shape[0], a_keep.shape[1] // 2
+
+    @pl.when(step == 0)
+    def _():
+        a_keep[...] = out
+
+    @pl.when(step == 2)
+    def _():
+        a_send[...] = out
+
+    for place, at in ((0, 1), (1, 3)):
+
+        @pl.when(step == at)
+        def _(place=place):
+            b_keep[place * rows : (place + 1) * rows, :] = out[:, :width]
+            b_send[place * rows : (place + 1) * rows, :] = out[:, width:]
+
+
+class Weights:
+    def __init__(self, step, sides, held_ref, sems):
+        self.step, self.held_ref = step, held_ref
+        kinds, padded = held_ref.shape[0], held_ref.shape[1] // 2
+        used = sides[0].shape[0] // kinds
+        part = used // N_ROW
+        self.copies = []
+        for kind in range(kinds):
+            self.copies.append([])
+            for side, ref in enumerate(sides):
+                for row in range(N_ROW):
+                    source = ref.at[pl.ds((row * kinds + kind) * part, part), :]
+                    target = held_ref.at[kind, pl.ds(side * padded + row * part, part), :]
+                    sem = sems.at[(kind * len(sides) + side) * N_ROW + row]
+                    self.copies[-1].append(pltpu.make_async_copy(source, target, sem))
+
+        @pl.when(step == 0)
+        def _():
+            for group in self.copies:
+                for copy in group:
+                    copy.start()
+            for kind in range(kinds):
+                for side in range(2):
+                    at = side * padded + used
+                    held_ref[kind, at : at + padded - used, :] = jnp.zeros(
+                        (padded - used, held_ref.shape[2]), held_ref.dtype
+                    )
+
+    def get(self, kind):
+        @pl.when(self.step == 0)
+        def _():
+            for copy in self.copies[kind]:
+                copy.wait()
+
+        return self.held_ref[kind]
+
+
+def gate_up_kernel(*refs):
+    pieces, sides, (gate_ref, up_ref, own_ref, other_ref, all_ref), scratch = refs[:5], refs[5:7], refs[7:-2], refs[-2:]
+    step = pl.program_id(0)
+    weights = Weights(step, sides, *scratch)
+    load_block(step, pieces, all_ref)
+    gate = dot_nt(all_ref[...], weights.get(0))
+    gate_ref[...] = gate
+    up = dot_nt(all_ref[...], weights.get(1))
+    up_ref[...] = up
     hid = low(gate * jax.nn.sigmoid(gate) * up)
-    gate_ref[...] = gate
-    up_ref[...] = up
-    hid_ref[...] = hid
-    out_ref[...] = low(dot_nn(hid, wd_ref[...]))
-
-
-def feed_back_kernel(gm_ref, gate_ref, up_ref, wg_ref, wu_ref, wd_ref, dgate_ref, dup_ref, out_ref):
-    dhid = dot_nt(gm_ref[...], wd_ref[...])
+    half = own_ref.shape[1]
+    own_ref[...] = hid[:, :half]
+    other_ref[...] = hid[:, half:]
+
+
+def down_kernel(own_ref, other_ref, *refs):
+    sides, outs, scratch = refs[:2], refs[2:-2], refs[-2:]
+    step = pl.program_id(0)
+    held = Weights(step, sides, *scratch).get(0)
+    half = own_ref.shape[1]
+    store_block(step, low(dot_nn(own_ref[...], held[:half]) + dot_nn(other_ref[...], held[half:])), outs)
+
+
+def down_back_kernel(*refs):
+    pieces, (gate_ref, up_ref), sides, outs, scratch = refs[:5], refs[5:7], refs[7:9], refs[9:-2], refs[-2:]
+    own_ref, other_ref, all_ref = outs
+    step = pl.program_id(0)
+    weights = Weights(step, sides, *scratch)
+    load_block(step, pieces, all_ref)
+    dhid = dot_nt(all_ref[...], weights.get(0))
     gate, up = gate_ref[...], up_ref[...]
     sigma = jax.nn.sigmoid(gate)
+    half = gate.shape[1] // 2
+    dup = low(dhid * (gate * sigma))
+    own_ref[:, half:] = dup[:, :half]
+    other_ref[:, half:] = dup[:, half:]
     dgate = low(dhid * up * sigma * (1.0 + gate * (1.0 - sigma)))
-    dup = low(dhid * (gate * sigma))
-    dgate_ref[...] = dgate
-    dup_ref[...] = dup
-    out_ref[...] = low(dot_nn(dgate, wg_ref[...]) + dot_nn(dup, wu_ref[...]))
-
-
-def feed_call(kernel, name, wide_in, narrow_in, weights, narrow_out, rows=256):
-    tokens, features = wide_in.shape
-    hidden = weights[0].shape[0]
+    own_ref[:, :half] = dgate[:, :half]
+    other_ref[:, :half] = dgate[:, half:]
+
+
+def gate_up_back_kernel(own_ref, other_ref, *refs):
+    sides, outs, scratch = refs[:2], refs[2:-2], refs[-2:]
+    step = pl.program_id(0)
+    weights = Weights(step, sides, *scratch)
+    half = own_ref.shape[1] // 2
+    total = None
+    for kind in range(2):
+        held = weights.get(kind)
+        columns = slice(kind * half, (kind + 1) * half)
+        term = dot_nn(own_ref[:, columns], held[:half]) + dot_nn(other_ref[:, columns], held[half:])
+        total = term if total is None else total + term
+    store_block(step, low(total), outs)
+
+
+def feed_call(kernel, name, pieces, narrow, sides, kinds, outs, share=SHARE):
+    features = sides[0].shape[1]
+    used = sides[0].shape[0] // kinds
+    hidden = 2 * (-(-used // 256) * 256)
+    blocks = 4
+    rows = (pieces[1].shape[0] if pieces else narrow[0].shape[0] // blocks)
+    once = dict(pipeline_mode=pl.Buffered(1))
+    fixed = lambda shape, **k: pl.BlockSpec(shape, lambda i: (0, 0), **k)
     by_rows = lambda width: pl.BlockSpec((rows, width), lambda i: (i, 0))
-    fixed = pl.BlockSpec((hidden, features), lambda i: (0, 0), pipeline_mode=pl.Buffered(1))
+    if outs:
+        shapes = [jax.ShapeDtypeStruct((blocks * rows, n * hidden // 2), t) for n, t in outs]
+        shapes.append(jax.ShapeDtypeStruct((blocks * rows, features), jnp.bfloat16))
+        specs = [by_rows(x.shape[1]) for x in shapes]
+    else:
+        pair = [(rows, features)] * 2 + [(2 * rows, features // 2)] * 2
+        shapes = [jax.ShapeDtypeStruct(x, jnp.bfloat16) for x in pair]
+        specs = [fixed(x) for x in pair]
     return pl.pallas_call(
         kernel,
-        out_shape=tuple(jax.ShapeDtypeStruct((tokens, hidden), t) for t in narrow_out)
-        + (jax.ShapeDtypeStruct((tokens, features), jnp.bfloat16),),
-        grid=(tokens // rows,),
-        in_specs=[by_rows(features)] + [by_rows(hidden) for _ in narrow_in] + [fixed] * len(weights),
-        out_specs=tuple(by_rows(hidden) for _ in narrow_out) + (by_rows(features),),
+        out_shape=tuple(shapes),
+        grid=(blocks,),
+        in_specs=[fixed(p.shape, **once) for p in pieces]
+        + [by_rows(x.shape[1]) for x in narrow]
+        + [pl.BlockSpec(memory_space=pl.ANY)] * 2,
+        out_specs=tuple(specs),
+        scratch_shapes=[
+            pltpu.VMEM((kinds, hidden, features), jnp.bfloat16),
+            pltpu.SemaphoreType.DMA((kinds * 2 * N_ROW,)),
+        ],
         compiler_params=pltpu.CompilerParams(vmem_limit_bytes=VMEM_BYTES),
-        cost_estimate=pl.CostEstimate(
-            flops=6 * tokens * hidden * features, transcendentals=tokens * hidden, bytes_accessed=40 << 20
-        ),
+        cost_estimate=cost(2 * kinds * blocks * rows * hidden * features, 20 << 20, blocks * rows * hidden, share),
         name=name,
-    )(wide_in, *narrow_in, *weights)
-
-
-def feed(tokens, wg, wu, wd):
-    return feed_call(feed_kernel, "feed", tokens, [], [wg, wu, wd], (jnp.float32, jnp.float32, jnp.bfloat16))
-
-
-def feed_back(grads, gate, up, wg, wu, wd):
-    return feed_call(feed_back_kernel, "feed_back", grads, [gate, up], [wg, wu, wd], (jnp.bfloat16, jnp.bfloat16))
+    )(*pieces, *narrow, *sides)
+
+
+def gate_up(pieces, sides):
+    outs = ((2, jnp.float32), (2, jnp.float32), (1, jnp.bfloat16), (1, jnp.bfloat16))
+    return feed_call(gate_up_kernel, "gate_up", pieces, [], sides, 2, outs)
+
+
+def down(hids, sides):
+    return feed_call(down_kernel, "down", [], hids, sides, 1, None)
+
+
+def down_back(pieces, gate, up, sides):
+    return feed_call(down_back_kernel, "down_back", pieces, [gate, up], sides, 1, ((2, jnp.bfloat16),) * 2)
+
+
+def gate_up_back(both, sides):
+    return feed_call(gate_up_back_kernel, "gate_up_back", [], both, sides, 2, None)
+
+
+def outer_kernel(kinds, used, left_ref, left_far_ref, right_ref, right_far_ref, out_ref):
+    step = pl.program_id(0)
+    block = left_ref.shape[1]
+    blocks = pl.num_programs(0) // kinds
+    part = used // N_ROW
+    total = low(dot_tn(left_ref[...], right_ref[...]) + dot_tn(left_far_ref[...], right_far_ref[...]))
+    for kind in range(kinds):
+        for index in range(-(-used // block)):
+
+            @pl.when(step == kind * blocks + index)
+            def _(kind=kind, index=index):
+                at, end = index * block, min((index + 1) * block, used)
+                while at < end:
+                    row = at // part
+                    stop = min(end, (row + 1) * part)
+                    target = row * kinds * part + kind * part + at - row * part
+                    out_ref[target : target + stop - at, :] = total[at - index * block : stop - index * block, :]
+                    at = stop
+
+
+def outer(lefts, rights, kinds, part):
+    tokens, features = rights[0].shape
+    columns = lefts[0].shape[1]
+    block = 256
+    out_rows = N_ROW * kinds * part
+    once = pl.BlockSpec((tokens, features), lambda i: (0, 0), pipeline_mode=pl.Buffered(1))
+    return pl.pallas_call(
+        functools.partial(outer_kernel, kinds, N_ROW * part),
+        out_shape=jax.ShapeDtypeStruct((out_rows, features), jnp.bfloat16),
+        grid=(columns // block,),
+        in_specs=[pl.BlockSpec((tokens, block), lambda i: (0, i))] * 2 + [once] * 2,
+        out_specs=pl.BlockSpec((out_rows, features), lambda i: (0, 0)),
+        compiler_params=pltpu.CompilerParams(vmem_limit_bytes=VMEM_BYTES),
+        cost_estimate=cost(4 * tokens * columns * features, 8 * tokens * features),
+        name="outer",
+    )(*lefts, *rights)
+
+
+def settle_kernel(kinds, turned, scalars, near_ref, far_ref, other_ref, *refs):
+    outs, held_ref = refs[:-1], refs[-1]
+    d, y = scalars[0], scalars[1]
+    part = near_ref.shape[0] // (2 * kinds)
+    for kind in range(kinds):
+        for slot in range(4):
+            ref = (near_ref, other_ref, far_ref, other_ref)[slot]
+            base = near_ref.shape[0] if slot == 3 else 0
+            for side in range(2):
+                at = ((d ^ slot) * 2 + (y if side == 0 else 1 - y)) * part
+                rows = slice(base + (side * kinds + kind) * part, base + (side * kinds + kind + 1) * part)
+                target = held_ref if turned else outs[kind]
+                target[pl.ds(pl.multiple_of(at, 16), part), :] = wide(ref[rows, :])
+        if turned:
+            outs[kind][...] = jnp.transpose(held_ref[...])
+
+
+def settle(d, y, near, far, other, kinds, turned):
+    width = near.shape[1]
+    hidden = 4 * near.shape[0] // kinds
+    lanes = 256
+    spec = lambda x: pl.BlockSpec((x.shape[0], lanes), lambda i: (0, i))
+    shape = (width, hidden) if turned else (hidden, width)
+    out_spec = pl.BlockSpec((lanes, hidden), lambda i: (i, 0)) if turned else pl.BlockSpec((hidden, lanes), lambda i: (0, i))
+    return pl.pallas_call(
+        functools.partial(settle_kernel, kinds, turned),
+        out_shape=(jax.ShapeDtypeStruct(shape, jnp.float32),) * kinds,
+        grid=(width // lanes,),
+        in_specs=[pl.BlockSpec(memory_space=pltpu.SMEM)] + [spec(x) for x in (near, far, other)],
+        out_specs=(out_spec,) * kinds,
+        scratch_shapes=[pltpu.VMEM((hidden, lanes), jnp.float32)],
+        compiler_params=pltpu.CompilerParams(vmem_limit_bytes=VMEM_BYTES),
+        cost_estimate=cost(hidden * width, 6 * kinds * hidden * width, 0),
+        name="settle",
+    )(jnp.stack([d, y]), near, far, other)
 
 
 def plane_gather(x):
@@ -686,34 +993,43 @@
     b_y = swap(b, "col", 1)
     a_y = swap(jnp.concatenate([a, a_x], axis=0), "col", 1)
     b_x = swap(jnp.concatenate([b, b_y], axis=1), "dp", 2)
-    pieces = [x, a_x, b_y, a_y, b_x]
-    sides = []
-    for x_, a_x_, b_y_, a_y_, b_x_ in (pieces, [swap(piece, "dp", 1) for piece in pieces]):
-        own = jnp.concatenate([x_, a_x_, b_x_[:, : x.shape[1]]], axis=0)
-        other = jnp.concatenate([a_y_[:half], b_y_, a_y_[half:], b_x_[:, x.shape[1] :]], axis=0)
-        sides.append(jnp.concatenate([own, other], axis=1))
-    return jnp.concatenate(sides, axis=0)
-
-
-def plane_scatter(p):
-    rows, width = p.shape[0] // 2, p.shape[1] // 2
-    half = rows // 4
-    q = wide(p[:rows]) + wide(swap(p[rows:], "dp", 1))
-    a_x = swap(low(q[2 * half : 3 * half]), "dp", 2)
-    b_y = swap(low(jnp.concatenate([q[half : 2 * half, width:], q[3 * half :, width:]], axis=0)), "col", 1)
-    a = q[:half] + wide(a_x)
-    b = jnp.concatenate([q[half : 2 * half, :width], q[3 * half :, :width]], axis=0) + wide(b_y)
-    a_y = swap(low(a[:, width:]), "col", 1)
-    b_x = swap(low(b[half:]), "dp", 2)
-    return jnp.concatenate([a[:, :width] + wide(a_y), b[:half] + wide(b_x)], axis=0)
+    return [x, a_x, b_y, a_y, b_x]
+
+
+def plane_scatter(parts):
+    a_keep, a_send, b_keep, b_send = parts
+    half, width = a_keep.shape[0], b_keep.shape[1]
+    a_x = swap(a_send, "dp", 2)
+    b_y = swap(b_send, "col", 1)
+    a_y = swap(low(wide(a_keep[:, width:]) + wide(a_x[:, width:])), "col", 1)
+    b_x = swap(low(wide(b_keep[half:]) + wide(b_y[half:])), "dp", 2)
+    return jnp.concatenate(
+        [
+            wide(a_keep[:, :width]) + wide(a_x[:, :width]) + wide(a_y),
+            wide(b_keep[:half]) + wide(b_y[:half]) + wide(b_x),
+        ],
+        axis=0,
+    )
 
 
 def dp_slots(x):
     far = swap(x, "dp", 2)
-    return [x, swap(x, "dp", 1), far, swap(far, "dp", 1)]
-
-
-def home(slots, order):
+    other = swap(jnp.concatenate([x, far], axis=0), "dp", 1)
+    return [x, other[: x.shape[0]], far, other[x.shape[0] :]]
+
+
+def heads_near(own, other, right, y):
+    half = own.shape[1] // 2
+    odd = low(dot_tn(jnp.concatenate([own[:, half:], other[:, half:]], axis=1), right))
+    odd = swap(odd, "dp", 1)
+    even = dot_tn(jnp.concatenate([own[:, :half], other[:, :half]], axis=1), right)
+    part = half // 2
+    total = [even[i * part : (i + 1) * part] + wide(odd[i * part : (i + 1) * part]) for i in range(4)]
+    far = swap(low(jnp.concatenate([total[1], total[3]], axis=0)), "dp", 2)
+    return xor_order([low(total[0] + wide(far[:part])), low(total[2] + wide(far[part:]))], y)
+
+
+def quarters_home(slots, order):
     odd = swap(low(jnp.concatenate([slots[1], slots[3]], axis=0)), "dp", 1)
     count = slots[0].shape[0]
     near = wide(slots[0]) + wide(odd[:count])
@@ -746,47 +1062,28 @@
     rows, width = states.shape
     n_row, n_col, n_dp = lax.axis_size("row"), lax.axis_size("col"), lax.axis_size("dp")
     d, r, y = lax.axis_index("dp"), lax.axis_index("row"), lax.axis_index("col")
+    core = d % 2
     groups = n_row // n_col
     features = width * n_col
-    heads_row = w_query.shape[1] // HEAD_SIZE
     order = r ^ (y * groups)
-
-    def along_row(x):
-        return xor_order([x] + [swap(x, "row", k) for k in range(1, n_row)], order)
-
-    kv_t = jnp.concatenate([key_projection.T, value_projection.T], axis=0)
-    kv_part = kv_t.shape[0] // n_dp
-    kv_rows = jnp.concatenate(along_row(rows_of(kv_t, d * kv_part, kv_part)), axis=0)
-    kv_slots = xor_order(dp_slots(kv_rows), d)
-
-    def kv_weights(side):
-        lo = side * groups * kv_part
-        return jnp.concatenate(
-            [s[lo + g * kv_part : lo + (g + 1) * kv_part] for g in range(groups) for s in kv_slots], axis=0
-        )
-
-    wkv = [kv_weights(0), kv_weights(1)]
-    q_part = jnp.concatenate(along_row(rows_of(w_query, d * HEAD_SIZE, HEAD_SIZE, 1).T), axis=0)
-    q_slots = dp_slots(q_part)
-    side_rows = groups * HEAD_SIZE
-    wq = [
-        jnp.concatenate([q_slots[m][s * side_rows : (s + 1) * side_rows] for m in ORDER], axis=0) for s in (0, 1)
-    ]
-    o_part = jnp.concatenate(along_row(rows_of(w_out, d * HEAD_SIZE, HEAD_SIZE)), axis=0)
-    o_slots = dp_slots(o_part)
-    wo = [
-        jnp.concatenate([o_slots[m][s * side_rows : (s + 1) * side_rows] for m in ORDER], axis=0) for s in (0, 1)
-    ]
+    side = y.reshape(1)
+    kv_scalars = jnp.stack([order, core])
+
+    kv_mine = jnp.where(core == 0, key_projection, value_projection).T
+    kv_mine = jnp.concatenate([kv_mine] + [swap(kv_mine, "row", k) for k in range(1, n_row)], axis=0)
+    kv_theirs = swap(kv_mine, "dp", 1)
+
+    heads = [rows_of(w_query, d * HEAD_SIZE, HEAD_SIZE, 1).T, rows_of(w_out, d * HEAD_SIZE, HEAD_SIZE)]
+    heads = gather_rows(jnp.concatenate(heads, axis=0))
 
     inner = w_down.shape[0]
     inner_part = inner // (n_dp * n_col)
 
-    def hidden_rows(w):
-        own = rows_of(w, (d * n_col + y) * inner_part, inner_part)
-        other = rows_of(w, (d * n_col + (1 - y)) * inner_part, inner_part)
-        return gather_rows(jnp.concatenate([own, swap(other, "col", 1)], axis=1))
-
-    wg, wu, wd = hidden_rows(w_gate.T), hidden_rows(w_up.T), hidden_rows(w_down)
+    def hidden_rows(at):
+        return jnp.concatenate([rows_of(w, at * inner_part, inner_part) for w in (w_gate.T, w_up.T, w_down)], axis=0)
+
+    hidden_other = after(swap(hidden_rows(d * n_col + (1 - y)), "col", 1), kv_theirs)
+    hidden_own = hidden_rows(d * n_col + y)
 
     positions, segment, counted = token_layout(cont_ids, answer_len)
     row_start = r * rows
@@ -803,7 +1100,7 @@
         least, most = jnp.min(key_segs[k]), jnp.max(key_segs[k])
         active = (r >= k) & ((least < 0) | (most >= jnp.min(query_seg)))
         flags.append(jnp.where(active, jnp.where(most < 0, 1, 2), 0).astype(jnp.int32))
-    flags = jnp.stack(flags)
+    flags = jnp.stack(flags + [(r - k) % n_row for k in range(n_row)])
     key_seg = jnp.concatenate(key_segs)[:, None]
     query_seg = query_seg[None, :]
     freqs = ROPE_BASE ** (-2.0 * jnp.arange(HEAD_SIZE // 2, dtype=jnp.float32) / HEAD_SIZE)
@@ -818,15 +1115,10 @@
         turned = jnp.concatenate([x[:, half:], x[:, :half]], axis=1)
         return x * cos_n + turned * (sign * sin_n)
 
-    def turn_heads(x, sign):
-        return jnp.concatenate(
-            [turn(x[:, i : i + HEAD_SIZE], sign) for i in range(0, x.shape[1], HEAD_SIZE)], axis=1
-        )
-
-    def turn_keys(x, sign):
+    def turn_heads(x, sign, every):
         return jnp.concatenate(
             [
-                turn(x[:, i : i + HEAD_SIZE], sign) if i % (2 * HEAD_SIZE) == 0 else x[:, i : i + HEAD_SIZE]
+                turn(x[:, i : i + HEAD_SIZE], sign) if i % every == 0 else x[:, i : i + HEAD_SIZE]
                 for i in range(0, x.shape[1], HEAD_SIZE)
             ],
             axis=1,
@@ -836,75 +1128,112 @@
     squares = jnp.sum(states_f * states_f, axis=1)
     scale_attn = lax.rsqrt((squares + swap(squares, "col", 1)) / features + EPSILON)[:, None]
     a1 = low(states_f * scale_attn * gain_attn[None, :])
-    kv_sum = dot_nt(a1, wkv[0]) + wide(swap(low(dot_nt(a1, wkv[1])), "col", 1))
-    key_value = low(turn_keys(kv_sum, 1.0))
-    key_values = [key_value] + [
-        lax.ppermute(key_value, "row", [(i, i + k) for i in range(n_row - k)]) for k in range(1, n_row)
+    kv_own, kv_send = key_value_project(kv_scalars, a1, kv_mine, kv_theirs)
+    kv_received, heads, count = lax.optimization_barrier((swap(kv_send, "col", 1), heads, count))
+    key_value = low(turn_heads(kv_own + wide(kv_received), 1.0, 2 * HEAD_SIZE))
+    key_values = gather_rows(key_value)
+    q_part, o_part = [
+        jnp.concatenate([heads[(2 * i + j) * HEAD_SIZE : (2 * i + j + 1) * HEAD_SIZE] for i in range(n_row)], axis=0)
+        for j in (0, 1)
     ]
-    q_sum = dot_nt(a1, wq[0]) + wide(swap(low(dot_nt(a1, wq[1])), "col", 1))
-    queries = low(turn_heads(q_sum, 1.0))
+    q_far = swap(q_part, "dp", 2)
+    q_slots = [q_part, swap(q_part, "dp", 1), q_far, swap(q_far, "dp", 1)]
+    q_own, q_send = project(side, a1, q_slots)
+    hidden_own, hidden_other = lax.optimization_barrier((hidden_own, hidden_other, key_values, q_send))[:2]
+    hidden_mine = jnp.concatenate([hidden_own, hidden_other], axis=1)
+    gate_up_mine = gather_rows(hidden_mine[: 2 * inner_part])
+    down_mine = gather_rows(hidden_mine[2 * inner_part :])
+    queries = low(turn_heads(q_own + wide(swap(q_send, "col", 1)), 1.0, HEAD_SIZE))
+    o_slots = dp_slots(after(o_part, q_send))
+    queries, *o_slots = lax.optimization_barrier((queries, *o_slots))
     context, lse = attend(flags, queries, query_seg, key_seg, key_values)
     context_other = swap(context, "col", 1)
-    attention = dot_nn(context, wo[0]) + dot_nn(context_other, wo[1])
-    hidden_res = states_f + keep_here * attention
+    hidden_res = states_f + keep_here * merge(side, context, context_other, o_slots)
 
     squares = jnp.sum(hidden_res * hidden_res, axis=1)
     scale_ffn = lax.rsqrt((squares + swap(squares, "col", 1)) / features + EPSILON)[:, None]
     a2 = low(hidden_res * scale_ffn * gain_ffn[None, :])
-    a2_all = plane_gather(a2)
-    gate, up, hidden, parts = feed(a2_all, wg, wu, wd)
-    result = hidden_res + keep_here * plane_scatter(parts)
+    a2_pieces = plane_gather(a2)
+    gate_up_mine = after(gate_up_mine, a2_pieces[1])
+    gate_up_sides = [gate_up_mine, swap(gate_up_mine, "dp", 1)]
+    gate, up, *hids, a2_all = gate_up(a2_pieces, gate_up_sides)
+    down_mine = after(down_mine, gate)
+    down_sides = [down_mine, swap(down_mine, "dp", 1)]
+    result = hidden_res + keep_here * plane_scatter(down(hids, down_sides))
     error = result - wide(teacher)
-    error_total = jnp.sum(counted_here * error * error).reshape(1)
-    for axis, mask in (("dp", 1), ("dp", 2), ("col", 1), ("row", 1), ("row", 2)):
-        error_total = error_total + swap(error_total, axis, mask)
-    loss = error_total[0] / (count * features)
+    error_part = jnp.sum(counted_here * error * error)
     grad_result = wide(out_grad) + 2.0 / (count * features) * counted_here * error
 
-    gm_all = plane_gather(low(keep_here * grad_result))
-    dgate, dup, parts = feed_back(gm_all, gate, up, wg, wu, wd)
-    grad_normed_ffn = plane_scatter(parts)
-
-    def hidden_home(left, right):
-        part = lax.psum_scatter(low(dot_tn(left, right)), "row", scatter_dimension=0, tiled=True)
-        own, other = part[:, :width], swap(part[:, width:], "col", 1)
-        pair = jnp.concatenate(xor_order([own, other], y), axis=0)
-        return lax.all_gather(pair, "dp", axis=0, tiled=True)
-
-    grad_down = wide(hidden_home(hidden, gm_all))
-    grad_gate = wide(hidden_home(dgate, a2_all).T)
-    grad_up = wide(hidden_home(dup, a2_all).T)
+    gm_pieces = plane_gather(low(keep_here * grad_result))
+    def both_cores(own, other):
+        return [own, swap(other, "dp", 1)]
+
+    hids, a2_sides = both_cores(*hids), both_cores(a2_all, a2_all)
+    gate, *hids_sides = lax.optimization_barrier((gate, *hids, *a2_sides))
+    hids, a2_sides = hids_sides[:2], hids_sides[2:]
+    *dboth, gm_all = down_back(gm_pieces, gate, up, down_sides)
+
+    def along_row(x):
+        return lax.psum_scatter(x, "row", scatter_dimension=0, tiled=True)
+
+    down_joined = outer(hids, both_cores(gm_all, gm_all), 1, inner_part)
+    dboth_sides = both_cores(*dboth)
+    *dboth, down_joined = lax.optimization_barrier((*dboth, *dboth_sides, down_joined))
+    dboth, dboth_sides = dboth[:2], dboth[2:]
+    down_part = along_row(down_joined)
+    grad_normed_ffn = plane_scatter(gate_up_back(dboth, gate_up_sides))
+    gate_up_joined = outer(dboth_sides, a2_sides, 2, inner_part)
+    grad_normed_ffn, gate_up_joined = lax.optimization_barrier((grad_normed_ffn, gate_up_joined))
+    gate_up_joined, down_part = lax.optimization_barrier((gate_up_joined, down_part))
+    gate_up_part = along_row(gate_up_joined)
+
+    def hidden_near(part):
+        near = jnp.concatenate([part[:, :width], swap(part[:, width:], "col", 1)], axis=0)
+        return near, swap(near, "dp", 2)
+
+    def hidden_home(near, far, kinds, turned):
+        other = swap(jnp.concatenate([near, far], axis=0), "dp", 1)
+        return settle(d, y, near, far, other, kinds, turned)
+
     gain_ffn_sum = jnp.sum(grad_normed_ffn * hidden_res * scale_ffn, axis=0)
     weighted = grad_normed_ffn * gain_ffn[None, :]
     inner_sum = jnp.sum(weighted * hidden_res, axis=1)
-    inner_sum = (inner_sum + swap(inner_sum, "col", 1))[:, None]
+    inner_sum = jnp.concatenate([inner_sum, jnp.full((128,), error_part)])
+    inner_sum = inner_sum + swap(inner_sum, "col", 1)
+    error_col = inner_sum[rows:]
+    inner_sum = inner_sum[:rows, None]
     grad_hidden_res = grad_result + scale_ffn * weighted - hidden_res * scale_ffn**3 * inner_sum / features
 
     ga = low(keep_here * grad_hidden_res)
-    grad_context = low(dot_nt(ga, wo[0]) + wide(swap(low(dot_nt(ga, wo[1])), "col", 1)))
-    dq, *dkv_parts = attend_back(flags, queries, grad_context, lse, cos_t, sin_t, query_seg, key_seg, key_values)
-    dkv_sum = dkv_parts[0]
-    for k in range(1, n_row):
-        dkv_sum += wide(lax.ppermute(dkv_parts[k], "row", [(i + k, i) for i in range(n_row - k)]))
-    dkv = low(turn_keys(wide(low(dkv_sum)), -1.0))
+    do_own, do_send = project(side, ga, o_slots)
+    do_received, *down_near = lax.optimization_barrier((swap(do_send, "col", 1), *hidden_near(down_part)))
+    grad_context = low(do_own + wide(do_received))
+    dq, dkv_parts = attend_back(flags, queries, grad_context, lse, cos_t, sin_t, query_seg, key_seg, key_values)
+    context, context_other, ga, gate_up_part = lax.optimization_barrier((context, context_other, ga, gate_up_part, dq))[:4]
+    gate_up_near = hidden_near(gate_up_part)
+    dkv_sum, *gate_up_near = lax.optimization_barrier((along_row(dkv_parts), *gate_up_near))
+    (grad_down,) = hidden_home(*down_near, 1, False)
+    grad_gate, grad_up = hidden_home(*gate_up_near, 2, True)
+    dkv = low(turn_heads(wide(dkv_sum), -1.0, 2 * HEAD_SIZE))
     dq_other = swap(dq, "col", 1)
     dkv_other = swap(dkv, "col", 1)
-    grad_normed_attn = (
-        dot_nn(dq, wq[0]) + dot_nn(dq_other, wq[1]) + dot_nn(dkv, wkv[0]) + dot_nn(dkv_other, wkv[1])
-    )
-
-    def head_slots(own, other):
-        sides = [x.reshape(n_dp, groups, HEAD_SIZE, width) for x in (own, other)]
-        return [jnp.concatenate([s[ORDER.index(m)] for s in sides], axis=0) for m in range(n_dp)]
-
-    grad_out = wide(jnp.concatenate(home(head_slots(dot_tn(context, ga), dot_tn(context_other, ga)), order), axis=0))
-    grad_query = wide(jnp.concatenate(home(head_slots(dot_tn(dq, a1), dot_tn(dq_other, a1)), order), axis=0).T)
+    grad_normed_attn = merge(side, dq, dq_other, q_slots) + key_value_back(
+        kv_scalars, dkv, dkv_other, kv_mine, kv_theirs
+    )
+
+    near = [heads_near(dq, dq_other, a1, y), heads_near(context, context_other, ga, y)]
+    near = [x[g * HEAD_SIZE : (g + 1) * HEAD_SIZE] for p in range(2) for g in range(groups) for x in (near[0][p], near[1][p])]
+    near = along_row(after(jnp.concatenate(near, axis=0), dkv_sum))
+    near = xor_order(dp_slots(near), d)
+    grad_query = wide(jnp.concatenate([x[:HEAD_SIZE] for x in near], axis=0).T)
+    grad_out = wide(jnp.concatenate([x[HEAD_SIZE:] for x in near], axis=0))
+    kv_part = 2 * HEAD_SIZE // n_dp
     dwkv = jnp.concatenate(
         [x.reshape(groups, n_dp, kv_part, width) for x in (dot_tn(dkv, a1), dot_tn(dkv_other, a1))], axis=0
     )
-    dwkv = jnp.concatenate(home(xor_order([dwkv[:, i] for i in range(n_dp)], d), order), axis=0)
-    grad_key = wide(dwkv[: kv_t.shape[0] // 2].T)
-    grad_value = wide(dwkv[kv_t.shape[0] // 2 :].T)
+    dwkv = jnp.concatenate(quarters_home(xor_order([dwkv[:, i] for i in range(n_dp)], d), order), axis=0)
+    grad_key = wide(dwkv[:HEAD_SIZE].T)
+    grad_value = wide(dwkv[HEAD_SIZE:].T)
 
     gain_attn_sum = jnp.sum(grad_normed_attn * states_f * scale_attn, axis=0)
     weighted = grad_normed_attn * gain_attn[None, :]
@@ -912,21 +1241,19 @@
     inner_sum = (inner_sum + swap(inner_sum, "col", 1))[:, None]
     grad_states = grad_hidden_res + scale_attn * weighted - states_f * scale_attn**3 * inner_sum / features
 
-    gains = []
-    for gain in (gain_attn_sum, gain_ffn_sum):
-        for axis, mask in (("dp", 1), ("dp", 2), ("row", 1), ("row", 2)):
-            gain = gain + swap(gain, axis, mask)
-        gains.append(gain)
+    sums = jnp.concatenate([gain_attn_sum, gain_ffn_sum, error_col])
+    for axis, mask in (("dp", 1), ("dp", 2), ("row", 1), ("row", 2)):
+        sums = sums + swap(sums, axis, mask)
     return (
         low(result),
-        loss,
+        sums[2 * width] / (count * features),
         grad_states,
-        gains[0],
+        sums[:width],
         grad_query,
         grad_key,
         grad_value,
         grad_out,
-        gains[1],
+        sums[width : 2 * width],
         grad_gate,
         grad_up,
         grad_down,

time: 1050 us -> 864 us (0.82)
  Pallas kernels: 85.2 us -> 183 us
  other arithmetic: 167 us -> 92.2 us
  waiting for transfers between devices: 471 us -> 398 us
  starting transfers between devices: 147 us -> 81.8 us
  matrix products: 65.6 us -> 11.4 us
  local copies, waits for them, and re-layouts: 82.6 us -> 59.8 us
    pallas_call x2 -> x14, Pallas kernels: 60.2 us -> 158 us  [the longest x4 73.1 us: feed_call(): pl.pallas_call(kernel, out_shape=tuple(shapes), grid=(blocks,), in_specs=...]
    concatenate x20 -> x21, other arithmetic: 85 us -> 20.5 us  [the longest x2 5.53 us: hidden_home(): other = swap(jnp.concatenate([near, far], axis=0), 'dp', 1)]
    reduce_scatter x3 -> x4, waiting for transfers between devices: 66.7 us -> 15.5 us  [along_row(): return lax.psum_scatter(x, 'row', scatter_dimension=0, tiled=True)]
    ppermute x101 -> x67, waiting for transfers between devices: 305 us -> 357 us  [swap(): return lax.ppermute(values, axis, [(i, i ^ mask) for i in range(size)])]
    ppermute x6 -> x0, waiting for transfers between devices: 50.6 us -> none  [the longest x3 40.6 us: fast_body(): lax.ppermute(dkv_parts[k], 'row', [(i + k, i) for i in range(n_row - k)])]
    ppermute x101 -> x67, starting transfers between devices: 130 us -> 80.8 us  [swap(): return lax.ppermute(values, axis, [(i, i ^ mask) for i in range(size)])]
    dot_general x9 -> x6, matrix products: 40.5 us -> 11.4 us  [dot_tn(): lax.dot_general(left, right, (((0,), (0,)), ((), ())), preferred_element_...]
    dot_general x12 -> x0, matrix products: 25.1 us -> none  [the longest x6 14 us: dot_nt(): lax.dot_general(left, right, (((1,), (1,)), ((), ())), preferred_element_...]
  transfers between devices with their start and end apart: 116 -> 75, of which waited for: 52 -> 41; matrix products, arithmetic and copies ran while one was open for 23% -> 15% of each run, Pallas kernels for 2% -> 18%
where the time goes in v2:
time: 864 us; the launch traced here: 854 us
  waiting for transfers between devices  398 us (46%)
  Pallas kernels  183 us (21%)
  other arithmetic  92.2 us (11%)
  starting transfers between devices  81.8 us (9%)
  local copies, waits for them, and re-layouts  59.8 us (7%)
  between operations  28 us (3%)
  matrix products  11.4 us (1%)
    ppermute x67, waiting for transfers between devices, swap(): return lax.ppermute(values, axis, [(i, i ^ mask) for i in range(size)])  357 us
    ppermute x67, starting transfers between devices, swap(): return lax.ppermute(values, axis, [(i, i ^ mask) for i in range(size)])  80.8 us
    pallas_call x4, Pallas kernels, feed_call(): pl.pallas_call(kernel, out_shape=tuple(shapes), grid=(blocks,), in_specs=...  73.1 us
    pallas_call x6, Pallas kernels, local_call(): pl.pallas_call(kernel, out_shape=outs, in_specs=[pl.BlockSpec(memory_spac...  37.1 us
    pallas_call x2, Pallas kernels, outer(): pl.pallas_call(functools.partial(outer_kernel, kinds, N_ROW * part), out_...  34.5 us
    unnamed x218, local copies, waits for them, and re-layouts  30.1 us
    all_gather x4, waiting for transfers between devices, gather_rows(): return lax.all_gather(values, 'row', axis=0, tiled=True)  25.7 us
    convert_element_type x11, other arithmetic, low(): return values.astype(jnp.bfloat16)  20.3 us
  transfers between devices with their start and end apart: 75, of which 41 were waited for; matrix products, arithmetic and copies ran while one was open for 15% of the time, Pallas kernels for 18%

profile of v2, /device:TPU:0, one launch (start us, length us, event | category | flops | bytes accessed | tf_op | source)
XLA Modules:
  0.0 853.6 jit_solution(12242256036347048128)
XLA Ops:
  18.8 8.6 %collective-permute-done.1 = bf16[128,1024]{1,0:T(8,128)(2,1)S(1)} collective-permute-done((bf16[128,1024]{1,0:T(8,128)(2,1)S(1)}, bf16[128,1024]{1,0:T(8,128)(2,1)S(1)}, u32[]{:S(2)}, u32[]{:S(2)}) %collective-permute-start.1) | collective-permute-done | bytes 262176 | tf_op jit(solution)/shard_map/ppermute | solution.py:406
  27.4 12.7 %collective-permute-done.2 = bf16[128,1024]{1,0:T(8,128)(2,1)S(1)} collective-permute-done((bf16[128,1024]{1,0:T(8,128)(2,1)S(1)}, bf16[128,1024]{1,0:T(8,128)(2,1)S(1)}, u32[]{:S(2)}, u32[]{:S(2)}) %collective-permute-start.2) | collective-permute-done | bytes 262176 | tf_op jit(solution)/shard_map/ppermute | solution.py:406
  48.1 5.5 key_value.1
  61.8 5.9 collective-permute-done.5
  67.7 6.1 all-gather.5.cloned.1.call-done
  79.8 3.8 constant_dynamic-slice_fusion.2
  91.2 12.4 %collective-permute-done.9.refs_2_ = bf16[512,1024]{1,0:T(8,128)(2,1)} collective-permute-done((bf16[512,1024]{1,0:T(8,128)(2,1)S(1)}, bf16[512,1024]{1,0:T(8,128)(2,1)}, u32[]{:S(2)}, u32[]{:S(2)}) %collective-permute-start.9) | collective-permute-done | bytes 1048608 | tf_op jit(solution)/shard_map/ppermute | solution.py:406
  105.8 9.6 %collective-permute-done.20 = bf16[528,1024]{1,0:T(8,128)(2,1)} collective-permute-done((bf16[528,1024]{1,0:T(8,128)(2,1)}, bf16[528,1024]{1,0:T(8,128)(2,1)}, u32[]{:S(2)}, u32[]{:S(2)}) %collective-permute-start.20) | collective-permute-done | bytes 1081376 | tf_op jit(solution)/shard_map/ppermute | solution.py:406
  115.4 6.5 project.2
  122.0 11.4 %all-gather.7.cloned.1.call-done.refs_0_.refs_1_.refs_2_.refs_3_ = bf16[2048,512]{1,0:T(8,128)(2,1)} async-done(((bf16[512,512]{1,0:T(8,128)(2,1)}), bf16[2048,512]{1,0:T(8,128)(2,1)}) %all-gather.7.cloned.1.call-update) | async-done | bytes 2097168 | tf_op jit(solution)/shard_map/all_gather | solution.py:67
  152.3 10.6 %collective-permute-done.12.refs_2_ = bf16[512,1024]{1,0:T(8,128)(2,1)S(1)} collective-permute-done((bf16[512,1024]{1,0:T(8,128)(2,1)S(1)}, bf16[512,1024]{1,0:T(8,128)(2,1)S(1)}, u32[]{:S(2)}, u32[]{:S(2)}) %collective-permute-start.12) | collective-permute-done | bytes 1048608 | tf_op jit(solution)/shard_map/ppermute | solution.py:406
  170.5 10.2 %attend.1 = (bf16[512,1024]{1,0:T(8,128)(2,1)}, f32[8,1,512]{2,1,0:T(1,128)}) custom-call(s32[8]{0:T(128)} %stack.50.flags, bf16[512,1024]{1,0:T(8,128)(2,1)} %copy-done.32, s32[1,512]{1,0:T(1,128)} %get-tuple-element.327.qseg_ref, s32[2048,1]{1,0:T(8,128)} %copy.66.kseg_ref, bf16[2048,512]{1,0:T(8,128)(2,1)} %all-gather.7.cloned.1.call-done.refs_0_.refs_1_.refs_2_.refs_3_, ...), custom_call_target="tpu_custom_call" | custom-call | flops 322122560 | bytes 838860 | tf_op jit(solution)/shard_map/attend/pallas_call | solution.py:574
  182.2 23.9 %collective-permute-done.14.other_ref = bf16[512,1024]{1,0:T(8,128)(2,1)S(1)} collective-permute-done((bf16[512,1024]{1,0:T(8,128)(2,1)}, bf16[512,1024]{1,0:T(8,128)(2,1)S(1)}, u32[]{:S(2)}, u32[]{:S(2)}) %collective-permute-start.14) | collective-permute-done | bytes 1048608 | tf_op jit(solution)/shard_map/ppermute | solution.py:406
  207.0 6.5 merge.2
  223.6 11.2 %collective-permute-done.16.refs_1_ = bf16[256,1024]{1,0:T(8,128)(2,1)S(1)} collective-permute-done((bf16[256,1024]{1,0:T(8,128)(2,1)S(1)}, bf16[256,1024]{1,0:T(8,128)(2,1)S(1)}, u32[]{:S(2)}, u32[]{:S(2)}) %collective-permute-start.16) | collective-permute-done | bytes 524320 | tf_op jit(solution)/shard_map/ppermute | solution.py:406
  234.8 8.2 all-gather.9.cloned.1.call-done.refs_5_.refs_0_
  246.9 13.0 %collective-permute-done.17.refs_2_ = bf16[256,1024]{1,0:T(8,128)(2,1)S(1)} collective-permute-done((bf16[256,1024]{1,0:T(8,128)(2,1)}, bf16[256,1024]{1,0:T(8,128)(2,1)S(1)}, u32[]{:S(2)}, u32[]{:S(2)}) %collective-permute-start.17) | collective-permute-done | bytes 524320 | tf_op jit(solution)/shard_map/ppermute | solution.py:406
  264.4 21.8 %collective-permute-done.19.refs_4_ = bf16[256,2048]{1,0:T(8,128)(2,1)S(1)} collective-permute-done((bf16[256,2048]{1,0:T(8,128)(2,1)S(1)}, bf16[256,2048]{1,0:T(8,128)(2,1)S(1)}, u32[]{:S(2)}, u32[]{:S(2)}) %collective-permute-start.19) | collective-permute-done | bytes 1048608 | tf_op jit(solution)/shard_map/ppermute | solution.py:406
  288.5 22.3 %gate_up.1 = (f32[1024,1536]{1,0:T(8,128)}, f32[1024,1536]{1,0:T(8,128)}, bf16[1024,768]{1,0:T(8,128)(2,1)}, bf16[1024,768]{1,0:T(8,128)(2,1)}, bf16[1024,2048]{1,0:T(8,128)(2,1)}) custom-call(bf16[512,1024]{1,0:T(8,128)(2,1)} %copy-done.26, bf16[256,1024]{1,0:T(8,128)(2,1)} %copy-done.53, bf16[256,1024]{1,0:T(8,128)(2,1)} %copy-done.56, ...), custom_call_target="tpu_custom_call" | custom-call | flops 1288490240 | bytes 2097152 | tf_op jit(solution)/shard_map/gate_up/pallas_call | solution.py:879
  310.9 5.6 collective-permute-done.22.refs_1_.refs_8_
  316.5 13.5 %down.1 = (bf16[256,2048]{1,0:T(8,128)(2,1)}, bf16[256,2048]{1,0:T(8,128)(2,1)}, bf16[512,1024]{1,0:T(8,128)(2,1)}, bf16[512,1024]{1,0:T(8,128)(2,1)}) custom-call(bf16[1024,768]{1,0:T(8,128)(2,1)} %get-tuple-element.110.own_ref.left_ref, bf16[1024,768]{1,0:T(8,128)(2,1)} %get-tuple-element.97.other_ref, ...), custom_call_target="tpu_custom_call" | custom-call | flops 644245120 | bytes 2097152 | tf_op jit(solution)/shard_map/down/pallas_call | solution.py:879
  332.8 22.7 %collective-permute-done.23 = bf16[256,2048]{1,0:T(8,128)(2,1)S(1)} collective-permute-done((bf16[256,2048]{1,0:T(8,128)(2,1)}, bf16[256,2048]{1,0:T(8,128)(2,1)S(1)}, u32[]{:S(2)}, u32[]{:S(2)}) %collective-permute-start.23) | collective-permute-done | bytes 1048608 | tf_op jit(solution)/shard_map/ppermute | solution.py:406
  363.6 7.6 collective-permute-done.24
  381.6 10.3 %collective-permute-done.28.refs_2_ = bf16[256,1024]{1,0:T(8,128)(2,1)S(1)} collective-permute-done((bf16[256,1024]{1,0:T(8,128)(2,1)S(1)}, bf16[256,1024]{1,0:T(8,128)(2,1)S(1)}, u32[]{:S(2)}, u32[]{:S(2)}) %collective-permute-start.28) | collective-permute-done | bytes 524320 | tf_op jit(solution)/shard_map/ppermute | solution.py:406
  395.0 19.8 %collective-permute-done.30.refs_4_ = bf16[256,2048]{1,0:T(8,128)(2,1)} collective-permute-done((bf16[256,2048]{1,0:T(8,128)(2,1)S(1)}, bf16[256,2048]{1,0:T(8,128)(2,1)}, u32[]{:S(2)}, u32[]{:S(2)}) %collective-permute-start.30) | collective-permute-done | bytes 1048608 | tf_op jit(solution)/shard_map/ppermute | solution.py:406
  416.3 16.5 %down_back.1 = (bf16[1024,1536]{1,0:T(8,128)(2,1)}, bf16[1024,1536]{1,0:T(8,128)(2,1)}, bf16[1024,2048]{1,0:T(8,128)(2,1)}) custom-call(bf16[512,1024]{1,0:T(8,128)(2,1)} %copy-done.21, bf16[256,1024]{1,0:T(8,128)(2,1)} %copy-done.55, bf16[256,1024]{1,0:T(8,128)(2,1)} %copy-done.54, bf16[512,1024]{1,0:T(8,128)(2,1)} %copy-done.70, ...), custom_call_target="tpu_custom_call" | custom-call | flops 644245120 | bytes 2097152 | tf_op jit(solution)/shard_map/down_back/pallas_call | solution.py:879
  433.4 7.0 collective-permute-done.34.right_far_ref
  440.4 13.2 %outer.2 = bf16[704,2048]{1,0:T(8,128)(2,1)} custom-call(bf16[1024,768]{1,0:T(8,128)(2,1)} %get-tuple-element.110.own_ref.left_ref, bf16[1024,768]{1,0:T(8,128)(2,1)} %collective-permute-done.31.left_far_ref, bf16[1024,2048]{1,0:T(8,128)(2,1)} %get-tuple-element.112.right_ref, bf16[1024,2048]{1,0:T(8,128)(2,1)} %collective-permute-done.34.right_far_ref), custom_call_target="tpu_custom_call" | custom-call | flops 644245120 | bytes 1677721 | tf_op jit(solution)/shard_map/outer/pallas_call | solution.py:940
  453.7 20.6 %gate_up_back.1 = (bf16[256,2048]{1,0:T(8,128)(2,1)}, bf16[256,2048]{1,0:T(8,128)(2,1)}, bf16[512,1024]{1,0:T(8,128)(2,1)}, bf16[512,1024]{1,0:T(8,128)(2,1)}) custom-call(bf16[1024,1536]{1,0:T(8,128)(2,1)} %get-tuple-element.119.own_ref.left_ref, bf16[1024,1536]{1,0:T(8,128)(2,1)} %get-tuple-element.114.other_ref, ...), custom_call_target="tpu_custom_call" | custom-call | flops 1288490240 | bytes 2097152 | tf_op jit(solution)/shard_map/gate_up_back/pallas_call | solution.py:879
  476.4 23.4 %collective-permute-done.35 = bf16[256,2048]{1,0:T(8,128)(2,1)S(1)} collective-permute-done((bf16[256,2048]{1,0:T(8,128)(2,1)}, bf16[256,2048]{1,0:T(8,128)(2,1)S(1)}, u32[]{:S(2)}, u32[]{:S(2)}) %collective-permute-start.35) | collective-permute-done | bytes 1048608 | tf_op jit(solution)/shard_map/ppermute | solution.py:406
  507.2 21.3 %outer.3 = bf16[1408,2048]{1,0:T(8,128)(2,1)} custom-call(bf16[1024,1536]{1,0:T(8,128)(2,1)} %get-tuple-element.119.own_ref.left_ref, bf16[1024,1536]{1,0:T(8,128)(2,1)} %collective-permute-done.33.left_far_ref, bf16[1024,2048]{1,0:T(8,128)(2,1)} %get-tuple-element.121.right_ref, bf16[1024,2048]{1,0:T(8,128)(2,1)} %collective-permute-done.32.right_far_ref), custom_call_target="tpu_custom_call" | custom-call | flops 1288490240 | bytes 1677721 | tf_op jit(solution)/shard_map/outer/pallas_call | solution.py:940
  542.8 3.9 multiply_convert_fusion
  546.7 6.5 project.3
  557.4 18.4 %collective-permute-done.40 = bf16[512,1024]{1,0:T(8,128)(2,1)S(1)} collective-permute-done((bf16[512,1024]{1,0:T(8,128)(2,1)}, bf16[512,1024]{1,0:T(8,128)(2,1)S(1)}, u32[]{:S(2)}, u32[]{:S(2)}) %collective-permute-start.40) | collective-permute-done | bytes 1048608 | tf_op jit(solution)/shard_map/ppermute | solution.py:406
  579.7 14.7 %attend_back.1 = (bf16[512,1024]{1,0:T(8,128)(2,1)}, bf16[2048,512]{1,0:T(8,128)(2,1)}) custom-call(s32[8]{0:T(128)} %stack.50.flags, bf16[512,1024]{1,0:T(8,128)(2,1)} %copy-done.32, bf16[512,1024]{1,0:T(8,128)(2,1)} %add_convert_fusion.do_ref, f32[8,1,512]{2,1,0:T(1,128)} %get-tuple-element.130.lse_ref, f32[64,512]{1,0:T(8,128)} %get-tuple-element.335.cos_ref, ...), custom_call_target="tpu_custom_call" | custom-call | flops 805306368 | bytes 1258291 | tf_op jit(solution)/shard_map/attend_back/pallas_call | solution.py:600
  596.8 19.4 %collective-permute-done.43.other_ref = bf16[512,1024]{1,0:T(8,128)(2,1)S(1)} collective-permute-done((bf16[512,1024]{1,0:T(8,128)(2,1)}, bf16[512,1024]{1,0:T(8,128)(2,1)S(1)}, u32[]{:S(2)}, u32[]{:S(2)}) %collective-permute-start.43) | collective-permute-done | bytes 1048608 | tf_op jit(solution)/shard_map/ppermute | solution.py:406
  626.8 9.0 %reduce-scatter.9.cloned.1.call-done = bf16[352,2048]{1,0:T(8,128)(2,1)} async-done(((bf16[1408,2048]{1,0:T(8,128)(2,1)}), bf16[352,2048]{1,0:T(8,128)(2,1)}) %reduce-scatter.9.cloned.1.call-update) | async-done | bytes 1441808 | tf_op jit(solution)/shard_map/reduce_scatter | solution.py:1177
  645.7 16.8 %collective-permute-done.44 = bf16[352,1024]{1,0:T(8,128)(2,1)S(1)} collective-permute-done((bf16[352,1024]{1,0:T(8,128)(2,1)S(1)}, bf16[352,1024]{1,0:T(8,128)(2,1)S(1)}, u32[]{:S(2)}, u32[]{:S(2)}) %collective-permute-start.44) | collective-permute-done | bytes 720928 | tf_op jit(solution)/shard_map/ppermute | solution.py:406
  678.7 5.2 reduce-scatter.7.cloned.1.call-done
  683.8 15.8 %collective-permute-done.45.far_ref = bf16[704,1024]{1,0:T(8,128)(2,1)} collective-permute-done((bf16[704,1024]{1,0:T(8,128)(2,1)S(1)}, bf16[704,1024]{1,0:T(8,128)(2,1)}, u32[]{:S(2)}, u32[]{:S(2)}) %collective-permute-start.45) | collective-permute-done | bytes 1441824 | tf_op jit(solution)/shard_map/ppermute | solution.py:406
  704.8 16.2 %collective-permute-done.55 = bf16[512,1024]{1,0:T(8,128)(2,1)} collective-permute-done((bf16[512,1024]{1,0:T(8,128)(2,1)}, bf16[512,1024]{1,0:T(8,128)(2,1)}, u32[]{:S(2)}, u32[]{:S(2)}) %collective-permute-start.55) | collective-permute-done | bytes 1048608 | tf_op jit(solution)/shard_map/ppermute | solution.py:406
  742.3 6.5 merge.3
  752.8 5.6 key_value_back.1
  762.3 12.5 %collective-permute-start.61 = (bf16[64,1024]{1,0:T(8,128)(2,1)S(1)}, bf16[64,1024]{1,0:T(8,128)(2,1)S(1)}, u32[]{:S(2)}, u32[]{:S(2)}) collective-permute-start(bf16[64,1024]{1,0:T(8,128)(2,1)S(1)} %get-tuple-element.312), channel_id=1, source_target_pairs={{0,4},{2,6},{4,0},{6,2},{1,5},{3,7},{5,1},{7,3},{8,12},{10,14},{12... | collective-permute-start | bytes 393224 | tf_op jit(solution)/shard_map/ppermute | solution.py:406
  776.9 11.5 %collective-permute-done.61 = bf16[64,1024]{1,0:T(8,128)(2,1)S(1)} collective-permute-done((bf16[64,1024]{1,0:T(8,128)(2,1)S(1)}, bf16[64,1024]{1,0:T(8,128)(2,1)S(1)}, u32[]{:S(2)}, u32[]{:S(2)}) %collective-permute-start.61) | collective-permute-done | bytes 131104 | tf_op jit(solution)/shard_map/ppermute | solution.py:406
  796.6 10.5 %collective-permute-done.48 = f32[2176]{0:T(1024)S(1)} collective-permute-done((f32[2176]{0:T(1024)S(1)}, f32[2176]{0:T(1024)S(1)}, u32[]{:S(2)}, u32[]{:S(2)}) %collective-permute-start.48) | collective-permute-done | bytes 8736 | tf_op jit(solution)/shard_map/ppermute | solution.py:406
  810.9 5.1 settle.3
  828.6 8.0 settle.2
  (485 shorter events, 248.4 us)
Async XLA Ops:
  7.2 66.5 %all-gather.5.cloned.1.call-start = ((), (), s32[]{:S(2)}) async-start(), calls=%async_computation.4 | async-start | bytes 2621440 | tf_op jit(solution)/shard_map/all_gather | solution.py:67
  10.5 122.8 %all-gather.7.cloned.1.call-start = ((), (), s32[]{:S(2)}) async-start(), calls=%async_computation.5 | async-start | bytes 2621440 | tf_op jit(solution)/shard_map/all_gather | solution.py:67
  11.0 16.4 %collective-permute-start.1 = (bf16[128,1024]{1,0:T(8,128)(2,1)S(1)}, bf16[128,1024]{1,0:T(8,128)(2,1)S(1)}, u32[]{:S(2)}, u32[]{:S(2)}) collective-permute-start(bf16[128,1024]{1,0:T(8,128)(2,1)S(1)} %select_bitcast_fusion), channel_id=1, source_target_pairs={{0,2},{2,0},{4,6},{6,4},{1,3},{3,1},{5,7},{7,5},{8,10},{10,8},{12,... | collective-permute-start | bytes 786440 | tf_op jit(solution)/shard_map/ppermute | solution.py:406
  14.1 26.0 %collective-permute-start.2 = (bf16[128,1024]{1,0:T(8,128)(2,1)S(1)}, bf16[128,1024]{1,0:T(8,128)(2,1)S(1)}, u32[]{:S(2)}, u32[]{:S(2)}) collective-permute-start(bf16[128,1024]{1,0:T(8,128)(2,1)S(1)} %select_bitcast_fusion), channel_id=1, source_target_pairs={{0,4},{2,6},{4,0},{6,2},{1,5},{3,7},{5,1},{7,3},{8,12},{10,14},{12... | collective-permute-start | bytes 786440 | tf_op jit(solution)/shard_map/ppermute | solution.py:406
  16.7 26.4 %collective-permute-start.3 = (bf16[128,1024]{1,0:T(8,128)(2,1)S(1)}, bf16[128,1024]{1,0:T(8,128)(2,1)S(1)}, u32[]{:S(2)}, u32[]{:S(2)}) collective-permute-start(bf16[128,1024]{1,0:T(8,128)(2,1)S(1)} %select_bitcast_fusion), channel_id=1, source_target_pairs={{0,6},{2,4},{4,2},{6,0},{1,7},{3,5},{5,3},{7,1},{8,14},{10,12},{12... | collective-permute-start | bytes 786440 | tf_op jit(solution)/shard_map/ppermute | solution.py:406
  17.0 28.3 %collective-permute-start = (f32[512]{0:T(512)S(1)}, f32[512]{0:T(512)S(1)}, u32[]{:S(2)}, u32[]{:S(2)}) collective-permute-start(f32[512]{0:T(512)S(1)} %fusion.1), channel_id=1, source_target_pairs={{0,1},{1,0},{2,3},{3,2},{4,5},{5,4},{6,7},{7,6},{8,9},{9,8},{10,11... | collective-permute-start | bytes 6152 | tf_op jit(solution)/shard_map/ppermute | solution.py:406
  76.8 166.2 %all-gather.9.cloned.1.call-start = ((), (), s32[]{:S(2)}) async-start(), calls=%async_computation.6 | async-start | bytes 7208960 | tf_op jit(solution)/shard_map/all_gather | solution.py:67
  78.3 25.3 %collective-permute-start.9 = (bf16[512,1024]{1,0:T(8,128)(2,1)S(1)}, bf16[512,1024]{1,0:T(8,128)(2,1)}, u32[]{:S(2)}, u32[]{:S(2)}) collective-permute-start(bf16[512,1024]{1,0:T(8,128)(2,1)S(1)} %pad_maximum_fusion.9.refs_0_), channel_id=1, source_target_pairs={{0,16},{8,24},{16,0},{24,8},{1,17},{9,25},{17,1},{25,9},{2,18},{10... | collective-permute-start | bytes 3145736 | tf_op jit(solution)/shard_map/ppermute | solution.py:406
  89.7 25.7 %collective-permute-start.20 = (bf16[528,1024]{1,0:T(8,128)(2,1)}, bf16[528,1024]{1,0:T(8,128)(2,1)}, u32[]{:S(2)}, u32[]{:S(2)}) collective-permute-start(bf16[528,1024]{1,0:T(8,128)(2,1)} %pad_maximum_fusion.6), channel_id=1, source_target_pairs={{0,1},{1,0},{2,3},{3,2},{4,5},{5,4},{6,7},{7,6},{8,9},{9,8},{10,11... | collective-permute-start | bytes 3244040 | tf_op jit(solution)/shard_map/ppermute | solution.py:406
  91.2 24.2 %collective-permute-start.8 = (bf16[512,1024]{1,0:T(8,128)(2,1)S(1)}, bf16[512,1024]{1,0:T(8,128)(2,1)}, u32[]{:S(2)}, u32[]{:S(2)}) collective-permute-start(bf16[512,1024]{1,0:T(8,128)(2,1)S(1)} %pad_maximum_fusion.9.refs_0_), channel_id=1, source_target_pairs={{0,8},{8,0},{16,24},{24,16},{1,9},{9,1},{17,25},{25,17},{2,10},{10... | collective-permute-start | bytes 3145736 | tf_op jit(solution)/shard_map/ppermute | solution.py:406
  137.4 173.5 %all-gather.11.cloned.1.call-start = ((), (), s32[]{:S(2)}) async-start(), calls=%async_computation.7 | async-start | bytes 3604480 | tf_op jit(solution)/shard_map/all_gather | solution.py:67
  137.9 25.0 %collective-permute-start.12 = (bf16[512,1024]{1,0:T(8,128)(2,1)S(1)}, bf16[512,1024]{1,0:T(8,128)(2,1)S(1)}, u32[]{:S(2)}, u32[]{:S(2)}) collective-permute-start(bf16[512,1024]{1,0:T(8,128)(2,1)S(1)} %pad_maximum_fusion.10.refs_0_), channel_id=1, source_target_pairs={{0,16},{8,24},{16,0},{24,8},{1,17},{9,25},{17,1},{25,9},{2,18},{10... | collective-permute-start | bytes 3145736 | tf_op jit(solution)/shard_map/ppermute | solution.py:406
  139.4 24.9 %collective-permute-start.11 = (bf16[512,1024]{1,0:T(8,128)(2,1)}, bf16[512,1024]{1,0:T(8,128)(2,1)}, u32[]{:S(2)}, u32[]{:S(2)}) collective-permute-start(bf16[512,1024]{1,0:T(8,128)(2,1)} %get-tuple-element.82), channel_id=1, source_target_pairs={{0,1},{1,0},{2,3},{3,2},{4,5},{5,4},{6,7},{7,6},{8,9},{9,8},{10,11... | collective-permute-start | bytes 3145736 | tf_op jit(solution)/shard_map/ppermute | solution.py:406
  180.7 25.3 %collective-permute-start.14 = (bf16[512,1024]{1,0:T(8,128)(2,1)}, bf16[512,1024]{1,0:T(8,128)(2,1)S(1)}, u32[]{:S(2)}, u32[]{:S(2)}) collective-permute-start(bf16[512,1024]{1,0:T(8,128)(2,1)} %get-tuple-element.136.own_ref), channel_id=1, source_target_pairs={{0,1},{1,0},{2,3},{3,2},{4,5},{5,4},{6,7},{7,6},{8,9},{9,8},{10,11... | collective-permute-start | bytes 3145736 | tf_op jit(solution)/shard_map/ppermute | solution.py:406
  243.0 45.5 %collective-permute-start.21 = (bf16[1408,2048]{1,0:T(8,128)(2,1)}, bf16[1408,2048]{1,0:T(8,128)(2,1)}, u32[]{:S(2)}, u32[]{:S(2)}) collective-permute-start(bf16[1408,2048]{1,0:T(8,128)(2,1)} %all-gather.9.cloned.1.call-done.refs_5_.refs_0_), channel_id=1, source_target_pairs={{0,8},{8,0},{16,24},{24,16},{1,9},{9,1},{17,25},{25,17},{2,10},{10... | collective-permute-start | bytes 17301512 | tf_op jit(solution)/shard_map/ppermute | solution.py:406
  245.1 288.0 %reduce-scatter.5.cloned.1.call-start = ((), (), s32[]{:S(2)}) async-start(), calls=%async_computation.8 | async-start | bytes 3604480 | tf_op jit(solution)/shard_map/reduce_scatter | solution.py:1177
  261.3 24.9 %collective-permute-start.19 = (bf16[256,2048]{1,0:T(8,128)(2,1)S(1)}, bf16[256,2048]{1,0:T(8,128)(2,1)S(1)}, u32[]{:S(2)}, u32[]{:S(2)}) collective-permute-start(bf16[256,2048]{1,0:T(8,128)(2,1)S(1)} %pad_maximum_fusion.12), channel_id=1, source_target_pairs={{0,16},{8,24},{16,0},{24,8},{1,17},{9,25},{17,1},{25,9},{2,18},{10... | collective-permute-start | bytes 3145736 | tf_op jit(solution)/shard_map/ppermute | solution.py:406
  262.9 24.6 %collective-permute-start.18 = (bf16[512,1024]{1,0:T(8,128)(2,1)S(1)}, bf16[512,1024]{1,0:T(8,128)(2,1)S(1)}, u32[]{:S(2)}, u32[]{:S(2)}) collective-permute-start(bf16[512,1024]{1,0:T(8,128)(2,1)S(1)} %pad_maximum_fusion.11), channel_id=1, source_target_pairs={{0,1},{1,0},{2,3},{3,2},{4,5},{5,4},{6,7},{7,6},{8,9},{9,8},{10,11... | collective-permute-start | bytes 3145736 | tf_op jit(solution)/shard_map/ppermute | solution.py:406
  330.1 25.5 %collective-permute-start.23 = (bf16[256,2048]{1,0:T(8,128)(2,1)}, bf16[256,2048]{1,0:T(8,128)(2,1)S(1)}, u32[]{:S(2)}, u32[]{:S(2)}) collective-permute-start(bf16[256,2048]{1,0:T(8,128)(2,1)} %get-tuple-element.101), channel_id=1, source_target_pairs={{0,16},{8,24},{16,0},{24,8},{1,17},{9,25},{17,1},{25,9},{2,18},{10... | collective-permute-start | bytes 3145736 | tf_op jit(solution)/shard_map/ppermute | solution.py:406
  331.3 28.2 %collective-permute-start.25 = (bf16[512,1024]{1,0:T(8,128)(2,1)}, bf16[512,1024]{1,0:T(8,128)(2,1)S(1)}, u32[]{:S(2)}, u32[]{:S(2)}) collective-permute-start(bf16[512,1024]{1,0:T(8,128)(2,1)} %get-tuple-element.103), channel_id=1, source_target_pairs={{0,1},{1,0},{2,3},{3,2},{4,5},{5,4},{6,7},{7,6},{8,9},{9,8},{10,11... | collective-permute-start | bytes 3145736 | tf_op jit(solution)/shard_map/ppermute | solution.py:406
  332.7 62.2 %collective-permute-start.32 = (bf16[1024,2048]{1,0:T(8,128)(2,1)}, bf16[1024,2048]{1,0:T(8,128)(2,1)}, u32[]{:S(2)}, u32[]{:S(2)}) collective-permute-start(bf16[1024,2048]{1,0:T(8,128)(2,1)} %get-tuple-element.121.right_ref), channel_id=1, source_target_pairs={{0,8},{8,0},{16,24},{24,16},{1,9},{9,1},{17,25},{25,17},{2,10},{10... | collective-permute-start | bytes 12582920 | tf_op jit(solution)/shard_map/ppermute | solution.py:406
  392.0 22.7 %collective-permute-start.30 = (bf16[256,2048]{1,0:T(8,128)(2,1)S(1)}, bf16[256,2048]{1,0:T(8,128)(2,1)}, u32[]{:S(2)}, u32[]{:S(2)}) collective-permute-start(bf16[256,2048]{1,0:T(8,128)(2,1)S(1)} %pad_maximum_fusion.14), channel_id=1, source_target_pairs={{0,16},{8,24},{16,0},{24,8},{1,17},{9,25},{17,1},{25,9},{2,18},{10... | collective-permute-start | bytes 3145736 | tf_op jit(solution)/shard_map/ppermute | solution.py:406
  393.3 22.0 %collective-permute-start.29 = (bf16[512,1024]{1,0:T(8,128)(2,1)S(1)}, bf16[512,1024]{1,0:T(8,128)(2,1)S(1)}, u32[]{:S(2)}, u32[]{:S(2)}) collective-permute-start(bf16[512,1024]{1,0:T(8,128)(2,1)S(1)} %pad_maximum_fusion.13), channel_id=1, source_target_pairs={{0,1},{1,0},{2,3},{3,2},{4,5},{5,4},{6,7},{7,6},{8,9},{9,8},{10,11... | collective-permute-start | bytes 3145736 | tf_op jit(solution)/shard_map/ppermute | solution.py:406
  432.9 20.7 %collective-permute-start.33 = (bf16[1024,1536]{1,0:T(8,128)(2,1)}, bf16[1024,1536]{1,0:T(8,128)(2,1)}, u32[]{:S(2)}, u32[]{:S(2)}) collective-permute-start(bf16[1024,1536]{1,0:T(8,128)(2,1)} %get-tuple-element.114.other_ref), channel_id=1, source_target_pairs={{0,8},{8,0},{16,24},{24,16},{1,9},{9,1},{17,25},{25,17},{2,10},{10... | collective-permute-start | bytes 9437192 | tf_op jit(solution)/shard_map/ppermute | solution.py:406
  453.6 182.2 %reduce-scatter.9.cloned.1.call-start = ((), (), s32[]{:S(2)}) async-start(), calls=%async_computation.10 | async-start | bytes 7208960 | tf_op jit(solution)/shard_map/reduce_scatter | solution.py:1177
  474.3 25.5 %collective-permute-start.35 = (bf16[256,2048]{1,0:T(8,128)(2,1)}, bf16[256,2048]{1,0:T(8,128)(2,1)S(1)}, u32[]{:S(2)}, u32[]{:S(2)}) collective-permute-start(bf16[256,2048]{1,0:T(8,128)(2,1)} %get-tuple-element.116), channel_id=1, source_target_pairs={{0,16},{8,24},{16,0},{24,8},{1,17},{9,25},{17,1},{25,9},{2,18},{10... | collective-permute-start | bytes 3145736 | tf_op jit(solution)/shard_map/ppermute | solution.py:406
  475.3 27.8 %collective-permute-start.37 = (bf16[512,1024]{1,0:T(8,128)(2,1)}, bf16[512,1024]{1,0:T(8,128)(2,1)S(1)}, u32[]{:S(2)}, u32[]{:S(2)}) collective-permute-start(bf16[512,1024]{1,0:T(8,128)(2,1)} %get-tuple-element.118), channel_id=1, source_target_pairs={{0,1},{1,0},{2,3},{3,2},{4,5},{5,4},{6,7},{7,6},{8,9},{9,8},{10,11... | collective-permute-start | bytes 3145736 | tf_op jit(solution)/shard_map/ppermute | solution.py:406
  502.2 26.4 %collective-permute-start.36 = (bf16[256,1024]{1,0:T(8,128)(2,1)}, bf16[256,1024]{1,0:T(8,128)(2,1)S(1)}, u32[]{:S(2)}, u32[]{:S(2)}) collective-permute-start(bf16[256,1024]{1,0:T(8,128)(2,1)} %add_convert_fusion.2), channel_id=1, source_target_pairs={{0,1},{1,0},{2,3},{3,2},{4,5},{5,4},{6,7},{7,6},{8,9},{9,8},{10,11... | collective-permute-start | bytes 1572872 | tf_op jit(solution)/shard_map/ppermute | solution.py:406
  506.1 24.0 %collective-permute-start.38 = (bf16[256,1024]{1,0:T(8,128)(2,1)}, bf16[256,1024]{1,0:T(8,128)(2,1)}, u32[]{:S(2)}, u32[]{:S(2)}) collective-permute-start(bf16[256,1024]{1,0:T(8,128)(2,1)} %add_convert_fusion.1), channel_id=1, source_target_pairs={{0,16},{8,24},{16,0},{24,8},{1,17},{9,25},{17,1},{25,9},{2,18},{10... | collective-permute-start | bytes 1572872 | tf_op jit(solution)/shard_map/ppermute | solution.py:406
  533.2 150.7 %reduce-scatter.7.cloned.1.call-start = ((), (), s32[]{:S(2)}) async-start(), calls=%async_computation.9 | async-start | bytes 2621440 | tf_op jit(solution)/shard_map/reduce_scatter | solution.py:1177
  553.2 22.6 %collective-permute-start.40 = (bf16[512,1024]{1,0:T(8,128)(2,1)}, bf16[512,1024]{1,0:T(8,128)(2,1)S(1)}, u32[]{:S(2)}, u32[]{:S(2)}) collective-permute-start(bf16[512,1024]{1,0:T(8,128)(2,1)} %get-tuple-element.125), channel_id=1, source_target_pairs={{0,1},{1,0},{2,3},{3,2},{4,5},{5,4},{6,7},{7,6},{8,9},{9,8},{10,11... | collective-permute-start | bytes 3145736 | tf_op jit(solution)/shard_map/ppermute | solution.py:406
  555.2 20.7 %collective-permute-start.42 = (bf16[352,1024]{1,0:T(8,128)(2,1)S(1)}, bf16[352,1024]{1,0:T(8,128)(2,1)S(1)}, u32[]{:S(2)}, u32[]{:S(2)}) collective-permute-start(bf16[352,1024]{1,0:T(8,128)(2,1)S(1)} %pad_maximum_fusion.19.near_ref), channel_id=1, source_target_pairs={{0,16},{8,24},{16,0},{24,8},{1,17},{9,25},{17,1},{25,9},{2,18},{10... | collective-permute-start | bytes 2162696 | tf_op jit(solution)/shard_map/ppermute | solution.py:406
  594.4 21.9 %collective-permute-start.43 = (bf16[512,1024]{1,0:T(8,128)(2,1)}, bf16[512,1024]{1,0:T(8,128)(2,1)S(1)}, u32[]{:S(2)}, u32[]{:S(2)}) collective-permute-start(bf16[512,1024]{1,0:T(8,128)(2,1)} %get-tuple-element.131.own_ref), channel_id=1, source_target_pairs={{0,1},{1,0},{2,3},{3,2},{4,5},{5,4},{6,7},{7,6},{8,9},{9,8},{10,11... | collective-permute-start | bytes 3145736 | tf_op jit(solution)/shard_map/ppermute | solution.py:406
  619.9 169.8 %reduce-scatter.11.cloned.1.call-start = ((), (), s32[]{:S(2)}) async-start(), calls=%async_computation.11 | async-start | bytes 2621440 | tf_op jit(solution)/shard_map/reduce_scatter | solution.py:1177
  640.7 32.3 %collective-permute-start.54 = (bf16[1024,1024]{1,0:T(8,128)(2,1)}, bf16[1024,1024]{1,0:T(8,128)(2,1)}, u32[]{:S(2)}, u32[]{:S(2)}) collective-permute-start(bf16[1024,1024]{1,0:T(8,128)(2,1)} %convolution_convert_fusion), channel_id=1, source_target_pairs={{0,8},{8,0},{16,24},{24,16},{1,9},{9,1},{17,25},{25,17},{2,10},{10... | collective-permute-start | bytes 6291464 | tf_op jit(solution)/shard_map/ppermute | solution.py:406
  641.8 26.3 %collective-permute-start.53 = (bf16[512,1024]{1,0:T(8,128)(2,1)}, bf16[512,1024]{1,0:T(8,128)(2,1)}, u32[]{:S(2)}, u32[]{:S(2)}) collective-permute-start(bf16[512,1024]{1,0:T(8,128)(2,1)} %pad_maximum_fusion.15), channel_id=1, source_target_pairs={{0,16},{8,24},{16,0},{24,8},{1,17},{9,25},{17,1},{25,9},{2,18},{10... | collective-permute-start | bytes 3145736 | tf_op jit(solution)/shard_map/ppermute | solution.py:406
  644.2 18.3 %collective-permute-start.44 = (bf16[352,1024]{1,0:T(8,128)(2,1)S(1)}, bf16[352,1024]{1,0:T(8,128)(2,1)S(1)}, u32[]{:S(2)}, u32[]{:S(2)}) collective-permute-start(bf16[352,1024]{1,0:T(8,128)(2,1)S(1)} %get-tuple-element.280), channel_id=1, source_target_pairs={{0,1},{1,0},{2,3},{3,2},{4,5},{5,4},{6,7},{7,6},{8,9},{9,8},{10,11... | collective-permute-start | bytes 2162696 | tf_op jit(solution)/shard_map/ppermute | solution.py:406
  664.9 34.7 %collective-permute-start.45 = (bf16[704,1024]{1,0:T(8,128)(2,1)S(1)}, bf16[704,1024]{1,0:T(8,128)(2,1)}, u32[]{:S(2)}, u32[]{:S(2)}) collective-permute-start(bf16[704,1024]{1,0:T(8,128)(2,1)S(1)} %pad_maximum_fusion.3.near_ref), channel_id=1, source_target_pairs={{0,16},{8,24},{16,0},{24,8},{1,17},{9,25},{17,1},{25,9},{2,18},{10... | collective-permute-start | bytes 4325384 | tf_op jit(solution)/shard_map/ppermute | solution.py:406
  676.4 44.6 %collective-permute-start.55 = (bf16[512,1024]{1,0:T(8,128)(2,1)}, bf16[512,1024]{1,0:T(8,128)(2,1)}, u32[]{:S(2)}, u32[]{:S(2)}) collective-permute-start(bf16[512,1024]{1,0:T(8,128)(2,1)} %pad_maximum_fusion.16), channel_id=1, source_target_pairs={{0,16},{8,24},{16,0},{24,8},{1,17},{9,25},{17,1},{25,9},{2,18},{10... | collective-permute-start | bytes 3145736 | tf_op jit(solution)/shard_map/ppermute | solution.py:406
  703.3 27.1 %collective-permute-start.46 = (bf16[512,512]{1,0:T(8,128)(2,1)}, bf16[512,512]{1,0:T(8,128)(2,1)}, u32[]{:S(2)}, u32[]{:S(2)}) collective-permute-start(bf16[512,512]{1,0:T(8,128)(2,1)} %pad_maximum_fusion.22.own_ref), channel_id=1, source_target_pairs={{0,1},{1,0},{2,3},{3,2},{4,5},{5,4},{6,7},{7,6},{8,9},{9,8},{10,11... | collective-permute-start | bytes 1572872 | tf_op jit(solution)/shard_map/ppermute | solution.py:406
  737.8 20.6 %collective-permute-start.59 = (bf16[4,64,1024]{2,1,0:T(8,128)(2,1)}, bf16[4,64,1024]{2,1,0:T(8,128)(2,1)}, u32[]{:S(2)}, u32[]{:S(2)}) collective-permute-start(bf16[4,64,1024]{2,1,0:T(8,128)(2,1)} %fusion.44), channel_id=1, source_target_pairs={{0,16},{8,24},{16,0},{24,8},{1,17},{9,25},{17,1},{25,9},{2,18},{10... | collective-permute-start | bytes 1572872 | tf_op jit(solution)/shard_map/ppermute | solution.py:406
  742.3 66.5 %collective-permute-start.66 = (bf16[704,1024]{1,0:T(8,128)(2,1)}, bf16[704,1024]{1,0:T(8,128)(2,1)}, u32[]{:S(2)}, u32[]{:S(2)}) collective-permute-start(bf16[704,1024]{1,0:T(8,128)(2,1)} %pad_maximum_fusion.4), channel_id=1, source_target_pairs={{0,8},{8,0},{16,24},{24,16},{1,9},{9,1},{17,25},{25,17},{2,10},{10... | collective-permute-start | bytes 4325384 | tf_op jit(solution)/shard_map/ppermute | solution.py:406
  752.2 76.3 %collective-permute-start.65 = (bf16[1408,1024]{1,0:T(8,128)(2,1)}, bf16[1408,1024]{1,0:T(8,128)(2,1)}, u32[]{:S(2)}, u32[]{:S(2)}) collective-permute-start(bf16[1408,1024]{1,0:T(8,128)(2,1)} %pad_maximum_fusion), channel_id=1, source_target_pairs={{0,8},{8,0},{16,24},{24,16},{1,9},{9,1},{17,25},{25,17},{2,10},{10... | collective-permute-start | bytes 8650760 | tf_op jit(solution)/shard_map/ppermute | solution.py:406
  762.3 26.1 %collective-permute-start.61 = (bf16[64,1024]{1,0:T(8,128)(2,1)S(1)}, bf16[64,1024]{1,0:T(8,128)(2,1)S(1)}, u32[]{:S(2)}, u32[]{:S(2)}) collective-permute-start(bf16[64,1024]{1,0:T(8,128)(2,1)S(1)} %get-tuple-element.312), channel_id=1, source_target_pairs={{0,4},{2,6},{4,0},{6,2},{1,5},{3,7},{5,1},{7,3},{8,12},{10,14},{12... | collective-permute-start | bytes 393224 | tf_op jit(solution)/shard_map/ppermute | solution.py:406
  774.8 17.7 %collective-permute-start.62 = (bf16[64,1024]{1,0:T(8,128)(2,1)S(1)}, bf16[64,1024]{1,0:T(8,128)(2,1)}, u32[]{:S(2)}, u32[]{:S(2)}) collective-permute-start(bf16[64,1024]{1,0:T(8,128)(2,1)S(1)} %get-tuple-element.313), channel_id=1, source_target_pairs={{0,6},{2,4},{4,2},{6,0},{1,7},{3,5},{5,3},{7,1},{8,14},{10,12},{12... | collective-permute-start | bytes 393224 | tf_op jit(solution)/shard_map/ppermute | solution.py:406
  776.9 17.3 %collective-permute-start.47 = (f32[2176]{0:T(1024)}, f32[2176]{0:T(1024)}, u32[]{:S(2)}, u32[]{:S(2)}) collective-permute-start(f32[2176]{0:T(1024)} %pad_maximum_fusion.26), channel_id=1, source_target_pairs={{0,8},{8,0},{16,24},{24,16},{1,9},{9,1},{17,25},{25,17},{2,10},{10... | collective-permute-start | bytes 26120 | tf_op jit(solution)/shard_map/ppermute | solution.py:406
  789.8 29.1 %collective-permute-start.56 = (bf16[256,1024]{1,0:T(8,128)(2,1)}, bf16[256,1024]{1,0:T(8,128)(2,1)}, u32[]{:S(2)}, u32[]{:S(2)}) collective-permute-start(bf16[256,1024]{1,0:T(8,128)(2,1)} %reduce-scatter.11.cloned.1.call-done), channel_id=1, source_target_pairs={{0,16},{8,24},{16,0},{24,8},{1,17},{9,25},{17,1},{25,9},{2,18},{10... | collective-permute-start | bytes 1572872 | tf_op jit(solution)/shard_map/ppermute | solution.py:406
  793.8 24.3 %collective-permute-start.63 = (bf16[64,1024]{1,0:T(8,128)(2,1)S(1)}, bf16[64,1024]{1,0:T(8,128)(2,1)S(1)}, u32[]{:S(2)}, u32[]{:S(2)}) collective-permute-start(bf16[64,1024]{1,0:T(8,128)(2,1)S(1)} %fusion.75), channel_id=1, source_target_pairs={{0,16},{8,24},{16,0},{24,8},{1,17},{9,25},{17,1},{25,9},{2,18},{10... | collective-permute-start | bytes 393224 | tf_op jit(solution)/shard_map/ppermute | solution.py:406
  (127 other events, 1128.2 us)
Sparse Core Ops, SparseCore 0:
  10.7 63.0 all-gather.4
  76.9 56.4 all-gather.6
  137.5 105.4 all-gather.8
  245.2 60.6 all-gather.10
  453.8 56.4 reduce-scatter.4
  533.3 102.4 reduce-scatter.8
  638.7 45.1 reduce-scatter.6
  728.7 60.9 reduce-scatter.10

commit v3 on v2

--- a/solution.py
+++ b/solution.py
@@ -996,20 +996,22 @@
     return [x, a_x, b_y, a_y, b_x]
 
 
-def plane_scatter(parts):
+def plane_scatter(parts, *others):
     a_keep, a_send, b_keep, b_send = parts
     half, width = a_keep.shape[0], b_keep.shape[1]
     a_x = swap(a_send, "dp", 2)
     b_y = swap(b_send, "col", 1)
+    a_x, b_y, *others = lax.optimization_barrier((a_x, b_y, *others))
     a_y = swap(low(wide(a_keep[:, width:]) + wide(a_x[:, width:])), "col", 1)
     b_x = swap(low(wide(b_keep[half:]) + wide(b_y[half:])), "dp", 2)
-    return jnp.concatenate(
+    total = jnp.concatenate(
         [
             wide(a_keep[:, :width]) + wide(a_x[:, :width]) + wide(a_y),
             wide(b_keep[:half]) + wide(b_y[:half]) + wide(b_x),
         ],
         axis=0,
     )
+    return (total, *others)
 
 
 def dp_slots(x):
@@ -1018,28 +1020,37 @@
     return [x, other[: x.shape[0]], far, other[x.shape[0] :]]
 
 
-def heads_near(own, other, right, y):
-    half = own.shape[1] // 2
-    odd = low(dot_tn(jnp.concatenate([own[:, half:], other[:, half:]], axis=1), right))
-    odd = swap(odd, "dp", 1)
-    even = dot_tn(jnp.concatenate([own[:, :half], other[:, :half]], axis=1), right)
+def with_core(x):
+    return jnp.concatenate([x, swap(x, "dp", 1)], axis=0)
+
+
+def heads_sum(left, right):
+    half = left.shape[1] // 2
+    both = jnp.concatenate([left[:, :half], swap(left[:, half:], "dp", 1)], axis=0)
+    even = low(dot_tn(both, right))
     part = half // 2
-    total = [even[i * part : (i + 1) * part] + wide(odd[i * part : (i + 1) * part]) for i in range(4)]
-    far = swap(low(jnp.concatenate([total[1], total[3]], axis=0)), "dp", 2)
-    return xor_order([low(total[0] + wide(far[:part])), low(total[2] + wide(far[part:]))], y)
-
-
-def quarters_home(slots, order):
-    odd = swap(low(jnp.concatenate([slots[1], slots[3]], axis=0)), "dp", 1)
-    count = slots[0].shape[0]
-    near = wide(slots[0]) + wide(odd[:count])
-    far = swap(low(wide(slots[2]) + wide(odd[count:])), "dp", 2)
-    total = near + wide(far)
-    parts = xor_order([low(total[i]) for i in range(count)], order)
-    summed = wide(parts[0])
-    for k in range(1, count):
-        summed += wide(swap(parts[k], "row", k))
-    return xor_order(dp_slots(low(summed)), lax.axis_index("dp"))
+    return even, swap(even[part:], "dp", 2)
+
+
+def heads_home(own, other, y, later):
+    near = jnp.concatenate(xor_order([low(own), low(other)], y), axis=0)
+    near = lax.psum_scatter(after(near, later), "row", scatter_dimension=0, tiled=True)
+    return jnp.concatenate(xor_order(dp_slots(near), lax.axis_index("dp")), axis=0)
+
+
+def quarters_home(pieces, r):
+    n_row, n_col = lax.axis_size("row"), lax.axis_size("col")
+    groups = n_row // n_col
+    slots = xor_order(pieces, r)
+    received = []
+    for k in range(n_row):
+        pairs = []
+        for row in range(n_row):
+            for col in range(n_col):
+                head, half = divmod(row ^ k, n_col)
+                pairs.append((row * n_col + col, (col * groups + head) * n_col + half))
+        received.append(wide(lax.ppermute(slots[k], ("row", "col"), pairs)))
+    return low(sum(received[1:], received[0]))
 
 
 def fast_body(
@@ -1082,8 +1093,9 @@
     def hidden_rows(at):
         return jnp.concatenate([rows_of(w, at * inner_part, inner_part) for w in (w_gate.T, w_up.T, w_down)], axis=0)
 
-    hidden_other = after(swap(hidden_rows(d * n_col + (1 - y)), "col", 1), kv_theirs)
+    hidden_other = swap(hidden_rows(d * n_col + (1 - y)), "col", 1)
     hidden_own = hidden_rows(d * n_col + y)
+    kv_theirs, hidden_other = lax.optimization_barrier((kv_theirs, hidden_other))
 
     positions, segment, counted = token_layout(cont_ids, answer_len)
     row_start = r * rows
@@ -1139,11 +1151,12 @@
     q_far = swap(q_part, "dp", 2)
     q_slots = [q_part, swap(q_part, "dp", 1), q_far, swap(q_far, "dp", 1)]
     q_own, q_send = project(side, a1, q_slots)
-    hidden_own, hidden_other = lax.optimization_barrier((hidden_own, hidden_other, key_values, q_send))[:2]
+    hidden_own, hidden_other = lax.optimization_barrier((hidden_own, hidden_other, q_send))[:2]
     hidden_mine = jnp.concatenate([hidden_own, hidden_other], axis=1)
     gate_up_mine = gather_rows(hidden_mine[: 2 * inner_part])
     down_mine = gather_rows(hidden_mine[2 * inner_part :])
-    queries = low(turn_heads(q_own + wide(swap(q_send, "col", 1)), 1.0, HEAD_SIZE))
+    q_received, key_values = lax.optimization_barrier((swap(q_send, "col", 1), key_values))
+    queries = low(turn_heads(q_own + wide(q_received), 1.0, HEAD_SIZE))
     o_slots = dp_slots(after(o_part, q_send))
     queries, *o_slots = lax.optimization_barrier((queries, *o_slots))
     context, lse = attend(flags, queries, query_seg, key_seg, key_values)
@@ -1157,9 +1170,9 @@
     gate_up_mine = after(gate_up_mine, a2_pieces[1])
     gate_up_sides = [gate_up_mine, swap(gate_up_mine, "dp", 1)]
     gate, up, *hids, a2_all = gate_up(a2_pieces, gate_up_sides)
-    down_mine = after(down_mine, gate)
+    down_mine, gate, a1_other = lax.optimization_barrier((down_mine, gate, swap(a1, "col", 1)))
     down_sides = [down_mine, swap(down_mine, "dp", 1)]
-    result = hidden_res + keep_here * plane_scatter(down(hids, down_sides))
+    result = hidden_res + keep_here * plane_scatter(down(hids, down_sides))[0]
     error = result - wide(teacher)
     error_part = jnp.sum(counted_here * error * error)
     grad_result = wide(out_grad) + 2.0 / (count * features) * counted_here * error
@@ -1169,7 +1182,14 @@
         return [own, swap(other, "dp", 1)]
 
     hids, a2_sides = both_cores(*hids), both_cores(a2_all, a2_all)
-    gate, *hids_sides = lax.optimization_barrier((gate, *hids, *a2_sides))
+    a1_both = with_core(jnp.concatenate([a1, a1_other], axis=1))
+    context_half = context.shape[1] // 2
+    context_even, context_odd = [
+        jnp.concatenate([context[:, i : i + context_half], context_other[:, i : i + context_half]], axis=1)
+        for i in (0, context_half)
+    ]
+    context_cores = jnp.concatenate([context_even, swap(context_odd, "dp", 1)], axis=0)
+    gate, a1_both, context_cores, *hids_sides = lax.optimization_barrier((gate, a1_both, context_cores, *hids, *a2_sides))
     hids, a2_sides = hids_sides[:2], hids_sides[2:]
     *dboth, gm_all = down_back(gm_pieces, gate, up, down_sides)
 
@@ -1181,9 +1201,9 @@
     *dboth, down_joined = lax.optimization_barrier((*dboth, *dboth_sides, down_joined))
     dboth, dboth_sides = dboth[:2], dboth[2:]
     down_part = along_row(down_joined)
-    grad_normed_ffn = plane_scatter(gate_up_back(dboth, gate_up_sides))
+    parts = gate_up_back(dboth, gate_up_sides)
     gate_up_joined = outer(dboth_sides, a2_sides, 2, inner_part)
-    grad_normed_ffn, gate_up_joined = lax.optimization_barrier((grad_normed_ffn, gate_up_joined))
+    grad_normed_ffn, gate_up_joined = plane_scatter(parts, gate_up_joined)
     gate_up_joined, down_part = lax.optimization_barrier((gate_up_joined, down_part))
     gate_up_part = along_row(gate_up_joined)
 
@@ -1191,9 +1211,11 @@
         near = jnp.concatenate([part[:, :width], swap(part[:, width:], "col", 1)], axis=0)
         return near, swap(near, "dp", 2)
 
-    def hidden_home(near, far, kinds, turned):
-        other = swap(jnp.concatenate([near, far], axis=0), "dp", 1)
-        return settle(d, y, near, far, other, kinds, turned)
+    def hidden_home(near, far, kinds, turned, *others):
+        both = jnp.concatenate([near, far], axis=0)
+        if others:
+            both = after(both, *others)
+        return settle(d, y, near, far, swap(both, "dp", 1), kinds, turned)
 
     gain_ffn_sum = jnp.sum(grad_normed_ffn * hidden_res * scale_ffn, axis=0)
     weighted = grad_normed_ffn * gain_ffn[None, :]
@@ -1206,32 +1228,51 @@
 
     ga = low(keep_here * grad_hidden_res)
     do_own, do_send = project(side, ga, o_slots)
-    do_received, *down_near = lax.optimization_barrier((swap(do_send, "col", 1), *hidden_near(down_part)))
+    context_cores, ga_cores = lax.optimization_barrier((context_cores, with_core(ga), do_send))[:2]
+    o_even = low(dot_tn(context_cores, ga_cores))
+    o_part = o_even.shape[0] // 4
+    o_far = swap(jnp.concatenate([o_even[o_part : 2 * o_part], o_even[3 * o_part :]], axis=0), "dp", 2)
+    do_received, o_far = lax.optimization_barrier((swap(do_send, "col", 1), o_far))
     grad_context = low(do_own + wide(do_received))
     dq, dkv_parts = attend_back(flags, queries, grad_context, lse, cos_t, sin_t, query_seg, key_seg, key_values)
-    context, context_other, ga, gate_up_part = lax.optimization_barrier((context, context_other, ga, gate_up_part, dq))[:4]
-    gate_up_near = hidden_near(gate_up_part)
-    dkv_sum, *gate_up_near = lax.optimization_barrier((along_row(dkv_parts), *gate_up_near))
-    (grad_down,) = hidden_home(*down_near, 1, False)
-    grad_gate, grad_up = hidden_home(*gate_up_near, 2, True)
+    q_even, q_far = heads_sum(dq, a1_both)
+    dkv_parts, gate_up_part = lax.optimization_barrier((dkv_parts, gate_up_part))
+    dkv_sum = along_row(dkv_parts)
+    gate_up_received, dkv_sum = lax.optimization_barrier((swap(gate_up_part[:, width:], "col", 1), dkv_sum))
+    down_near = hidden_near(after(down_part, q_even))
+    gate_up_near = jnp.concatenate([gate_up_part[:, :width], gate_up_received], axis=0)
     dkv = low(turn_heads(wide(dkv_sum), -1.0, 2 * HEAD_SIZE))
+    gate_up_far = swap(gate_up_near, "dp", 2)
+    dkv_cores = with_core(dkv)
+    q_far = after(q_far, dkv_cores)
+    q_sum = wide(q_even[: q_far.shape[0]]) + wide(q_far)
     dq_other = swap(dq, "col", 1)
-    dkv_other = swap(dkv, "col", 1)
+    kv_part = 2 * HEAD_SIZE // n_dp
+    dwkv = low(dot_tn(dkv_cores, a1_both)).reshape(groups, n_dp, kv_part, features)
+    dwkv = [dwkv[:, i].reshape(groups * kv_part, features) for i in range(n_dp)]
+    kv_near, kv_far = xor_order(dwkv, d)[0], xor_order(dwkv, d ^ 2)[0]
+    q_sum = after(q_sum, kv_far)
+    kv_far, dkv_other = lax.optimization_barrier((swap(kv_far, "dp", 2), swap(dkv, "col", 1)))
+    dwkv = low(wide(kv_near) + wide(kv_far))
     grad_normed_attn = merge(side, dq, dq_other, q_slots) + key_value_back(
         kv_scalars, dkv, dkv_other, kv_mine, kv_theirs
     )
 
-    near = [heads_near(dq, dq_other, a1, y), heads_near(context, context_other, ga, y)]
-    near = [x[g * HEAD_SIZE : (g + 1) * HEAD_SIZE] for p in range(2) for g in range(groups) for x in (near[0][p], near[1][p])]
-    near = along_row(after(jnp.concatenate(near, axis=0), dkv_sum))
-    near = xor_order(dp_slots(near), d)
-    grad_query = wide(jnp.concatenate([x[:HEAD_SIZE] for x in near], axis=0).T)
-    grad_out = wide(jnp.concatenate([x[HEAD_SIZE:] for x in near], axis=0))
-    kv_part = 2 * HEAD_SIZE // n_dp
-    dwkv = jnp.concatenate(
-        [x.reshape(groups, n_dp, kv_part, width) for x in (dot_tn(dkv, a1), dot_tn(dkv_other, a1))], axis=0
-    )
-    dwkv = jnp.concatenate(quarters_home(xor_order([dwkv[:, i] for i in range(n_dp)], d), order), axis=0)
+    q_other = swap(low(q_sum[:, width:]), "col", 1)
+    grad_query = wide(heads_home(q_sum[:, :width], q_other, y, dkv_sum).T)
+    o_own, o_other = [
+        wide(o_even[2 * i * o_part : (2 * i + 1) * o_part]) + wide(o_far[i * o_part : (i + 1) * o_part]) for i in (0, 1)
+    ]
+    grad_out = wide(heads_home(o_own, o_other, y, dkv_sum))
+    pieces = []
+    for g in range(groups):
+        block = dwkv[g * kv_part : (g + 1) * kv_part]
+        pieces += xor_order([block[:, :width], block[:, width:]], y)
+    dwkv = quarters_home(pieces, r)
+    (grad_down,) = hidden_home(*down_near, 1, False, dwkv)
+    grad_gate, grad_up = hidden_home(gate_up_near, gate_up_far, 2, True, dwkv)
+    later = dwkv
+    dwkv = jnp.concatenate(xor_order(dp_slots(dwkv), d), axis=0)
     grad_key = wide(dwkv[:HEAD_SIZE].T)
     grad_value = wide(dwkv[HEAD_SIZE:].T)
 
@@ -1241,7 +1282,7 @@
     inner_sum = (inner_sum + swap(inner_sum, "col", 1))[:, None]
     grad_states = grad_hidden_res + scale_attn * weighted - states_f * scale_attn**3 * inner_sum / features
 
-    sums = jnp.concatenate([gain_attn_sum, gain_ffn_sum, error_col])
+    sums = after(jnp.concatenate([gain_attn_sum, gain_ffn_sum, error_col]), later)
     for axis, mask in (("dp", 1), ("dp", 2), ("row", 1), ("row", 2)):
         sums = sums + swap(sums, axis, mask)
     return (

time: 864 us -> 807 us (0.934)
  waiting for transfers between devices: 398 us -> 369 us
  other arithmetic: 92.2 us -> 74.8 us
    ppermute x67 -> x70, waiting for transfers between devices: 357 us -> 290 us  [swap(): return lax.ppermute(values, axis, [(i, i ^ mask) for i in range(size)])]
    reduce_scatter x4 -> x3, waiting for transfers between devices: 15.5 us -> 53.8 us  [along_row(): return lax.psum_scatter(x, 'row', scatter_dimension=0, tiled=True)]
    ppermute x67 -> x70, starting transfers between devices: 80.8 us -> 68.5 us  [swap(): return lax.ppermute(values, axis, [(i, i ^ mask) for i in range(size)])]
    unnamed x218 -> x191, local copies, waits for them, and re-layouts: 30.1 us -> 22.6 us
  transfers between devices with their start and end apart: 75 -> 83, of which waited for: 41 -> 48; matrix products, arithmetic and copies ran while one was open for 15% -> 15% of each run, Pallas kernels for 18% -> 18%
where the time goes in v3:
time: 807 us; the launch traced here: 797 us
  waiting for transfers between devices  369 us (46%)
  Pallas kernels  183 us (23%)
  starting transfers between devices  76.2 us (9%)
  other arithmetic  74.8 us (9%)
  local copies, waits for them, and re-layouts  53.9 us (7%)
  between operations  27.4 us (3%)
  matrix products  11.9 us (1%)
    ppermute x70, waiting for transfers between devices, swap(): return lax.ppermute(values, axis, [(i, i ^ mask) for i in range(size)])  290 us
    pallas_call x4, Pallas kernels, feed_call(): pl.pallas_call(kernel, out_shape=tuple(shapes), grid=(blocks,), in_specs=...  74.2 us
    ppermute x70, starting transfers between devices, swap(): return lax.ppermute(values, axis, [(i, i ^ mask) for i in range(size)])  68.5 us
    reduce_scatter x3, waiting for transfers between devices, along_row(): return lax.psum_scatter(x, 'row', scatter_dimension=0, tiled=True)  53.8 us
    pallas_call x6, Pallas kernels, local_call(): pl.pallas_call(kernel, out_shape=outs, in_specs=[pl.BlockSpec(memory_spac...  37.2 us
    pallas_call x2, Pallas kernels, outer(): pl.pallas_call(functools.partial(outer_kernel, kinds, N_ROW * part), out_...  34.1 us
    all_gather x4, waiting for transfers between devices, gather_rows(): return lax.all_gather(values, 'row', axis=0, tiled=True)  25.8 us
    unnamed x191, local copies, waits for them, and re-layouts  22.6 us
  transfers between devices with their start and end apart: 83, of which 48 were waited for; matrix products, arithmetic and copies ran while one was open for 15% of the time, Pallas kernels for 18%

profile of v3, /device:TPU:0, one launch (start us, length us, event | category | flops | bytes accessed | tf_op | source)
XLA Modules:
  0.0 797.0 jit_solution(14720771976565912227)
XLA Ops:
  16.5 4.0 constant_dynamic-slice_fusion.2
  27.2 12.7 %collective-permute-done.2 = bf16[128,1024]{1,0:T(8,128)(2,1)S(1)} collective-permute-done((bf16[128,1024]{1,0:T(8,128)(2,1)S(1)}, bf16[128,1024]{1,0:T(8,128)(2,1)S(1)}, u32[]{:S(2)}, u32[]{:S(2)}) %collective-permute-start.2) | collective-permute-done | bytes 262176 | tf_op jit(solution)/shard_map/ppermute | solution.py:406
  45.0 4.3 collective-permute-done
  52.2 5.5 key_value.1
  65.8 4.2 collective-permute-done.6
  79.7 23.6 %collective-permute-done.10.refs_2_ = bf16[512,1024]{1,0:T(8,128)(2,1)S(1)} collective-permute-done((bf16[512,1024]{1,0:T(8,128)(2,1)S(1)}, bf16[512,1024]{1,0:T(8,128)(2,1)S(1)}, u32[]{:S(2)}, u32[]{:S(2)}) %collective-permute-start.10) | collective-permute-done | bytes 1048608 | tf_op jit(solution)/shard_map/ppermute | solution.py:406
  107.0 6.5 project.2
  132.3 11.1 %collective-permute-done.13.refs_2_ = bf16[512,1024]{1,0:T(8,128)(2,1)S(1)} collective-permute-done((bf16[512,1024]{1,0:T(8,128)(2,1)S(1)}, bf16[512,1024]{1,0:T(8,128)(2,1)S(1)}, u32[]{:S(2)}, u32[]{:S(2)}) %collective-permute-start.13) | collective-permute-done | bytes 1048608 | tf_op jit(solution)/shard_map/ppermute | solution.py:406
  153.7 10.2 %attend.1 = (bf16[512,1024]{1,0:T(8,128)(2,1)}, f32[8,1,512]{2,1,0:T(1,128)}) custom-call(s32[8]{0:T(128)} %stack.50.flags, bf16[512,1024]{1,0:T(8,128)(2,1)} %copy-done.24, s32[1,512]{1,0:T(1,128)} %get-tuple-element.341.qseg_ref, s32[2048,1]{1,0:T(8,128)} %copy.58.kseg_ref, bf16[2048,512]{1,0:T(8,128)(2,1)} %all-gather.7.cloned.1.call-done.refs_0_.refs_1_.refs_2_.refs_3_, ...), custom_call_target="tpu_custom_call" | custom-call | flops 322122560 | bytes 838860 | tf_op jit(solution)/shard_map/attend/pallas_call | solution.py:574
  165.5 24.1 %collective-permute-done.15.other_ref = bf16[512,1024]{1,0:T(8,128)(2,1)S(1)} collective-permute-done((bf16[512,1024]{1,0:T(8,128)(2,1)}, bf16[512,1024]{1,0:T(8,128)(2,1)S(1)}, u32[]{:S(2)}, u32[]{:S(2)}) %collective-permute-start.15) | collective-permute-done | bytes 1048608 | tf_op jit(solution)/shard_map/ppermute | solution.py:406
  190.6 6.5 merge.2
  207.3 11.3 %collective-permute-done.17.refs_1_ = bf16[256,1024]{1,0:T(8,128)(2,1)S(1)} collective-permute-done((bf16[256,1024]{1,0:T(8,128)(2,1)S(1)}, bf16[256,1024]{1,0:T(8,128)(2,1)S(1)}, u32[]{:S(2)}, u32[]{:S(2)}) %collective-permute-start.17) | collective-permute-done | bytes 524320 | tf_op jit(solution)/shard_map/ppermute | solution.py:406
  218.6 22.2 %all-gather.9.cloned.1.call-done.refs_5_.refs_0_ = bf16[1408,2048]{1,0:T(8,128)(2,1)} async-done(((bf16[352,2048]{1,0:T(8,128)(2,1)}), bf16[1408,2048]{1,0:T(8,128)(2,1)}) %all-gather.9.cloned.1.call-update) | async-done | bytes 5767184 | tf_op jit(solution)/shard_map/all_gather | solution.py:67
  244.5 13.0 %collective-permute-done.18.refs_2_ = bf16[256,1024]{1,0:T(8,128)(2,1)S(1)} collective-permute-done((bf16[256,1024]{1,0:T(8,128)(2,1)}, bf16[256,1024]{1,0:T(8,128)(2,1)S(1)}, u32[]{:S(2)}, u32[]{:S(2)}) %collective-permute-start.18) | collective-permute-done | bytes 524320 | tf_op jit(solution)/shard_map/ppermute | solution.py:406
  262.6 21.2 %collective-permute-done.20.refs_4_ = bf16[256,2048]{1,0:T(8,128)(2,1)S(1)} collective-permute-done((bf16[256,2048]{1,0:T(8,128)(2,1)S(1)}, bf16[256,2048]{1,0:T(8,128)(2,1)S(1)}, u32[]{:S(2)}, u32[]{:S(2)}) %collective-permute-start.20) | collective-permute-done | bytes 1048608 | tf_op jit(solution)/shard_map/ppermute | solution.py:406
  287.6 22.5 %gate_up.1 = (f32[1024,1536]{1,0:T(8,128)}, f32[1024,1536]{1,0:T(8,128)}, bf16[1024,768]{1,0:T(8,128)(2,1)}, bf16[1024,768]{1,0:T(8,128)(2,1)}, bf16[1024,2048]{1,0:T(8,128)(2,1)}) custom-call(bf16[512,1024]{1,0:T(8,128)(2,1)} %copy-done.19, bf16[256,1024]{1,0:T(8,128)(2,1)} %copy-done.50, bf16[256,1024]{1,0:T(8,128)(2,1)} %copy-done.51, ...), custom_call_target="tpu_custom_call" | custom-call | flops 1288490240 | bytes 2097152 | tf_op jit(solution)/shard_map/gate_up/pallas_call | solution.py:879
  310.3 5.6 collective-permute-done.23.refs_1_.refs_8_
  315.9 13.6 %down.1 = (bf16[256,2048]{1,0:T(8,128)(2,1)}, bf16[256,2048]{1,0:T(8,128)(2,1)}, bf16[512,1024]{1,0:T(8,128)(2,1)}, bf16[512,1024]{1,0:T(8,128)(2,1)}) custom-call(bf16[1024,768]{1,0:T(8,128)(2,1)} %get-tuple-element.134.own_ref.left_ref, bf16[1024,768]{1,0:T(8,128)(2,1)} %get-tuple-element.117.other_ref, ...), custom_call_target="tpu_custom_call" | custom-call | flops 644245120 | bytes 2097152 | tf_op jit(solution)/shard_map/down/pallas_call | solution.py:879
  334.6 20.4 %collective-permute-done.24 = bf16[256,2048]{1,0:T(8,128)(2,1)} collective-permute-done((bf16[256,2048]{1,0:T(8,128)(2,1)}, bf16[256,2048]{1,0:T(8,128)(2,1)}, u32[]{:S(2)}, u32[]{:S(2)}) %collective-permute-start.24) | collective-permute-done | bytes 1048608 | tf_op jit(solution)/shard_map/ppermute | solution.py:406
  362.6 7.1 collective-permute-done.26
  378.9 9.4 %collective-permute-done.29.refs_2_ = bf16[256,1024]{1,0:T(8,128)(2,1)S(1)} collective-permute-done((bf16[256,1024]{1,0:T(8,128)(2,1)S(1)}, bf16[256,1024]{1,0:T(8,128)(2,1)S(1)}, u32[]{:S(2)}, u32[]{:S(2)}) %collective-permute-start.29) | collective-permute-done | bytes 524320 | tf_op jit(solution)/shard_map/ppermute | solution.py:406
  396.3 5.8 pad_maximum_fusion
  404.2 12.4 %collective-permute-done.31.refs_4_ = bf16[256,2048]{1,0:T(8,128)(2,1)S(1)} collective-permute-done((bf16[256,2048]{1,0:T(8,128)(2,1)S(1)}, bf16[256,2048]{1,0:T(8,128)(2,1)S(1)}, u32[]{:S(2)}, u32[]{:S(2)}) %collective-permute-start.31) | collective-permute-done | bytes 1048608 | tf_op jit(solution)/shard_map/ppermute | solution.py:406
  418.9 16.9 %down_back.1 = (bf16[1024,1536]{1,0:T(8,128)(2,1)}, bf16[1024,1536]{1,0:T(8,128)(2,1)}, bf16[1024,2048]{1,0:T(8,128)(2,1)}) custom-call(bf16[512,1024]{1,0:T(8,128)(2,1)} %copy-done.13, bf16[256,1024]{1,0:T(8,128)(2,1)} %copy-done.49, bf16[256,1024]{1,0:T(8,128)(2,1)} %copy-done.48, bf16[512,1024]{1,0:T(8,128)(2,1)} %copy-done.63, ...), custom_call_target="tpu_custom_call" | custom-call | flops 644245120 | bytes 2097152 | tf_op jit(solution)/shard_map/down_back/pallas_call | solution.py:879
  436.4 7.0 collective-permute-done.37.right_far_ref
  443.4 12.8 %outer.2 = bf16[704,2048]{1,0:T(8,128)(2,1)} custom-call(bf16[1024,768]{1,0:T(8,128)(2,1)} %get-tuple-element.134.own_ref.left_ref, bf16[1024,768]{1,0:T(8,128)(2,1)} %copy-done.54, bf16[1024,2048]{1,0:T(8,128)(2,1)} %get-tuple-element.136.right_ref, bf16[1024,2048]{1,0:T(8,128)(2,1)} %collective-permute-done.37.right_far_ref), custom_call_target="tpu_custom_call" | custom-call | flops 644245120 | bytes 1677721 | tf_op jit(solution)/shard_map/outer/pallas_call | solution.py:940
  456.3 21.2 %gate_up_back.1 = (bf16[256,2048]{1,0:T(8,128)(2,1)}, bf16[256,2048]{1,0:T(8,128)(2,1)}, bf16[512,1024]{1,0:T(8,128)(2,1)}, bf16[512,1024]{1,0:T(8,128)(2,1)}) custom-call(bf16[1024,1536]{1,0:T(8,128)(2,1)} %get-tuple-element.142.own_ref.left_ref, bf16[1024,1536]{1,0:T(8,128)(2,1)} %get-tuple-element.138.other_ref, ...), custom_call_target="tpu_custom_call" | custom-call | flops 1288490240 | bytes 2097152 | tf_op jit(solution)/shard_map/gate_up_back/pallas_call | solution.py:879
  479.9 21.3 %outer.3 = bf16[1408,2048]{1,0:T(8,128)(2,1)} custom-call(bf16[1024,1536]{1,0:T(8,128)(2,1)} %get-tuple-element.142.own_ref.left_ref, bf16[1024,1536]{1,0:T(8,128)(2,1)} %collective-permute-done.36.left_far_ref, bf16[1024,2048]{1,0:T(8,128)(2,1)} %get-tuple-element.144.right_ref, bf16[1024,2048]{1,0:T(8,128)(2,1)} %copy-done.26), custom_call_target="tpu_custom_call" | custom-call | flops 1288490240 | bytes 1677721 | tf_op jit(solution)/shard_map/outer/pallas_call | solution.py:940
  503.8 6.5 reduce-scatter.6.cloned.1.call-done
  516.5 9.0 %collective-permute-done.40 = bf16[256,1024]{1,0:T(8,128)(2,1)S(1)} collective-permute-done((bf16[256,1024]{1,0:T(8,128)(2,1)S(1)}, bf16[256,1024]{1,0:T(8,128)(2,1)S(1)}, u32[]{:S(2)}, u32[]{:S(2)}) %collective-permute-start.40) | collective-permute-done | bytes 524320 | tf_op jit(solution)/shard_map/ppermute | solution.py:406
  539.5 6.5 project.3
  554.6 16.3 %collective-permute-done.43 = bf16[512,1024]{1,0:T(8,128)(2,1)S(1)} collective-permute-done((bf16[512,1024]{1,0:T(8,128)(2,1)}, bf16[512,1024]{1,0:T(8,128)(2,1)S(1)}, u32[]{:S(2)}, u32[]{:S(2)}) %collective-permute-start.43) | collective-permute-done | bytes 1048608 | tf_op jit(solution)/shard_map/ppermute | solution.py:406
  570.9 5.6 collective-permute-done.45
  577.8 14.7 %attend_back.1 = (bf16[512,1024]{1,0:T(8,128)(2,1)}, bf16[2048,512]{1,0:T(8,128)(2,1)}) custom-call(s32[8]{0:T(128)} %stack.50.flags, bf16[512,1024]{1,0:T(8,128)(2,1)} %copy-done.24, bf16[512,1024]{1,0:T(8,128)(2,1)} %add_convert_fusion.do_ref, f32[8,1,512]{2,1,0:T(1,128)} %get-tuple-element.155.lse_ref, f32[64,512]{1,0:T(8,128)} %get-tuple-element.349.cos_ref, ...), custom_call_target="tpu_custom_call" | custom-call | flops 805306368 | bytes 1258291 | tf_op jit(solution)/shard_map/attend_back/pallas_call | solution.py:600
  592.5 22.7 %reduce-scatter.8.cloned.1.call-done = bf16[352,2048]{1,0:T(8,128)(2,1)} async-done(((bf16[1408,2048]{1,0:T(8,128)(2,1)}), bf16[352,2048]{1,0:T(8,128)(2,1)}) %reduce-scatter.8.cloned.1.call-update) | async-done | bytes 1441808 | tf_op jit(solution)/shard_map/reduce_scatter | solution.py:1197
  621.2 4.7 convolution_convert_fusion
  629.1 8.7 %collective-permute-done.47 = bf16[352,1024]{1,0:T(8,128)(2,1)S(1)} collective-permute-done((bf16[352,1024]{1,0:T(8,128)(2,1)}, bf16[352,1024]{1,0:T(8,128)(2,1)S(1)}, u32[]{:S(2)}, u32[]{:S(2)}) %collective-permute-start.47) | collective-permute-done | bytes 720928 | tf_op jit(solution)/shard_map/ppermute | solution.py:406
  637.8 24.6 %reduce-scatter.10.cloned.1.call-done = bf16[512,512]{1,0:T(8,128)(2,1)} async-done(((bf16[2048,512]{1,0:T(8,128)(2,1)}), bf16[512,512]{1,0:T(8,128)(2,1)}) %reduce-scatter.10.cloned.1.call-update) | async-done | bytes 524304 | tf_op jit(solution)/shard_map/reduce_scatter | solution.py:1197
  668.5 6.5 merge.3
  677.3 4.7 convolution_convert_fusion.1
  690.7 7.1 collective-permute-done.50.other_ref
  704.3 6.4 collective-permute-done.62
  713.4 5.7 key_value_back.1
  721.8 6.3 collective-permute-done.69.far_ref
  753.8 4.4 collective-permute-done.67
  762.6 6.3 collective-permute-done.63
  770.0 5.0 settle.3
  781.0 8.0 settle.2
  (471 shorter events, 233.3 us)
Async XLA Ops:
  7.2 66.4 %all-gather.5.cloned.1.call-start = ((), (), s32[]{:S(2)}) async-start(), calls=%async_computation.5 | async-start | bytes 2621440 | tf_op jit(solution)/shard_map/all_gather | solution.py:67
  10.4 134.7 %all-gather.7.cloned.1.call-start = ((), (), s32[]{:S(2)}) async-start(), calls=%async_computation.6 | async-start | bytes 2621440 | tf_op jit(solution)/shard_map/all_gather | solution.py:67
  10.9 16.3 %collective-permute-start.1 = (bf16[128,1024]{1,0:T(8,128)(2,1)S(1)}, bf16[128,1024]{1,0:T(8,128)(2,1)S(1)}, u32[]{:S(2)}, u32[]{:S(2)}) collective-permute-start(bf16[128,1024]{1,0:T(8,128)(2,1)S(1)} %select_bitcast_fusion), channel_id=1, source_target_pairs={{0,2},{2,0},{4,6},{6,4},{1,3},{3,1},{5,7},{7,5},{8,10},{10,8},{12,... | collective-permute-start | bytes 786440 | tf_op jit(solution)/shard_map/ppermute | solution.py:406
  13.9 26.0 %collective-permute-start.2 = (bf16[128,1024]{1,0:T(8,128)(2,1)S(1)}, bf16[128,1024]{1,0:T(8,128)(2,1)S(1)}, u32[]{:S(2)}, u32[]{:S(2)}) collective-permute-start(bf16[128,1024]{1,0:T(8,128)(2,1)S(1)} %select_bitcast_fusion), channel_id=1, source_target_pairs={{0,4},{2,6},{4,0},{6,2},{1,5},{3,7},{5,1},{7,3},{8,12},{10,14},{12... | collective-permute-start | bytes 786440 | tf_op jit(solution)/shard_map/ppermute | solution.py:406
  16.5 26.4 %collective-permute-start.3 = (bf16[128,1024]{1,0:T(8,128)(2,1)S(1)}, bf16[128,1024]{1,0:T(8,128)(2,1)S(1)}, u32[]{:S(2)}, u32[]{:S(2)}) collective-permute-start(bf16[128,1024]{1,0:T(8,128)(2,1)S(1)} %select_bitcast_fusion), channel_id=1, source_target_pairs={{0,6},{2,4},{4,2},{6,0},{1,7},{3,5},{5,3},{7,1},{8,14},{10,12},{12... | collective-permute-start | bytes 786440 | tf_op jit(solution)/shard_map/ppermute | solution.py:406
  24.0 27.2 %collective-permute-start.5 = (bf16[528,1024]{1,0:T(8,128)(2,1)}, bf16[528,1024]{1,0:T(8,128)(2,1)}, u32[]{:S(2)}, u32[]{:S(2)}) collective-permute-start(bf16[528,1024]{1,0:T(8,128)(2,1)} %pad_maximum_fusion.9), channel_id=1, source_target_pairs={{0,1},{1,0},{2,3},{3,2},{4,5},{5,4},{6,7},{7,6},{8,9},{9,8},{10,11... | collective-permute-start | bytes 3244040 | tf_op jit(solution)/shard_map/ppermute | solution.py:406
  26.0 23.3 %collective-permute-start = (f32[512]{0:T(512)S(1)}, f32[512]{0:T(512)S(1)}, u32[]{:S(2)}, u32[]{:S(2)}) collective-permute-start(f32[512]{0:T(512)S(1)} %fusion.1), channel_id=1, source_target_pairs={{0,1},{1,0},{2,3},{3,2},{4,5},{5,4},{6,7},{7,6},{8,9},{9,8},{10,11... | collective-permute-start | bytes 6152 | tf_op jit(solution)/shard_map/ppermute | solution.py:406
  44.0 16.3 %collective-permute-start.7 = (f32[1]{0:T(128)}, f32[1]{0:T(128)}, u32[]{:S(2)}, u32[]{:S(2)}) collective-permute-start(f32[1]{0:T(128)} %bitcast.18), channel_id=1, source_target_pairs={{0,8},{8,0},{16,24},{24,16},{1,9},{9,1},{17,25},{25,17},{2,10},{10... | collective-permute-start | bytes 20 | tf_op jit(solution)/shard_map/ppermute | solution.py:406
  76.6 164.1 %all-gather.9.cloned.1.call-start = ((), (), s32[]{:S(2)}) async-start(), calls=%async_computation.7 | async-start | bytes 7208960 | tf_op jit(solution)/shard_map/all_gather | solution.py:67
  78.1 25.2 %collective-permute-start.10 = (bf16[512,1024]{1,0:T(8,128)(2,1)S(1)}, bf16[512,1024]{1,0:T(8,128)(2,1)S(1)}, u32[]{:S(2)}, u32[]{:S(2)}) collective-permute-start(bf16[512,1024]{1,0:T(8,128)(2,1)S(1)} %pad_maximum_fusion.12.refs_0_), channel_id=1, source_target_pairs={{0,16},{8,24},{16,0},{24,8},{1,17},{9,25},{17,1},{25,9},{2,18},{10... | collective-permute-start | bytes 3145736 | tf_op jit(solution)/shard_map/ppermute | solution.py:406
  79.7 27.4 %collective-permute-start.9 = (bf16[512,1024]{1,0:T(8,128)(2,1)S(1)}, bf16[512,1024]{1,0:T(8,128)(2,1)}, u32[]{:S(2)}, u32[]{:S(2)}) collective-permute-start(bf16[512,1024]{1,0:T(8,128)(2,1)S(1)} %pad_maximum_fusion.12.refs_0_), channel_id=1, source_target_pairs={{0,8},{8,0},{16,24},{24,16},{1,9},{9,1},{17,25},{25,17},{2,10},{10... | collective-permute-start | bytes 3145736 | tf_op jit(solution)/shard_map/ppermute | solution.py:406
  117.6 192.6 %all-gather.11.cloned.1.call-start = ((), (), s32[]{:S(2)}) async-start(), calls=%async_computation.8 | async-start | bytes 3604480 | tf_op jit(solution)/shard_map/all_gather | solution.py:67
  118.2 25.3 %collective-permute-start.13 = (bf16[512,1024]{1,0:T(8,128)(2,1)S(1)}, bf16[512,1024]{1,0:T(8,128)(2,1)S(1)}, u32[]{:S(2)}, u32[]{:S(2)}) collective-permute-start(bf16[512,1024]{1,0:T(8,128)(2,1)S(1)} %pad_maximum_fusion.13.refs_0_), channel_id=1, source_target_pairs={{0,16},{8,24},{16,0},{24,8},{1,17},{9,25},{17,1},{25,9},{2,18},{10... | collective-permute-start | bytes 3145736 | tf_op jit(solution)/shard_map/ppermute | solution.py:406
  119.7 25.4 %collective-permute-start.12 = (bf16[512,1024]{1,0:T(8,128)(2,1)}, bf16[512,1024]{1,0:T(8,128)(2,1)}, u32[]{:S(2)}, u32[]{:S(2)}) collective-permute-start(bf16[512,1024]{1,0:T(8,128)(2,1)} %get-tuple-element.100), channel_id=1, source_target_pairs={{0,1},{1,0},{2,3},{3,2},{4,5},{5,4},{6,7},{7,6},{8,9},{9,8},{10,11... | collective-permute-start | bytes 3145736 | tf_op jit(solution)/shard_map/ppermute | solution.py:406
  163.9 25.7 %collective-permute-start.15 = (bf16[512,1024]{1,0:T(8,128)(2,1)}, bf16[512,1024]{1,0:T(8,128)(2,1)S(1)}, u32[]{:S(2)}, u32[]{:S(2)}) collective-permute-start(bf16[512,1024]{1,0:T(8,128)(2,1)} %get-tuple-element.107.own_ref), channel_id=1, source_target_pairs={{0,1},{1,0},{2,3},{3,2},{4,5},{5,4},{6,7},{7,6},{8,9},{9,8},{10,11... | collective-permute-start | bytes 3145736 | tf_op jit(solution)/shard_map/ppermute | solution.py:406
  240.8 45.9 %collective-permute-start.21 = (bf16[1408,2048]{1,0:T(8,128)(2,1)}, bf16[1408,2048]{1,0:T(8,128)(2,1)}, u32[]{:S(2)}, u32[]{:S(2)}) collective-permute-start(bf16[1408,2048]{1,0:T(8,128)(2,1)} %all-gather.9.cloned.1.call-done.refs_5_.refs_0_), channel_id=1, source_target_pairs={{0,8},{8,0},{16,24},{24,16},{1,9},{9,1},{17,25},{25,17},{2,10},{10... | collective-permute-start | bytes 17301512 | tf_op jit(solution)/shard_map/ppermute | solution.py:406
  242.9 267.4 %reduce-scatter.6.cloned.1.call-start = ((), (), s32[]{:S(2)}) async-start(), calls=%async_computation.9 | async-start | bytes 3604480 | tf_op jit(solution)/shard_map/reduce_scatter | solution.py:1197
  258.9 24.9 %collective-permute-start.20 = (bf16[256,2048]{1,0:T(8,128)(2,1)S(1)}, bf16[256,2048]{1,0:T(8,128)(2,1)S(1)}, u32[]{:S(2)}, u32[]{:S(2)}) collective-permute-start(bf16[256,2048]{1,0:T(8,128)(2,1)S(1)} %pad_maximum_fusion.15), channel_id=1, source_target_pairs={{0,16},{8,24},{16,0},{24,8},{1,17},{9,25},{17,1},{25,9},{2,18},{10... | collective-permute-start | bytes 3145736 | tf_op jit(solution)/shard_map/ppermute | solution.py:406
  260.5 26.2 %collective-permute-start.19 = (bf16[512,1024]{1,0:T(8,128)(2,1)S(1)}, bf16[512,1024]{1,0:T(8,128)(2,1)S(1)}, u32[]{:S(2)}, u32[]{:S(2)}) collective-permute-start(bf16[512,1024]{1,0:T(8,128)(2,1)S(1)} %pad_maximum_fusion.14), channel_id=1, source_target_pairs={{0,1},{1,0},{2,3},{3,2},{4,5},{5,4},{6,7},{7,6},{8,9},{9,8},{10,11... | collective-permute-start | bytes 3145736 | tf_op jit(solution)/shard_map/ppermute | solution.py:406
  262.0 48.1 %collective-permute-start.22 = (bf16[512,1024]{1,0:T(8,128)(2,1)S(1)}, bf16[512,1024]{1,0:T(8,128)(2,1)}, u32[]{:S(2)}, u32[]{:S(2)}) collective-permute-start(bf16[512,1024]{1,0:T(8,128)(2,1)S(1)} %copy-done.5), channel_id=1, source_target_pairs={{0,1},{1,0},{2,3},{3,2},{4,5},{5,4},{6,7},{7,6},{8,9},{9,8},{10,11... | collective-permute-start | bytes 3145736 | tf_op jit(solution)/shard_map/ppermute | solution.py:406
  329.5 25.6 %collective-permute-start.24 = (bf16[256,2048]{1,0:T(8,128)(2,1)}, bf16[256,2048]{1,0:T(8,128)(2,1)}, u32[]{:S(2)}, u32[]{:S(2)}) collective-permute-start(bf16[256,2048]{1,0:T(8,128)(2,1)} %get-tuple-element.121), channel_id=1, source_target_pairs={{0,16},{8,24},{16,0},{24,8},{1,17},{9,25},{17,1},{25,9},{2,18},{10... | collective-permute-start | bytes 3145736 | tf_op jit(solution)/shard_map/ppermute | solution.py:406
  330.1 25.2 %collective-permute-start.25 = (bf16[512,1024]{1,0:T(8,128)(2,1)}, bf16[512,1024]{1,0:T(8,128)(2,1)}, u32[]{:S(2)}, u32[]{:S(2)}) collective-permute-start(bf16[512,1024]{1,0:T(8,128)(2,1)} %get-tuple-element.122), channel_id=1, source_target_pairs={{0,1},{1,0},{2,3},{3,2},{4,5},{5,4},{6,7},{7,6},{8,9},{9,8},{10,11... | collective-permute-start | bytes 3145736 | tf_op jit(solution)/shard_map/ppermute | solution.py:406
  334.6 67.5 %collective-permute-start.35 = (bf16[1024,2048]{1,0:T(8,128)(2,1)S(1)}, bf16[1024,2048]{1,0:T(8,128)(2,1)S(1)}, u32[]{:S(2)}, u32[]{:S(2)}) collective-permute-start(bf16[1024,2048]{1,0:T(8,128)(2,1)S(1)} %copy-done.25), channel_id=1, source_target_pairs={{0,8},{8,0},{16,24},{24,16},{1,9},{9,1},{17,25},{25,17},{2,10},{10... | collective-permute-start | bytes 12582920 | tf_op jit(solution)/shard_map/ppermute | solution.py:406
  362.5 33.8 %collective-permute-start.32 = (bf16[512,2048]{1,0:T(8,128)(2,1)S(1)}, bf16[512,2048]{1,0:T(8,128)(2,1)S(1)}, u32[]{:S(2)}, u32[]{:S(2)}) collective-permute-start(bf16[512,2048]{1,0:T(8,128)(2,1)S(1)} %pad_maximum_fusion.3), channel_id=1, source_target_pairs={{0,8},{8,0},{16,24},{24,16},{1,9},{9,1},{17,25},{25,17},{2,10},{10... | collective-permute-start | bytes 6291464 | tf_op jit(solution)/shard_map/ppermute | solution.py:406
  377.5 15.8 %collective-permute-start.33 = (bf16[512,1024]{1,0:T(8,128)(2,1)S(1)}, bf16[512,1024]{1,0:T(8,128)(2,1)S(1)}, u32[]{:S(2)}, u32[]{:S(2)}) collective-permute-start(bf16[512,1024]{1,0:T(8,128)(2,1)S(1)} %pad_maximum_fusion.18), channel_id=1, source_target_pairs={{0,8},{8,0},{16,24},{24,16},{1,9},{9,1},{17,25},{25,17},{2,10},{10... | collective-permute-start | bytes 3145736 | tf_op jit(solution)/shard_map/ppermute | solution.py:406
  391.8 24.8 %collective-permute-start.31 = (bf16[256,2048]{1,0:T(8,128)(2,1)S(1)}, bf16[256,2048]{1,0:T(8,128)(2,1)S(1)}, u32[]{:S(2)}, u32[]{:S(2)}) collective-permute-start(bf16[256,2048]{1,0:T(8,128)(2,1)S(1)} %pad_maximum_fusion.17), channel_id=1, source_target_pairs={{0,16},{8,24},{16,0},{24,8},{1,17},{9,25},{17,1},{25,9},{2,18},{10... | collective-permute-start | bytes 3145736 | tf_op jit(solution)/shard_map/ppermute | solution.py:406
  393.3 24.6 %collective-permute-start.30 = (bf16[512,1024]{1,0:T(8,128)(2,1)S(1)}, bf16[512,1024]{1,0:T(8,128)(2,1)S(1)}, u32[]{:S(2)}, u32[]{:S(2)}) collective-permute-start(bf16[512,1024]{1,0:T(8,128)(2,1)S(1)} %pad_maximum_fusion.16), channel_id=1, source_target_pairs={{0,1},{1,0},{2,3},{3,2},{4,5},{5,4},{6,7},{7,6},{8,9},{9,8},{10,11... | collective-permute-start | bytes 3145736 | tf_op jit(solution)/shard_map/ppermute | solution.py:406
  435.9 20.3 %collective-permute-start.36 = (bf16[1024,1536]{1,0:T(8,128)(2,1)}, bf16[1024,1536]{1,0:T(8,128)(2,1)}, u32[]{:S(2)}, u32[]{:S(2)}) collective-permute-start(bf16[1024,1536]{1,0:T(8,128)(2,1)} %get-tuple-element.138.other_ref), channel_id=1, source_target_pairs={{0,8},{8,0},{16,24},{24,16},{1,9},{9,1},{17,25},{25,17},{2,10},{10... | collective-permute-start | bytes 9437192 | tf_op jit(solution)/shard_map/ppermute | solution.py:406
  456.2 159.0 %reduce-scatter.8.cloned.1.call-start = ((), (), s32[]{:S(2)}) async-start(), calls=%async_computation.10 | async-start | bytes 7208960 | tf_op jit(solution)/shard_map/reduce_scatter | solution.py:1197
  477.4 25.6 %collective-permute-start.38 = (bf16[256,2048]{1,0:T(8,128)(2,1)}, bf16[256,2048]{1,0:T(8,128)(2,1)}, u32[]{:S(2)}, u32[]{:S(2)}) collective-permute-start(bf16[256,2048]{1,0:T(8,128)(2,1)} %get-tuple-element.140), channel_id=1, source_target_pairs={{0,16},{8,24},{16,0},{24,8},{1,17},{9,25},{17,1},{25,9},{2,18},{10... | collective-permute-start | bytes 3145736 | tf_op jit(solution)/shard_map/ppermute | solution.py:406
  478.6 25.2 %collective-permute-start.39 = (bf16[512,1024]{1,0:T(8,128)(2,1)}, bf16[512,1024]{1,0:T(8,128)(2,1)}, u32[]{:S(2)}, u32[]{:S(2)}) collective-permute-start(bf16[512,1024]{1,0:T(8,128)(2,1)} %get-tuple-element.141), channel_id=1, source_target_pairs={{0,1},{1,0},{2,3},{3,2},{4,5},{5,4},{6,7},{7,6},{8,9},{9,8},{10,11... | collective-permute-start | bytes 3145736 | tf_op jit(solution)/shard_map/ppermute | solution.py:406
  510.3 152.1 %reduce-scatter.10.cloned.1.call-start = ((), (), s32[]{:S(2)}) async-start(), calls=%async_computation.11 | async-start | bytes 2621440 | tf_op jit(solution)/shard_map/reduce_scatter | solution.py:1197
  546.1 24.8 %collective-permute-start.43 = (bf16[512,1024]{1,0:T(8,128)(2,1)}, bf16[512,1024]{1,0:T(8,128)(2,1)S(1)}, u32[]{:S(2)}, u32[]{:S(2)}) collective-permute-start(bf16[512,1024]{1,0:T(8,128)(2,1)} %get-tuple-element.150), channel_id=1, source_target_pairs={{0,1},{1,0},{2,3},{3,2},{4,5},{5,4},{6,7},{7,6},{8,9},{9,8},{10,11... | collective-permute-start | bytes 3145736 | tf_op jit(solution)/shard_map/ppermute | solution.py:406
  551.9 24.6 %collective-permute-start.45 = (bf16[512,1024]{1,0:T(8,128)(2,1)S(1)}, bf16[512,1024]{1,0:T(8,128)(2,1)}, u32[]{:S(2)}, u32[]{:S(2)}) collective-permute-start(bf16[512,1024]{1,0:T(8,128)(2,1)S(1)} %pad_maximum_fusion.19), channel_id=1, source_target_pairs={{0,16},{8,24},{16,0},{24,8},{1,17},{9,25},{17,1},{25,9},{2,18},{10... | collective-permute-start | bytes 3145736 | tf_op jit(solution)/shard_map/ppermute | solution.py:406
  615.2 136.3 %reduce-scatter.14.cloned.1.call-start = ((), (), s32[]{:S(2)}) async-start(), calls=%async_computation.13 | async-start | bytes 1310720 | tf_op jit(solution)/shard_map/reduce_scatter | solution.py:1037
  618.7 19.1 %collective-permute-start.47 = (bf16[352,1024]{1,0:T(8,128)(2,1)}, bf16[352,1024]{1,0:T(8,128)(2,1)S(1)}, u32[]{:S(2)}, u32[]{:S(2)}) collective-permute-start(bf16[352,1024]{1,0:T(8,128)(2,1)} %get-tuple-element.296), channel_id=1, source_target_pairs={{0,1},{1,0},{2,3},{3,2},{4,5},{5,4},{6,7},{7,6},{8,9},{9,8},{10,11... | collective-permute-start | bytes 2162696 | tf_op jit(solution)/shard_map/ppermute | solution.py:406
  620.7 47.8 %collective-permute-start.46 = (bf16[512,1024]{1,0:T(8,128)(2,1)S(1)}, bf16[512,1024]{1,0:T(8,128)(2,1)}, u32[]{:S(2)}, u32[]{:S(2)}) collective-permute-start(bf16[512,1024]{1,0:T(8,128)(2,1)S(1)} %copy-done.28), channel_id=1, source_target_pairs={{0,1},{1,0},{2,3},{3,2},{4,5},{5,4},{6,7},{7,6},{8,9},{9,8},{10,11... | collective-permute-start | bytes 3145736 | tf_op jit(solution)/shard_map/ppermute | solution.py:406
  627.6 47.4 %collective-permute-start.61 = (bf16[256,2048]{1,0:T(8,128)(2,1)}, bf16[256,2048]{1,0:T(8,128)(2,1)}, u32[]{:S(2)}, u32[]{:S(2)}) collective-permute-start(bf16[256,2048]{1,0:T(8,128)(2,1)} %slice.545), channel_id=1, source_target_pairs={{0,16},{8,24},{16,0},{24,8},{1,17},{9,25},{17,1},{25,9},{2,18},{10... | collective-permute-start | bytes 3145736 | tf_op jit(solution)/shard_map/ppermute | solution.py:406
  676.6 21.2 %collective-permute-start.50 = (bf16[512,512]{1,0:T(8,128)(2,1)}, bf16[512,512]{1,0:T(8,128)(2,1)}, u32[]{:S(2)}, u32[]{:S(2)}) collective-permute-start(bf16[512,512]{1,0:T(8,128)(2,1)} %pad_maximum_fusion.26.own_ref), channel_id=1, source_target_pairs={{0,1},{1,0},{2,3},{3,2},{4,5},{5,4},{6,7},{7,6},{8,9},{9,8},{10,11... | collective-permute-start | bytes 1572872 | tf_op jit(solution)/shard_map/ppermute | solution.py:406
  677.2 82.7 %reduce-scatter.12.cloned.1.call-start = ((), (), s32[]{:S(2)}) async-start(), calls=%async_computation.12 | async-start | bytes 1310720 | tf_op jit(solution)/shard_map/reduce_scatter | solution.py:1037
  687.6 40.5 %collective-permute-start.69 = (bf16[704,1024]{1,0:T(8,128)(2,1)S(1)}, bf16[704,1024]{1,0:T(8,128)(2,1)}, u32[]{:S(2)}, u32[]{:S(2)}) collective-permute-start(bf16[704,1024]{1,0:T(8,128)(2,1)S(1)} %pad_maximum_fusion.7.near_ref), channel_id=1, source_target_pairs={{0,16},{8,24},{16,0},{24,8},{1,17},{9,25},{17,1},{25,9},{2,18},{10... | collective-permute-start | bytes 4325384 | tf_op jit(solution)/shard_map/ppermute | solution.py:406
  689.2 21.5 %collective-permute-start.62 = (bf16[256,1024]{1,0:T(8,128)(2,1)S(1)}, bf16[256,1024]{1,0:T(8,128)(2,1)S(1)}, u32[]{:S(2)}, u32[]{:S(2)}) collective-permute-start(bf16[256,1024]{1,0:T(8,128)(2,1)S(1)} %slice.546), channel_id=1, source_target_pairs={{0,1},{1,0},{2,3},{3,2},{4,5},{5,4},{6,7},{7,6},{8,9},{9,8},{10,11... | collective-permute-start | bytes 1572872 | tf_op jit(solution)/shard_map/ppermute | solution.py:406
  698.8 20.2 %collective-permute-start.52 = (bf16[64,1024]{1,0:T(8,128)(2,1)}, bf16[64,1024]{1,0:T(8,128)(2,1)S(1)}, u32[]{:S(2)}, u32[]{:S(2)}) collective-permute-start(bf16[64,1024]{1,0:T(8,128)(2,1)} %get-tuple-element.325), channel_id=1, source_target_pairs={{0,1},{1,5},{2,0},{3,4},{4,3},{5,7},{6,2},{7,6},{8,9},{9,13},{10,8... | collective-permute-start | bytes 393224 | tf_op jit(solution)/shard_map/ppermute | solution.py:1052
  700.2 20.4 %collective-permute-start.53 = (bf16[64,1024]{1,0:T(8,128)(2,1)}, bf16[64,1024]{1,0:T(8,128)(2,1)}, u32[]{:S(2)}, u32[]{:S(2)}) collective-permute-start(bf16[64,1024]{1,0:T(8,128)(2,1)} %get-tuple-element.326), channel_id=1, source_target_pairs={{0,2},{1,6},{2,3},{3,7},{4,0},{5,4},{6,1},{7,5},{8,10},{9,14},{10,... | collective-permute-start | bytes 393224 | tf_op jit(solution)/shard_map/ppermute | solution.py:1052
  700.9 19.8 %collective-permute-start.54 = (bf16[64,1024]{1,0:T(8,128)(2,1)}, bf16[64,1024]{1,0:T(8,128)(2,1)}, u32[]{:S(2)}, u32[]{:S(2)}) collective-permute-start(bf16[64,1024]{1,0:T(8,128)(2,1)} %get-tuple-element.327), channel_id=1, source_target_pairs={{0,3},{1,7},{2,2},{3,6},{4,1},{5,5},{6,0},{7,4},{8,11},{9,15},{10,... | collective-permute-start | bytes 393224 | tf_op jit(solution)/shard_map/ppermute | solution.py:1052
  719.1 23.1 %collective-permute-start.72 = (bf16[352,1024]{1,0:T(8,128)(2,1)S(1)}, bf16[352,1024]{1,0:T(8,128)(2,1)S(1)}, u32[]{:S(2)}, u32[]{:S(2)}) collective-permute-start(bf16[352,1024]{1,0:T(8,128)(2,1)S(1)} %copy-done.35), channel_id=1, source_target_pairs={{0,16},{8,24},{16,0},{24,8},{1,17},{9,25},{17,1},{25,9},{2,18},{10... | collective-permute-start | bytes 2162696 | tf_op jit(solution)/shard_map/ppermute | solution.py:406
  731.4 49.6 %collective-permute-start.70 = (bf16[1408,1024]{1,0:T(8,128)(2,1)}, bf16[1408,1024]{1,0:T(8,128)(2,1)}, u32[]{:S(2)}, u32[]{:S(2)}) collective-permute-start(bf16[1408,1024]{1,0:T(8,128)(2,1)} %pad_maximum_fusion.1), channel_id=1, source_target_pairs={{0,8},{8,0},{16,24},{24,16},{1,9},{9,1},{17,25},{25,17},{2,10},{10... | collective-permute-start | bytes 8650760 | tf_op jit(solution)/shard_map/ppermute | solution.py:406
  743.7 26.3 %collective-permute-start.73 = (bf16[704,1024]{1,0:T(8,128)(2,1)S(1)}, bf16[704,1024]{1,0:T(8,128)(2,1)}, u32[]{:S(2)}, u32[]{:S(2)}) collective-permute-start(bf16[704,1024]{1,0:T(8,128)(2,1)S(1)} %pad_maximum_fusion.8), channel_id=1, source_target_pairs={{0,8},{8,0},{16,24},{24,16},{1,9},{9,1},{17,25},{25,17},{2,10},{10... | collective-permute-start | bytes 4325384 | tf_op jit(solution)/shard_map/ppermute | solution.py:406
  (125 other events, 1100.3 us)
Sparse Core Ops, SparseCore 0:
  10.6 62.9 all-gather.4
  76.8 56.3 all-gather.6
  135.3 105.4 all-gather.8
  243.0 57.5 all-gather.10
  456.3 53.9 reduce-scatter.5
  513.1 102.1 reduce-scatter.7
  618.1 44.3 reduce-scatter.9
  677.4 28.1 reduce-scatter.13
  713.5 31.4 reduce-scatter.11

commit v4 on v3

--- a/solution.py
+++ b/solution.py
@@ -949,41 +949,73 @@
     )(*lefts, *rights)
 
 
-def settle_kernel(kinds, turned, scalars, near_ref, far_ref, other_ref, *refs):
-    outs, held_ref = refs[:-1], refs[-1]
+def settle_kernel(kinds, turned, scalars, *refs):
+    slots, outs, held_ref = refs[:4], refs[4:-1], refs[-1]
     d, y = scalars[0], scalars[1]
-    part = near_ref.shape[0] // (2 * kinds)
+    part = slots[0].shape[0] // (2 * kinds)
     for kind in range(kinds):
-        for slot in range(4):
-            ref = (near_ref, other_ref, far_ref, other_ref)[slot]
-            base = near_ref.shape[0] if slot == 3 else 0
+        for slot, ref in enumerate(slots):
             for side in range(2):
                 at = ((d ^ slot) * 2 + (y if side == 0 else 1 - y)) * part
-                rows = slice(base + (side * kinds + kind) * part, base + (side * kinds + kind + 1) * part)
+                rows = slice((side * kinds + kind) * part, (side * kinds + kind + 1) * part)
                 target = held_ref if turned else outs[kind]
                 target[pl.ds(pl.multiple_of(at, 16), part), :] = wide(ref[rows, :])
         if turned:
             outs[kind][...] = jnp.transpose(held_ref[...])
 
 
-def settle(d, y, near, far, other, kinds, turned):
-    width = near.shape[1]
-    hidden = 4 * near.shape[0] // kinds
+def settle(scalars, slots, kinds, turned):
+    rows, width = slots[0].shape
+    hidden = 4 * rows // kinds
     lanes = 256
-    spec = lambda x: pl.BlockSpec((x.shape[0], lanes), lambda i: (0, i))
+    across = lambda n: pl.BlockSpec((n, lanes), lambda i: (0, i))
     shape = (width, hidden) if turned else (hidden, width)
-    out_spec = pl.BlockSpec((lanes, hidden), lambda i: (i, 0)) if turned else pl.BlockSpec((hidden, lanes), lambda i: (0, i))
+    out_spec = pl.BlockSpec((lanes, hidden), lambda i: (i, 0)) if turned else across(hidden)
     return pl.pallas_call(
         functools.partial(settle_kernel, kinds, turned),
         out_shape=(jax.ShapeDtypeStruct(shape, jnp.float32),) * kinds,
         grid=(width // lanes,),
-        in_specs=[pl.BlockSpec(memory_space=pltpu.SMEM)] + [spec(x) for x in (near, far, other)],
+        in_specs=[pl.BlockSpec(memory_space=pltpu.SMEM)] + [across(rows)] * 4,
         out_specs=(out_spec,) * kinds,
         scratch_shapes=[pltpu.VMEM((hidden, lanes), jnp.float32)],
         compiler_params=pltpu.CompilerParams(vmem_limit_bytes=VMEM_BYTES),
-        cost_estimate=cost(hidden * width, 6 * kinds * hidden * width, 0),
+        cost_estimate=cost(hidden * width, 6 * kinds * hidden * width),
         name="settle",
-    )(jnp.stack([d, y]), near, far, other)
+    )(scalars, *slots)
+
+
+def finish_kernel(scalars, *refs):
+    slots, (q_ref, k_ref, v_ref, o_ref, q_held, kv_held) = refs[:4], refs[4:]
+    part = kv_held.shape[0] // 4
+    for slot, ref in enumerate(slots):
+        at = scalars[0] ^ slot
+        heads = pl.ds(pl.multiple_of(at * HEAD_SIZE, HEAD_SIZE), HEAD_SIZE)
+        q_held[heads, :] = wide(ref[:HEAD_SIZE, :])
+        kv_held[pl.ds(pl.multiple_of(at * part, part), part), :] = wide(ref[HEAD_SIZE : HEAD_SIZE + part, :])
+        o_ref[heads, :] = wide(ref[HEAD_SIZE + part :, :])
+    q_ref[...] = jnp.transpose(q_held[...])
+    k_ref[...] = jnp.transpose(kv_held[:HEAD_SIZE, :])
+    v_ref[...] = jnp.transpose(kv_held[HEAD_SIZE:, :])
+
+
+def finish(scalars, slots):
+    rows, width = slots[0].shape
+    lanes = 256
+    across = lambda n: pl.BlockSpec((n, lanes), lambda i: (0, i))
+    down = lambda n: pl.BlockSpec((lanes, n), lambda i: (i, 0))
+    heads = 4 * HEAD_SIZE
+    shapes = [(width, heads), (width, HEAD_SIZE), (width, HEAD_SIZE), (heads, width)]
+    return pl.pallas_call(
+        finish_kernel,
+        out_shape=tuple(jax.ShapeDtypeStruct(shape, jnp.float32) for shape in shapes),
+        grid=(width // lanes,),
+        in_specs=[pl.BlockSpec(memory_space=pltpu.SMEM)] + [across(rows)] * 4,
+        out_specs=(down(heads), down(HEAD_SIZE), down(HEAD_SIZE), across(heads)),
+        scratch_shapes=[pltpu.VMEM((heads, lanes), jnp.float32), pltpu.VMEM((2 * HEAD_SIZE, lanes), jnp.float32)],
+        compiler_params=pltpu.CompilerParams(vmem_limit_bytes=VMEM_BYTES),
+        cost_estimate=cost(rows * width, 24 * rows * width),
+        name="finish",
+    )(scalars, *slots)
 
 
 def plane_gather(x):
@@ -1030,27 +1062,6 @@
     even = low(dot_tn(both, right))
     part = half // 2
     return even, swap(even[part:], "dp", 2)
-
-
-def heads_home(own, other, y, later):
-    near = jnp.concatenate(xor_order([low(own), low(other)], y), axis=0)
-    near = lax.psum_scatter(after(near, later), "row", scatter_dimension=0, tiled=True)
-    return jnp.concatenate(xor_order(dp_slots(near), lax.axis_index("dp")), axis=0)
-
-
-def quarters_home(pieces, r):
-    n_row, n_col = lax.axis_size("row"), lax.axis_size("col")
-    groups = n_row // n_col
-    slots = xor_order(pieces, r)
-    received = []
-    for k in range(n_row):
-        pairs = []
-        for row in range(n_row):
-            for col in range(n_col):
-                head, half = divmod(row ^ k, n_col)
-                pairs.append((row * n_col + col, (col * groups + head) * n_col + half))
-        received.append(wide(lax.ppermute(slots[k], ("row", "col"), pairs)))
-    return low(sum(received[1:], received[0]))
 
 
 def fast_body(
@@ -1211,11 +1222,10 @@
         near = jnp.concatenate([part[:, :width], swap(part[:, width:], "col", 1)], axis=0)
         return near, swap(near, "dp", 2)
 
-    def hidden_home(near, far, kinds, turned, *others):
-        both = jnp.concatenate([near, far], axis=0)
-        if others:
-            both = after(both, *others)
-        return settle(d, y, near, far, swap(both, "dp", 1), kinds, turned)
+    place = jnp.stack([d, y])
+
+    def over_cores(near, far):
+        return [near, swap(near, "dp", 1), far, swap(far, "dp", 1)]
 
     gain_ffn_sum = jnp.sum(grad_normed_ffn * hidden_res * scale_ffn, axis=0)
     weighted = grad_normed_ffn * gain_ffn[None, :]
@@ -1236,55 +1246,62 @@
     grad_context = low(do_own + wide(do_received))
     dq, dkv_parts = attend_back(flags, queries, grad_context, lse, cos_t, sin_t, query_seg, key_seg, key_values)
     q_even, q_far = heads_sum(dq, a1_both)
+    q_sum = wide(q_even[: q_far.shape[0]]) + wide(q_far)
     dkv_parts, gate_up_part = lax.optimization_barrier((dkv_parts, gate_up_part))
     dkv_sum = along_row(dkv_parts)
-    gate_up_received, dkv_sum = lax.optimization_barrier((swap(gate_up_part[:, width:], "col", 1), dkv_sum))
-    down_near = hidden_near(after(down_part, q_even))
+    gate_up_received, dkv_sum, q_other, *down_near = lax.optimization_barrier(
+        (
+            swap(gate_up_part[:, width:], "col", 1),
+            dkv_sum,
+            swap(low(q_sum[:, width:]), "col", 1),
+            *hidden_near(after(down_part, q_even)),
+        )
+    )
     gate_up_near = jnp.concatenate([gate_up_part[:, :width], gate_up_received], axis=0)
     dkv = low(turn_heads(wide(dkv_sum), -1.0, 2 * HEAD_SIZE))
-    gate_up_far = swap(gate_up_near, "dp", 2)
-    dkv_cores = with_core(dkv)
-    q_far = after(q_far, dkv_cores)
-    q_sum = wide(q_even[: q_far.shape[0]]) + wide(q_far)
-    dq_other = swap(dq, "col", 1)
     kv_part = 2 * HEAD_SIZE // n_dp
-    dwkv = low(dot_tn(dkv_cores, a1_both)).reshape(groups, n_dp, kv_part, features)
+    dwkv = low(dot_tn(with_core(dkv), a1_both)).reshape(groups, n_dp, kv_part, features)
     dwkv = [dwkv[:, i].reshape(groups * kv_part, features) for i in range(n_dp)]
-    kv_near, kv_far = xor_order(dwkv, d)[0], xor_order(dwkv, d ^ 2)[0]
-    q_sum = after(q_sum, kv_far)
-    kv_far, dkv_other = lax.optimization_barrier((swap(kv_far, "dp", 2), swap(dkv, "col", 1)))
-    dwkv = low(wide(kv_near) + wide(kv_far))
+    kv_far, dq_other = lax.optimization_barrier((swap(xor_order(dwkv, d ^ 2)[0], "dp", 2), swap(dq, "col", 1)))
+    dwkv = low(wide(xor_order(dwkv, d)[0]) + wide(kv_far))
+    kv_other, dkv_other = lax.optimization_barrier((swap(dwkv[:, width:], "col", 1), swap(dkv, "col", 1)))
+    kv_heads = xor_order([dwkv[:, :width], kv_other], y)
+    q_heads = xor_order([low(q_sum[:, :width]), q_other], y)
+    o_heads = xor_order(
+        [
+            low(wide(o_even[2 * i * o_part : (2 * i + 1) * o_part]) + wide(o_far[i * o_part : (i + 1) * o_part]))
+            for i in (0, 1)
+        ],
+        y,
+    )
+    o_home = along_row(after(jnp.concatenate(o_heads, axis=0), dkv_sum))
+    mixed = [
+        x[g * part : (g + 1) * part]
+        for i in range(n_col)
+        for g in range(groups)
+        for x, part in ((q_heads[i], HEAD_SIZE), (kv_heads[i], kv_part))
+    ]
+    mixed = along_row(jnp.concatenate(mixed, axis=0))
     grad_normed_attn = merge(side, dq, dq_other, q_slots) + key_value_back(
         kv_scalars, dkv, dkv_other, kv_mine, kv_theirs
     )
-
-    q_other = swap(low(q_sum[:, width:]), "col", 1)
-    grad_query = wide(heads_home(q_sum[:, :width], q_other, y, dkv_sum).T)
-    o_own, o_other = [
-        wide(o_even[2 * i * o_part : (2 * i + 1) * o_part]) + wide(o_far[i * o_part : (i + 1) * o_part]) for i in (0, 1)
-    ]
-    grad_out = wide(heads_home(o_own, o_other, y, dkv_sum))
-    pieces = []
-    for g in range(groups):
-        block = dwkv[g * kv_part : (g + 1) * kv_part]
-        pieces += xor_order([block[:, :width], block[:, width:]], y)
-    dwkv = quarters_home(pieces, r)
-    (grad_down,) = hidden_home(*down_near, 1, False, dwkv)
-    grad_gate, grad_up = hidden_home(gate_up_near, gate_up_far, 2, True, dwkv)
-    later = dwkv
-    dwkv = jnp.concatenate(xor_order(dp_slots(dwkv), d), axis=0)
-    grad_key = wide(dwkv[:HEAD_SIZE].T)
-    grad_value = wide(dwkv[HEAD_SIZE:].T)
-
     gain_attn_sum = jnp.sum(grad_normed_attn * states_f * scale_attn, axis=0)
     weighted = grad_normed_attn * gain_attn[None, :]
     inner_sum = jnp.sum(weighted * states_f, axis=1)
     inner_sum = (inner_sum + swap(inner_sum, "col", 1))[:, None]
     grad_states = grad_hidden_res + scale_attn * weighted - states_f * scale_attn**3 * inner_sum / features
 
-    sums = after(jnp.concatenate([gain_attn_sum, gain_ffn_sum, error_col]), later)
+    sums = jnp.concatenate([gain_attn_sum, gain_ffn_sum, error_col])
     for axis, mask in (("dp", 1), ("dp", 2), ("row", 1), ("row", 2)):
         sums = sums + swap(sums, axis, mask)
+    mixed, o_home, sums, grad_states, gate_up_far = lax.optimization_barrier(
+        (mixed, o_home, sums, grad_states, swap(gate_up_near, "dp", 2))
+    )
+    (grad_down,) = settle(place, over_cores(*down_near), 1, False)
+    grad_gate, grad_up = settle(place, over_cores(gate_up_near, gate_up_far), 2, True)
+    home = jnp.concatenate([mixed, o_home], axis=0)
+    home_far, grad_down, grad_gate, grad_up = lax.optimization_barrier((swap(home, "dp", 2), grad_down, grad_gate, grad_up))
+    grad_query, grad_key, grad_value, grad_out = finish(place, over_cores(home, home_far))
     return (
         low(result),
         sums[2 * width] / (count * features),

time: 807 us -> 804 us (level)
  other arithmetic: 74.8 us -> 65.5 us
    ppermute x70, waiting for transfers between devices: 290 us -> 320 us  [swap(): return lax.ppermute(values, axis, [(i, i ^ mask) for i in range(size)])]
    reduce_scatter x3 -> x5, waiting for transfers between devices: 53.8 us -> 29.4 us  [along_row(): return lax.psum_scatter(x, 'row', scatter_dimension=0, tiled=True)]
    unnamed x191 -> x184, local copies, waits for them, and re-layouts: 22.6 us -> 26.3 us
  transfers between devices with their start and end apart: 83 -> 79, of which waited for: 48 -> 48; matrix products, arithmetic and copies ran while one was open for 15% -> 13% of each run, Pallas kernels for 18% -> 19%
where the time goes in v4:
time: 804 us; the launch traced here: 795 us
  waiting for transfers between devices  375 us (47%)
  Pallas kernels  189 us (24%)
  starting transfers between devices  70.6 us (9%)
  other arithmetic  65.5 us (8%)
  local copies, waits for them, and re-layouts  55.6 us (7%)
  between operations  27.4 us (3%)
  matrix products  11.9 us (1%)
    ppermute x70, waiting for transfers between devices, swap(): return lax.ppermute(values, axis, [(i, i ^ mask) for i in range(size)])  320 us
    pallas_call x4, Pallas kernels, feed_call(): pl.pallas_call(kernel, out_shape=tuple(shapes), grid=(blocks,), in_specs=...  74.2 us
    ppermute x70, starting transfers between devices, swap(): return lax.ppermute(values, axis, [(i, i ^ mask) for i in range(size)])  69.5 us
    pallas_call x6, Pallas kernels, local_call(): pl.pallas_call(kernel, out_shape=outs, in_specs=[pl.BlockSpec(memory_spac...  37.2 us
    pallas_call x2, Pallas kernels, outer(): pl.pallas_call(functools.partial(outer_kernel, kinds, N_ROW * part), out_...  34 us
    reduce_scatter x5, waiting for transfers between devices, along_row(): return lax.psum_scatter(x, 'row', scatter_dimension=0, tiled=True)  29.4 us
    unnamed x184, local copies, waits for them, and re-layouts  26.3 us
    all_gather x4, waiting for transfers between devices, gather_rows(): return lax.all_gather(values, 'row', axis=0, tiled=True)  25.8 us
  transfers between devices with their start and end apart: 79, of which 48 were waited for; matrix products, arithmetic and copies ran while one was open for 13% of the time, Pallas kernels for 19%

profile of v4, /device:TPU:0, one launch (start us, length us, event | category | flops | bytes accessed | tf_op | source)
XLA Modules:
  0.0 795.0 jit_solution(6809799206649038391)
XLA Ops:
  27.2 12.7 %collective-permute-done.2 = bf16[128,1024]{1,0:T(8,128)(2,1)S(1)} collective-permute-done((bf16[128,1024]{1,0:T(8,128)(2,1)S(1)}, bf16[128,1024]{1,0:T(8,128)(2,1)S(1)}, u32[]{:S(2)}, u32[]{:S(2)}) %collective-permute-start.2) | collective-permute-done | bytes 262176 | tf_op jit(solution)/shard_map/ppermute | solution.py:406
  45.0 4.3 collective-permute-done
  52.2 5.5 key_value.1
  65.9 4.2 collective-permute-done.6
  79.7 23.6 %collective-permute-done.10.refs_2_ = bf16[512,1024]{1,0:T(8,128)(2,1)S(1)} collective-permute-done((bf16[512,1024]{1,0:T(8,128)(2,1)S(1)}, bf16[512,1024]{1,0:T(8,128)(2,1)S(1)}, u32[]{:S(2)}, u32[]{:S(2)}) %collective-permute-start.10) | collective-permute-done | bytes 1048608 | tf_op jit(solution)/shard_map/ppermute | solution.py:406
  107.1 6.5 project.2
  132.7 10.8 %collective-permute-done.13.refs_2_ = bf16[512,1024]{1,0:T(8,128)(2,1)S(1)} collective-permute-done((bf16[512,1024]{1,0:T(8,128)(2,1)S(1)}, bf16[512,1024]{1,0:T(8,128)(2,1)S(1)}, u32[]{:S(2)}, u32[]{:S(2)}) %collective-permute-start.13) | collective-permute-done | bytes 1048608 | tf_op jit(solution)/shard_map/ppermute | solution.py:406
  153.7 10.2 %attend.1 = (bf16[512,1024]{1,0:T(8,128)(2,1)}, f32[8,1,512]{2,1,0:T(1,128)}) custom-call(s32[8]{0:T(128)} %stack.47.flags, bf16[512,1024]{1,0:T(8,128)(2,1)} %copy-done.24, s32[1,512]{1,0:T(1,128)} %get-tuple-element.311.qseg_ref, s32[2048,1]{1,0:T(8,128)} %copy.56.kseg_ref, bf16[2048,512]{1,0:T(8,128)(2,1)} %all-gather.7.cloned.1.call-done.refs_0_.refs_1_.refs_2_.refs_3_, ...), custom_call_target="tpu_custom_call" | custom-call | flops 322122560 | bytes 838860 | tf_op jit(solution)/shard_map/attend/pallas_call | solution.py:574
  165.5 24.1 %collective-permute-done.15.other_ref = bf16[512,1024]{1,0:T(8,128)(2,1)S(1)} collective-permute-done((bf16[512,1024]{1,0:T(8,128)(2,1)}, bf16[512,1024]{1,0:T(8,128)(2,1)S(1)}, u32[]{:S(2)}, u32[]{:S(2)}) %collective-permute-start.15) | collective-permute-done | bytes 1048608 | tf_op jit(solution)/shard_map/ppermute | solution.py:406
  190.6 6.5 merge.2
  207.3 11.3 %collective-permute-done.17.refs_1_ = bf16[256,1024]{1,0:T(8,128)(2,1)S(1)} collective-permute-done((bf16[256,1024]{1,0:T(8,128)(2,1)S(1)}, bf16[256,1024]{1,0:T(8,128)(2,1)S(1)}, u32[]{:S(2)}, u32[]{:S(2)}) %collective-permute-start.17) | collective-permute-done | bytes 524320 | tf_op jit(solution)/shard_map/ppermute | solution.py:406
  218.6 22.2 %all-gather.9.cloned.1.call-done.refs_5_.refs_0_ = bf16[1408,2048]{1,0:T(8,128)(2,1)} async-done(((bf16[352,2048]{1,0:T(8,128)(2,1)}), bf16[1408,2048]{1,0:T(8,128)(2,1)}) %all-gather.9.cloned.1.call-update) | async-done | bytes 5767184 | tf_op jit(solution)/shard_map/all_gather | solution.py:67
  244.6 13.0 %collective-permute-done.18.refs_2_ = bf16[256,1024]{1,0:T(8,128)(2,1)S(1)} collective-permute-done((bf16[256,1024]{1,0:T(8,128)(2,1)}, bf16[256,1024]{1,0:T(8,128)(2,1)S(1)}, u32[]{:S(2)}, u32[]{:S(2)}) %collective-permute-start.18) | collective-permute-done | bytes 524320 | tf_op jit(solution)/shard_map/ppermute | solution.py:406
  262.6 21.2 %collective-permute-done.20.refs_4_ = bf16[256,2048]{1,0:T(8,128)(2,1)S(1)} collective-permute-done((bf16[256,2048]{1,0:T(8,128)(2,1)S(1)}, bf16[256,2048]{1,0:T(8,128)(2,1)S(1)}, u32[]{:S(2)}, u32[]{:S(2)}) %collective-permute-start.20) | collective-permute-done | bytes 1048608 | tf_op jit(solution)/shard_map/ppermute | solution.py:406
  287.7 22.5 %gate_up.1 = (f32[1024,1536]{1,0:T(8,128)}, f32[1024,1536]{1,0:T(8,128)}, bf16[1024,768]{1,0:T(8,128)(2,1)}, bf16[1024,768]{1,0:T(8,128)(2,1)}, bf16[1024,2048]{1,0:T(8,128)(2,1)}) custom-call(bf16[512,1024]{1,0:T(8,128)(2,1)} %copy-done.19, bf16[256,1024]{1,0:T(8,128)(2,1)} %copy-done.44, bf16[256,1024]{1,0:T(8,128)(2,1)} %copy-done.45, ...), custom_call_target="tpu_custom_call" | custom-call | flops 1288490240 | bytes 2097152 | tf_op jit(solution)/shard_map/gate_up/pallas_call | solution.py:879
  310.3 5.6 collective-permute-done.23.refs_1_.refs_8_
  315.9 13.6 %down.1 = (bf16[256,2048]{1,0:T(8,128)(2,1)}, bf16[256,2048]{1,0:T(8,128)(2,1)}, bf16[512,1024]{1,0:T(8,128)(2,1)}, bf16[512,1024]{1,0:T(8,128)(2,1)}) custom-call(bf16[1024,768]{1,0:T(8,128)(2,1)} %get-tuple-element.146.own_ref.left_ref, bf16[1024,768]{1,0:T(8,128)(2,1)} %get-tuple-element.129.other_ref, ...), custom_call_target="tpu_custom_call" | custom-call | flops 644245120 | bytes 2097152 | tf_op jit(solution)/shard_map/down/pallas_call | solution.py:879
  334.6 20.4 %collective-permute-done.24 = bf16[256,2048]{1,0:T(8,128)(2,1)} collective-permute-done((bf16[256,2048]{1,0:T(8,128)(2,1)}, bf16[256,2048]{1,0:T(8,128)(2,1)}, u32[]{:S(2)}, u32[]{:S(2)}) %collective-permute-start.24) | collective-permute-done | bytes 1048608 | tf_op jit(solution)/shard_map/ppermute | solution.py:406
  362.6 7.1 collective-permute-done.26
  378.8 9.4 %collective-permute-done.29.refs_2_ = bf16[256,1024]{1,0:T(8,128)(2,1)S(1)} collective-permute-done((bf16[256,1024]{1,0:T(8,128)(2,1)S(1)}, bf16[256,1024]{1,0:T(8,128)(2,1)S(1)}, u32[]{:S(2)}, u32[]{:S(2)}) %collective-permute-start.29) | collective-permute-done | bytes 524320 | tf_op jit(solution)/shard_map/ppermute | solution.py:406
  396.2 5.8 pad_maximum_fusion
  404.1 12.4 %collective-permute-done.31.refs_4_ = bf16[256,2048]{1,0:T(8,128)(2,1)S(1)} collective-permute-done((bf16[256,2048]{1,0:T(8,128)(2,1)S(1)}, bf16[256,2048]{1,0:T(8,128)(2,1)S(1)}, u32[]{:S(2)}, u32[]{:S(2)}) %collective-permute-start.31) | collective-permute-done | bytes 1048608 | tf_op jit(solution)/shard_map/ppermute | solution.py:406
  418.7 16.9 %down_back.1 = (bf16[1024,1536]{1,0:T(8,128)(2,1)}, bf16[1024,1536]{1,0:T(8,128)(2,1)}, bf16[1024,2048]{1,0:T(8,128)(2,1)}) custom-call(bf16[512,1024]{1,0:T(8,128)(2,1)} %copy-done.13, bf16[256,1024]{1,0:T(8,128)(2,1)} %copy-done.43, bf16[256,1024]{1,0:T(8,128)(2,1)} %copy-done.42, bf16[512,1024]{1,0:T(8,128)(2,1)} %copy-done.58, ...), custom_call_target="tpu_custom_call" | custom-call | flops 644245120 | bytes 2097152 | tf_op jit(solution)/shard_map/down_back/pallas_call | solution.py:879
  436.2 7.0 collective-permute-done.37.right_far_ref
  443.2 12.8 %outer.2 = bf16[704,2048]{1,0:T(8,128)(2,1)} custom-call(bf16[1024,768]{1,0:T(8,128)(2,1)} %get-tuple-element.146.own_ref.left_ref, bf16[1024,768]{1,0:T(8,128)(2,1)} %copy-done.49, bf16[1024,2048]{1,0:T(8,128)(2,1)} %get-tuple-element.148.right_ref, bf16[1024,2048]{1,0:T(8,128)(2,1)} %collective-permute-done.37.right_far_ref), custom_call_target="tpu_custom_call" | custom-call | flops 644245120 | bytes 1677721 | tf_op jit(solution)/shard_map/outer/pallas_call | solution.py:940
  456.1 21.2 %gate_up_back.1 = (bf16[256,2048]{1,0:T(8,128)(2,1)}, bf16[256,2048]{1,0:T(8,128)(2,1)}, bf16[512,1024]{1,0:T(8,128)(2,1)}, bf16[512,1024]{1,0:T(8,128)(2,1)}) custom-call(bf16[1024,1536]{1,0:T(8,128)(2,1)} %get-tuple-element.154.own_ref.left_ref, bf16[1024,1536]{1,0:T(8,128)(2,1)} %get-tuple-element.150.other_ref, ...), custom_call_target="tpu_custom_call" | custom-call | flops 1288490240 | bytes 2097152 | tf_op jit(solution)/shard_map/gate_up_back/pallas_call | solution.py:879
  479.8 21.3 %outer.3 = bf16[1408,2048]{1,0:T(8,128)(2,1)} custom-call(bf16[1024,1536]{1,0:T(8,128)(2,1)} %get-tuple-element.154.own_ref.left_ref, bf16[1024,1536]{1,0:T(8,128)(2,1)} %collective-permute-done.36.left_far_ref, bf16[1024,2048]{1,0:T(8,128)(2,1)} %get-tuple-element.156.right_ref, bf16[1024,2048]{1,0:T(8,128)(2,1)} %copy-done.26), custom_call_target="tpu_custom_call" | custom-call | flops 1288490240 | bytes 1677721 | tf_op jit(solution)/shard_map/outer/pallas_call | solution.py:940
  503.7 6.5 reduce-scatter.6.cloned.1.call-done
  516.3 9.0 %collective-permute-done.40 = bf16[256,1024]{1,0:T(8,128)(2,1)S(1)} collective-permute-done((bf16[256,1024]{1,0:T(8,128)(2,1)S(1)}, bf16[256,1024]{1,0:T(8,128)(2,1)S(1)}, u32[]{:S(2)}, u32[]{:S(2)}) %collective-permute-start.40) | collective-permute-done | bytes 524320 | tf_op jit(solution)/shard_map/ppermute | solution.py:406
  539.2 6.5 project.3
  554.3 16.3 %collective-permute-done.43 = bf16[512,1024]{1,0:T(8,128)(2,1)S(1)} collective-permute-done((bf16[512,1024]{1,0:T(8,128)(2,1)}, bf16[512,1024]{1,0:T(8,128)(2,1)S(1)}, u32[]{:S(2)}, u32[]{:S(2)}) %collective-permute-start.43) | collective-permute-done | bytes 1048608 | tf_op jit(solution)/shard_map/ppermute | solution.py:406
  570.6 5.6 collective-permute-done.45
  577.5 14.7 %attend_back.1 = (bf16[512,1024]{1,0:T(8,128)(2,1)}, bf16[2048,512]{1,0:T(8,128)(2,1)}) custom-call(s32[8]{0:T(128)} %stack.47.flags, bf16[512,1024]{1,0:T(8,128)(2,1)} %copy-done.24, bf16[512,1024]{1,0:T(8,128)(2,1)} %add_convert_fusion.1.do_ref, f32[8,1,512]{2,1,0:T(1,128)} %get-tuple-element.167.lse_ref, f32[64,512]{1,0:T(8,128)} %get-tuple-element.319.cos_ref, ...), custom_call_target="tpu_custom_call" | custom-call | flops 805306368 | bytes 1258291 | tf_op jit(solution)/shard_map/attend_back/pallas_call | solution.py:600
  592.2 22.8 %reduce-scatter.8.cloned.1.call-done = bf16[352,2048]{1,0:T(8,128)(2,1)} async-done(((bf16[1408,2048]{1,0:T(8,128)(2,1)}), bf16[352,2048]{1,0:T(8,128)(2,1)}) %reduce-scatter.8.cloned.1.call-update) | async-done | bytes 1441808 | tf_op jit(solution)/shard_map/reduce_scatter | solution.py:1208
  617.4 4.6 convolution_convert_fusion.1
  625.3 8.7 %collective-permute-done.50 = bf16[176,1024]{1,0:T(8,128)(2,1)S(1)} collective-permute-done((bf16[176,1024]{1,0:T(8,128)(2,1)S(1)}, bf16[176,1024]{1,0:T(8,128)(2,1)S(1)}, u32[]{:S(2)}, u32[]{:S(2)}) %collective-permute-start.50) | collective-permute-done | bytes 360480 | tf_op jit(solution)/shard_map/ppermute | solution.py:406
  637.1 11.1 %collective-permute-done.48 = bf16[256,2048]{1,0:T(8,128)(2,1)S(1)} collective-permute-done((bf16[256,2048]{1,0:T(8,128)(2,1)S(1)}, bf16[256,2048]{1,0:T(8,128)(2,1)S(1)}, u32[]{:S(2)}, u32[]{:S(2)}) %collective-permute-start.48) | collective-permute-done | bytes 1048608 | tf_op jit(solution)/shard_map/ppermute | solution.py:406
  650.2 13.5 %collective-permute-done.49 = bf16[256,1024]{1,0:T(8,128)(2,1)S(1)} collective-permute-done((bf16[256,1024]{1,0:T(8,128)(2,1)S(1)}, bf16[256,1024]{1,0:T(8,128)(2,1)S(1)}, u32[]{:S(2)}, u32[]{:S(2)}) %collective-permute-start.49) | collective-permute-done | bytes 524320 | tf_op jit(solution)/shard_map/ppermute | solution.py:406
  669.1 4.8 convolution_convert_fusion
  681.1 12.1 %collective-permute-done.54.other_ref = bf16[512,1024]{1,0:T(8,128)(2,1)} collective-permute-done((bf16[512,1024]{1,0:T(8,128)(2,1)S(1)}, bf16[512,1024]{1,0:T(8,128)(2,1)}, u32[]{:S(2)}, u32[]{:S(2)}) %collective-permute-start.54) | collective-permute-done | bytes 1048608 | tf_op jit(solution)/shard_map/ppermute | solution.py:406
  697.1 7.3 collective-permute-done.56.other_ref
  704.4 5.0 collective-permute-done.55
  713.7 6.5 merge.3
  720.1 5.7 key_value_back.1
  730.2 15.4 %collective-permute-done.58 = f32[2176]{0:T(1024)S(1)} collective-permute-done((f32[2176]{0:T(1024)S(1)}, f32[2176]{0:T(1024)S(1)}, u32[]{:S(2)}, u32[]{:S(2)}) %collective-permute-start.58) | collective-permute-done | bytes 8736 | tf_op jit(solution)/shard_map/ppermute | solution.py:406
  763.5 5.0 settle.2
  769.8 8.1 %settle.3 = (f32[1024,1408]{1,0:T(8,128)}, f32[1024,1408]{1,0:T(8,128)}) custom-call(s32[2]{0:T(128)} %pad_add_fusion.3.scalars, bf16[704,1024]{1,0:T(8,128)(2,1)} %copy-done.22, bf16[704,1024]{1,0:T(8,128)(2,1)} %collective-permute-done.67.refs_1_, bf16[704,1024]{1,0:T(8,128)(2,1)} %collective-permute-done.62.refs_2_, bf16[704,1024]{1,0:T(8,128)(2,1)} %copy-done.52), custom_call_target="tpu_custom_call" | custom-call | flops 144179 | bytes 1730150 | tf_op jit(solution)/shard_map/settle/pallas_call | solution.py:974
  781.7 5.2 finish.1
  (445 shorter events, 221.1 us)
Async XLA Ops:
  7.2 66.4 %all-gather.5.cloned.1.call-start = ((), (), s32[]{:S(2)}) async-start(), calls=%async_computation.5 | async-start | bytes 2621440 | tf_op jit(solution)/shard_map/all_gather | solution.py:67
  10.4 134.7 %all-gather.7.cloned.1.call-start = ((), (), s32[]{:S(2)}) async-start(), calls=%async_computation.6 | async-start | bytes 2621440 | tf_op jit(solution)/shard_map/all_gather | solution.py:67
  10.9 16.3 %collective-permute-start.1 = (bf16[128,1024]{1,0:T(8,128)(2,1)S(1)}, bf16[128,1024]{1,0:T(8,128)(2,1)S(1)}, u32[]{:S(2)}, u32[]{:S(2)}) collective-permute-start(bf16[128,1024]{1,0:T(8,128)(2,1)S(1)} %select_bitcast_fusion), channel_id=1, source_target_pairs={{0,2},{2,0},{4,6},{6,4},{1,3},{3,1},{5,7},{7,5},{8,10},{10,8},{12,... | collective-permute-start | bytes 786440 | tf_op jit(solution)/shard_map/ppermute | solution.py:406
  13.9 26.0 %collective-permute-start.2 = (bf16[128,1024]{1,0:T(8,128)(2,1)S(1)}, bf16[128,1024]{1,0:T(8,128)(2,1)S(1)}, u32[]{:S(2)}, u32[]{:S(2)}) collective-permute-start(bf16[128,1024]{1,0:T(8,128)(2,1)S(1)} %select_bitcast_fusion), channel_id=1, source_target_pairs={{0,4},{2,6},{4,0},{6,2},{1,5},{3,7},{5,1},{7,3},{8,12},{10,14},{12... | collective-permute-start | bytes 786440 | tf_op jit(solution)/shard_map/ppermute | solution.py:406
  16.5 26.4 %collective-permute-start.3 = (bf16[128,1024]{1,0:T(8,128)(2,1)S(1)}, bf16[128,1024]{1,0:T(8,128)(2,1)S(1)}, u32[]{:S(2)}, u32[]{:S(2)}) collective-permute-start(bf16[128,1024]{1,0:T(8,128)(2,1)S(1)} %select_bitcast_fusion), channel_id=1, source_target_pairs={{0,6},{2,4},{4,2},{6,0},{1,7},{3,5},{5,3},{7,1},{8,14},{10,12},{12... | collective-permute-start | bytes 786440 | tf_op jit(solution)/shard_map/ppermute | solution.py:406
  24.0 27.2 %collective-permute-start.5 = (bf16[528,1024]{1,0:T(8,128)(2,1)}, bf16[528,1024]{1,0:T(8,128)(2,1)}, u32[]{:S(2)}, u32[]{:S(2)}) collective-permute-start(bf16[528,1024]{1,0:T(8,128)(2,1)} %pad_maximum_fusion.7), channel_id=1, source_target_pairs={{0,1},{1,0},{2,3},{3,2},{4,5},{5,4},{6,7},{7,6},{8,9},{9,8},{10,11... | collective-permute-start | bytes 3244040 | tf_op jit(solution)/shard_map/ppermute | solution.py:406
  26.0 23.3 %collective-permute-start = (f32[512]{0:T(512)S(1)}, f32[512]{0:T(512)S(1)}, u32[]{:S(2)}, u32[]{:S(2)}) collective-permute-start(f32[512]{0:T(512)S(1)} %fusion.1), channel_id=1, source_target_pairs={{0,1},{1,0},{2,3},{3,2},{4,5},{5,4},{6,7},{7,6},{8,9},{9,8},{10,11... | collective-permute-start | bytes 6152 | tf_op jit(solution)/shard_map/ppermute | solution.py:406
  44.0 16.4 %collective-permute-start.7 = (f32[1]{0:T(128)}, f32[1]{0:T(128)}, u32[]{:S(2)}, u32[]{:S(2)}) collective-permute-start(f32[1]{0:T(128)} %bitcast.18), channel_id=1, source_target_pairs={{0,8},{8,0},{16,24},{24,16},{1,9},{9,1},{17,25},{25,17},{2,10},{10... | collective-permute-start | bytes 20 | tf_op jit(solution)/shard_map/ppermute | solution.py:406
  76.6 164.2 %all-gather.9.cloned.1.call-start = ((), (), s32[]{:S(2)}) async-start(), calls=%async_computation.7 | async-start | bytes 7208960 | tf_op jit(solution)/shard_map/all_gather | solution.py:67
  78.1 25.2 %collective-permute-start.10 = (bf16[512,1024]{1,0:T(8,128)(2,1)S(1)}, bf16[512,1024]{1,0:T(8,128)(2,1)S(1)}, u32[]{:S(2)}, u32[]{:S(2)}) collective-permute-start(bf16[512,1024]{1,0:T(8,128)(2,1)S(1)} %pad_maximum_fusion.10.refs_0_), channel_id=1, source_target_pairs={{0,16},{8,24},{16,0},{24,8},{1,17},{9,25},{17,1},{25,9},{2,18},{10... | collective-permute-start | bytes 3145736 | tf_op jit(solution)/shard_map/ppermute | solution.py:406
  79.7 27.4 %collective-permute-start.9 = (bf16[512,1024]{1,0:T(8,128)(2,1)S(1)}, bf16[512,1024]{1,0:T(8,128)(2,1)}, u32[]{:S(2)}, u32[]{:S(2)}) collective-permute-start(bf16[512,1024]{1,0:T(8,128)(2,1)S(1)} %pad_maximum_fusion.10.refs_0_), channel_id=1, source_target_pairs={{0,8},{8,0},{16,24},{24,16},{1,9},{9,1},{17,25},{25,17},{2,10},{10... | collective-permute-start | bytes 3145736 | tf_op jit(solution)/shard_map/ppermute | solution.py:406
  117.6 192.6 %all-gather.11.cloned.1.call-start = ((), (), s32[]{:S(2)}) async-start(), calls=%async_computation.8 | async-start | bytes 3604480 | tf_op jit(solution)/shard_map/all_gather | solution.py:67
  118.2 25.3 %collective-permute-start.13 = (bf16[512,1024]{1,0:T(8,128)(2,1)S(1)}, bf16[512,1024]{1,0:T(8,128)(2,1)S(1)}, u32[]{:S(2)}, u32[]{:S(2)}) collective-permute-start(bf16[512,1024]{1,0:T(8,128)(2,1)S(1)} %pad_maximum_fusion.11.refs_0_), channel_id=1, source_target_pairs={{0,16},{8,24},{16,0},{24,8},{1,17},{9,25},{17,1},{25,9},{2,18},{10... | collective-permute-start | bytes 3145736 | tf_op jit(solution)/shard_map/ppermute | solution.py:406
  119.7 25.4 %collective-permute-start.12 = (bf16[512,1024]{1,0:T(8,128)(2,1)}, bf16[512,1024]{1,0:T(8,128)(2,1)}, u32[]{:S(2)}, u32[]{:S(2)}) collective-permute-start(bf16[512,1024]{1,0:T(8,128)(2,1)} %get-tuple-element.112), channel_id=1, source_target_pairs={{0,1},{1,0},{2,3},{3,2},{4,5},{5,4},{6,7},{7,6},{8,9},{9,8},{10,11... | collective-permute-start | bytes 3145736 | tf_op jit(solution)/shard_map/ppermute | solution.py:406
  163.9 25.7 %collective-permute-start.15 = (bf16[512,1024]{1,0:T(8,128)(2,1)}, bf16[512,1024]{1,0:T(8,128)(2,1)S(1)}, u32[]{:S(2)}, u32[]{:S(2)}) collective-permute-start(bf16[512,1024]{1,0:T(8,128)(2,1)} %get-tuple-element.119.own_ref), channel_id=1, source_target_pairs={{0,1},{1,0},{2,3},{3,2},{4,5},{5,4},{6,7},{7,6},{8,9},{9,8},{10,11... | collective-permute-start | bytes 3145736 | tf_op jit(solution)/shard_map/ppermute | solution.py:406
  240.8 45.9 %collective-permute-start.21 = (bf16[1408,2048]{1,0:T(8,128)(2,1)}, bf16[1408,2048]{1,0:T(8,128)(2,1)}, u32[]{:S(2)}, u32[]{:S(2)}) collective-permute-start(bf16[1408,2048]{1,0:T(8,128)(2,1)} %all-gather.9.cloned.1.call-done.refs_5_.refs_0_), channel_id=1, source_target_pairs={{0,8},{8,0},{16,24},{24,16},{1,9},{9,1},{17,25},{25,17},{2,10},{10... | collective-permute-start | bytes 17301512 | tf_op jit(solution)/shard_map/ppermute | solution.py:406
  242.9 267.2 %reduce-scatter.6.cloned.1.call-start = ((), (), s32[]{:S(2)}) async-start(), calls=%async_computation.9 | async-start | bytes 3604480 | tf_op jit(solution)/shard_map/reduce_scatter | solution.py:1208
  258.9 24.9 %collective-permute-start.20 = (bf16[256,2048]{1,0:T(8,128)(2,1)S(1)}, bf16[256,2048]{1,0:T(8,128)(2,1)S(1)}, u32[]{:S(2)}, u32[]{:S(2)}) collective-permute-start(bf16[256,2048]{1,0:T(8,128)(2,1)S(1)} %pad_maximum_fusion.13), channel_id=1, source_target_pairs={{0,16},{8,24},{16,0},{24,8},{1,17},{9,25},{17,1},{25,9},{2,18},{10... | collective-permute-start | bytes 3145736 | tf_op jit(solution)/shard_map/ppermute | solution.py:406
  260.5 26.2 %collective-permute-start.19 = (bf16[512,1024]{1,0:T(8,128)(2,1)S(1)}, bf16[512,1024]{1,0:T(8,128)(2,1)S(1)}, u32[]{:S(2)}, u32[]{:S(2)}) collective-permute-start(bf16[512,1024]{1,0:T(8,128)(2,1)S(1)} %pad_maximum_fusion.12), channel_id=1, source_target_pairs={{0,1},{1,0},{2,3},{3,2},{4,5},{5,4},{6,7},{7,6},{8,9},{9,8},{10,11... | collective-permute-start | bytes 3145736 | tf_op jit(solution)/shard_map/ppermute | solution.py:406
  262.1 48.1 %collective-permute-start.22 = (bf16[512,1024]{1,0:T(8,128)(2,1)S(1)}, bf16[512,1024]{1,0:T(8,128)(2,1)}, u32[]{:S(2)}, u32[]{:S(2)}) collective-permute-start(bf16[512,1024]{1,0:T(8,128)(2,1)S(1)} %copy-done.5), channel_id=1, source_target_pairs={{0,1},{1,0},{2,3},{3,2},{4,5},{5,4},{6,7},{7,6},{8,9},{9,8},{10,11... | collective-permute-start | bytes 3145736 | tf_op jit(solution)/shard_map/ppermute | solution.py:406
  329.5 25.6 %collective-permute-start.24 = (bf16[256,2048]{1,0:T(8,128)(2,1)}, bf16[256,2048]{1,0:T(8,128)(2,1)}, u32[]{:S(2)}, u32[]{:S(2)}) collective-permute-start(bf16[256,2048]{1,0:T(8,128)(2,1)} %get-tuple-element.133), channel_id=1, source_target_pairs={{0,16},{8,24},{16,0},{24,8},{1,17},{9,25},{17,1},{25,9},{2,18},{10... | collective-permute-start | bytes 3145736 | tf_op jit(solution)/shard_map/ppermute | solution.py:406
  330.1 25.2 %collective-permute-start.25 = (bf16[512,1024]{1,0:T(8,128)(2,1)}, bf16[512,1024]{1,0:T(8,128)(2,1)}, u32[]{:S(2)}, u32[]{:S(2)}) collective-permute-start(bf16[512,1024]{1,0:T(8,128)(2,1)} %get-tuple-element.134), channel_id=1, source_target_pairs={{0,1},{1,0},{2,3},{3,2},{4,5},{5,4},{6,7},{7,6},{8,9},{9,8},{10,11... | collective-permute-start | bytes 3145736 | tf_op jit(solution)/shard_map/ppermute | solution.py:406
  334.6 67.4 %collective-permute-start.35 = (bf16[1024,2048]{1,0:T(8,128)(2,1)S(1)}, bf16[1024,2048]{1,0:T(8,128)(2,1)S(1)}, u32[]{:S(2)}, u32[]{:S(2)}) collective-permute-start(bf16[1024,2048]{1,0:T(8,128)(2,1)S(1)} %copy-done.25), channel_id=1, source_target_pairs={{0,8},{8,0},{16,24},{24,16},{1,9},{9,1},{17,25},{25,17},{2,10},{10... | collective-permute-start | bytes 12582920 | tf_op jit(solution)/shard_map/ppermute | solution.py:406
  362.5 33.7 %collective-permute-start.32 = (bf16[512,2048]{1,0:T(8,128)(2,1)S(1)}, bf16[512,2048]{1,0:T(8,128)(2,1)S(1)}, u32[]{:S(2)}, u32[]{:S(2)}) collective-permute-start(bf16[512,2048]{1,0:T(8,128)(2,1)S(1)} %pad_maximum_fusion.2), channel_id=1, source_target_pairs={{0,8},{8,0},{16,24},{24,16},{1,9},{9,1},{17,25},{25,17},{2,10},{10... | collective-permute-start | bytes 6291464 | tf_op jit(solution)/shard_map/ppermute | solution.py:406
  377.4 15.8 %collective-permute-start.33 = (bf16[512,1024]{1,0:T(8,128)(2,1)S(1)}, bf16[512,1024]{1,0:T(8,128)(2,1)S(1)}, u32[]{:S(2)}, u32[]{:S(2)}) collective-permute-start(bf16[512,1024]{1,0:T(8,128)(2,1)S(1)} %pad_maximum_fusion.16), channel_id=1, source_target_pairs={{0,8},{8,0},{16,24},{24,16},{1,9},{9,1},{17,25},{25,17},{2,10},{10... | collective-permute-start | bytes 3145736 | tf_op jit(solution)/shard_map/ppermute | solution.py:406
  391.7 24.8 %collective-permute-start.31 = (bf16[256,2048]{1,0:T(8,128)(2,1)S(1)}, bf16[256,2048]{1,0:T(8,128)(2,1)S(1)}, u32[]{:S(2)}, u32[]{:S(2)}) collective-permute-start(bf16[256,2048]{1,0:T(8,128)(2,1)S(1)} %pad_maximum_fusion.15), channel_id=1, source_target_pairs={{0,16},{8,24},{16,0},{24,8},{1,17},{9,25},{17,1},{25,9},{2,18},{10... | collective-permute-start | bytes 3145736 | tf_op jit(solution)/shard_map/ppermute | solution.py:406
  393.2 24.6 %collective-permute-start.30 = (bf16[512,1024]{1,0:T(8,128)(2,1)S(1)}, bf16[512,1024]{1,0:T(8,128)(2,1)S(1)}, u32[]{:S(2)}, u32[]{:S(2)}) collective-permute-start(bf16[512,1024]{1,0:T(8,128)(2,1)S(1)} %pad_maximum_fusion.14), channel_id=1, source_target_pairs={{0,1},{1,0},{2,3},{3,2},{4,5},{5,4},{6,7},{7,6},{8,9},{9,8},{10,11... | collective-permute-start | bytes 3145736 | tf_op jit(solution)/shard_map/ppermute | solution.py:406
  435.7 20.3 %collective-permute-start.36 = (bf16[1024,1536]{1,0:T(8,128)(2,1)}, bf16[1024,1536]{1,0:T(8,128)(2,1)}, u32[]{:S(2)}, u32[]{:S(2)}) collective-permute-start(bf16[1024,1536]{1,0:T(8,128)(2,1)} %get-tuple-element.150.other_ref), channel_id=1, source_target_pairs={{0,8},{8,0},{16,24},{24,16},{1,9},{9,1},{17,25},{25,17},{2,10},{10... | collective-permute-start | bytes 9437192 | tf_op jit(solution)/shard_map/ppermute | solution.py:406
  456.0 159.0 %reduce-scatter.8.cloned.1.call-start = ((), (), s32[]{:S(2)}) async-start(), calls=%async_computation.10 | async-start | bytes 7208960 | tf_op jit(solution)/shard_map/reduce_scatter | solution.py:1208
  477.3 25.6 %collective-permute-start.38 = (bf16[256,2048]{1,0:T(8,128)(2,1)}, bf16[256,2048]{1,0:T(8,128)(2,1)}, u32[]{:S(2)}, u32[]{:S(2)}) collective-permute-start(bf16[256,2048]{1,0:T(8,128)(2,1)} %get-tuple-element.152), channel_id=1, source_target_pairs={{0,16},{8,24},{16,0},{24,8},{1,17},{9,25},{17,1},{25,9},{2,18},{10... | collective-permute-start | bytes 3145736 | tf_op jit(solution)/shard_map/ppermute | solution.py:406
  478.4 25.2 %collective-permute-start.39 = (bf16[512,1024]{1,0:T(8,128)(2,1)}, bf16[512,1024]{1,0:T(8,128)(2,1)}, u32[]{:S(2)}, u32[]{:S(2)}) collective-permute-start(bf16[512,1024]{1,0:T(8,128)(2,1)} %get-tuple-element.153), channel_id=1, source_target_pairs={{0,1},{1,0},{2,3},{3,2},{4,5},{5,4},{6,7},{7,6},{8,9},{9,8},{10,11... | collective-permute-start | bytes 3145736 | tf_op jit(solution)/shard_map/ppermute | solution.py:406
  510.2 154.6 %reduce-scatter.10.cloned.1.call-start = ((), (), s32[]{:S(2)}) async-start(), calls=%async_computation.11 | async-start | bytes 2621440 | tf_op jit(solution)/shard_map/reduce_scatter | solution.py:1208
  545.8 24.8 %collective-permute-start.43 = (bf16[512,1024]{1,0:T(8,128)(2,1)}, bf16[512,1024]{1,0:T(8,128)(2,1)S(1)}, u32[]{:S(2)}, u32[]{:S(2)}) collective-permute-start(bf16[512,1024]{1,0:T(8,128)(2,1)} %get-tuple-element.162), channel_id=1, source_target_pairs={{0,1},{1,0},{2,3},{3,2},{4,5},{5,4},{6,7},{7,6},{8,9},{9,8},{10,11... | collective-permute-start | bytes 3145736 | tf_op jit(solution)/shard_map/ppermute | solution.py:406
  551.6 24.6 %collective-permute-start.45 = (bf16[512,1024]{1,0:T(8,128)(2,1)S(1)}, bf16[512,1024]{1,0:T(8,128)(2,1)}, u32[]{:S(2)}, u32[]{:S(2)}) collective-permute-start(bf16[512,1024]{1,0:T(8,128)(2,1)S(1)} %pad_maximum_fusion.17), channel_id=1, source_target_pairs={{0,16},{8,24},{16,0},{24,8},{1,17},{9,25},{17,1},{25,9},{2,18},{10... | collective-permute-start | bytes 3145736 | tf_op jit(solution)/shard_map/ppermute | solution.py:406
  615.1 140.4 %reduce-scatter.14.cloned.1.call-start = ((), (), s32[]{:S(2)}) async-start(), calls=%async_computation.13 | async-start | bytes 1310720 | tf_op jit(solution)/shard_map/reduce_scatter | solution.py:1208
  622.1 26.1 %collective-permute-start.48 = (bf16[256,2048]{1,0:T(8,128)(2,1)S(1)}, bf16[256,2048]{1,0:T(8,128)(2,1)S(1)}, u32[]{:S(2)}, u32[]{:S(2)}) collective-permute-start(bf16[256,2048]{1,0:T(8,128)(2,1)S(1)} %slice.519), channel_id=1, source_target_pairs={{0,16},{8,24},{16,0},{24,8},{1,17},{9,25},{17,1},{25,9},{2,18},{10... | collective-permute-start | bytes 3145736 | tf_op jit(solution)/shard_map/ppermute | solution.py:406
  634.0 29.7 %collective-permute-start.51 = (bf16[352,1024]{1,0:T(8,128)(2,1)S(1)}, bf16[352,1024]{1,0:T(8,128)(2,1)S(1)}, u32[]{:S(2)}, u32[]{:S(2)}) collective-permute-start(bf16[352,1024]{1,0:T(8,128)(2,1)S(1)} %pad_maximum_fusion.19.refs_0_), channel_id=1, source_target_pairs={{0,16},{8,24},{16,0},{24,8},{1,17},{9,25},{17,1},{25,9},{2,18},{10... | collective-permute-start | bytes 2162696 | tf_op jit(solution)/shard_map/ppermute | solution.py:406
  635.6 29.0 %collective-permute-start.46 = (bf16[352,1024]{1,0:T(8,128)(2,1)S(1)}, bf16[352,1024]{1,0:T(8,128)(2,1)}, u32[]{:S(2)}, u32[]{:S(2)}) collective-permute-start(bf16[352,1024]{1,0:T(8,128)(2,1)S(1)} %get-tuple-element.279), channel_id=1, source_target_pairs={{0,1},{1,0},{2,3},{3,2},{4,5},{5,4},{6,7},{7,6},{8,9},{9,8},{10,11... | collective-permute-start | bytes 2162696 | tf_op jit(solution)/shard_map/ppermute | solution.py:406
  648.7 15.1 %collective-permute-start.49 = (bf16[256,1024]{1,0:T(8,128)(2,1)S(1)}, bf16[256,1024]{1,0:T(8,128)(2,1)S(1)}, u32[]{:S(2)}, u32[]{:S(2)}) collective-permute-start(bf16[256,1024]{1,0:T(8,128)(2,1)S(1)} %slice.520), channel_id=1, source_target_pairs={{0,1},{1,0},{2,3},{3,2},{4,5},{5,4},{6,7},{7,6},{8,9},{9,8},{10,11... | collective-permute-start | bytes 1572872 | tf_op jit(solution)/shard_map/ppermute | solution.py:406
  667.1 26.1 %collective-permute-start.54 = (bf16[512,1024]{1,0:T(8,128)(2,1)S(1)}, bf16[512,1024]{1,0:T(8,128)(2,1)}, u32[]{:S(2)}, u32[]{:S(2)}) collective-permute-start(bf16[512,1024]{1,0:T(8,128)(2,1)S(1)} %copy-done.27), channel_id=1, source_target_pairs={{0,1},{1,0},{2,3},{3,2},{4,5},{5,4},{6,7},{7,6},{8,9},{9,8},{10,11... | collective-permute-start | bytes 3145736 | tf_op jit(solution)/shard_map/ppermute | solution.py:406
  674.8 18.4 %collective-permute-start.53 = (bf16[128,2048]{1,0:T(8,128)(2,1)}, bf16[128,2048]{1,0:T(8,128)(2,1)}, u32[]{:S(2)}, u32[]{:S(2)}) collective-permute-start(bf16[128,2048]{1,0:T(8,128)(2,1)} %bitcast.31), channel_id=1, source_target_pairs={{0,16},{8,24},{16,0},{24,8},{1,17},{9,25},{17,1},{25,9},{2,18},{10... | collective-permute-start | bytes 1572872 | tf_op jit(solution)/shard_map/ppermute | solution.py:406
  679.3 25.1 %collective-permute-start.56 = (bf16[512,512]{1,0:T(8,128)(2,1)}, bf16[512,512]{1,0:T(8,128)(2,1)}, u32[]{:S(2)}, u32[]{:S(2)}) collective-permute-start(bf16[512,512]{1,0:T(8,128)(2,1)} %copy-done.48), channel_id=1, source_target_pairs={{0,1},{1,0},{2,3},{3,2},{4,5},{5,4},{6,7},{7,6},{8,9},{9,8},{10,11... | collective-permute-start | bytes 1572872 | tf_op jit(solution)/shard_map/ppermute | solution.py:406
  680.8 74.7 %reduce-scatter.12.cloned.1.call-start = ((), (), s32[]{:S(2)}) async-start(), calls=%async_computation.12 | async-start | bytes 1966080 | tf_op jit(solution)/shard_map/reduce_scatter | solution.py:1208
  694.4 15.1 %collective-permute-start.55 = (bf16[128,1024]{1,0:T(8,128)(2,1)S(1)}, bf16[128,1024]{1,0:T(8,128)(2,1)S(1)}, u32[]{:S(2)}, u32[]{:S(2)}) collective-permute-start(bf16[128,1024]{1,0:T(8,128)(2,1)S(1)} %slice.533), channel_id=1, source_target_pairs={{0,1},{1,0},{2,3},{3,2},{4,5},{5,4},{6,7},{7,6},{8,9},{9,8},{10,11... | collective-permute-start | bytes 786440 | tf_op jit(solution)/shard_map/ppermute | solution.py:406
  712.1 43.3 %collective-permute-start.62 = (bf16[704,1024]{1,0:T(8,128)(2,1)S(1)}, bf16[704,1024]{1,0:T(8,128)(2,1)}, u32[]{:S(2)}, u32[]{:S(2)}) collective-permute-start(bf16[704,1024]{1,0:T(8,128)(2,1)S(1)} %pad_maximum_fusion.6.refs_0_), channel_id=1, source_target_pairs={{0,16},{8,24},{16,0},{24,8},{1,17},{9,25},{17,1},{25,9},{2,18},{10... | collective-permute-start | bytes 4325384 | tf_op jit(solution)/shard_map/ppermute | solution.py:406
  729.6 15.9 %collective-permute-start.58 = (f32[2176]{0:T(1024)S(1)}, f32[2176]{0:T(1024)S(1)}, u32[]{:S(2)}, u32[]{:S(2)}) collective-permute-start(f32[2176]{0:T(1024)S(1)} %fusion.64), channel_id=1, source_target_pairs={{0,16},{8,24},{16,0},{24,8},{1,17},{9,25},{17,1},{25,9},{2,18},{10... | collective-permute-start | bytes 26120 | tf_op jit(solution)/shard_map/ppermute | solution.py:406
  748.5 20.1 %collective-permute-start.67 = (bf16[704,1024]{1,0:T(8,128)(2,1)S(1)}, bf16[704,1024]{1,0:T(8,128)(2,1)}, u32[]{:S(2)}, u32[]{:S(2)}) collective-permute-start(bf16[704,1024]{1,0:T(8,128)(2,1)S(1)} %pad_maximum_fusion.6.refs_0_), channel_id=1, source_target_pairs={{0,8},{8,0},{16,24},{24,16},{1,9},{9,1},{17,25},{25,17},{2,10},{10... | collective-permute-start | bytes 4325384 | tf_op jit(solution)/shard_map/ppermute | solution.py:406
  759.6 18.2 %collective-permute-start.64 = (bf16[320,1024]{1,0:T(8,128)(2,1)}, bf16[320,1024]{1,0:T(8,128)(2,1)}, u32[]{:S(2)}, u32[]{:S(2)}) collective-permute-start(bf16[320,1024]{1,0:T(8,128)(2,1)} %constant_dynamic-update-slice_fusion.2.refs_0_), channel_id=1, source_target_pairs={{0,16},{8,24},{16,0},{24,8},{1,17},{9,25},{17,1},{25,9},{2,18},{10... | collective-permute-start | bytes 1966088 | tf_op jit(solution)/shard_map/ppermute | solution.py:406
  (115 other events, 1014.7 us)
Sparse Core Ops, SparseCore 0:
  10.6 62.9 all-gather.4
  76.8 56.4 all-gather.6
  135.4 105.4 all-gather.8
  243.1 57.5 all-gather.10
  456.1 53.9 reduce-scatter.5
  512.9 102.0 reduce-scatter.7
  617.9 44.3 reduce-scatter.9
  680.9 26.2 reduce-scatter.13
  711.0 35.8 reduce-scatter.11

commit v5 on v4

--- a/solution.py
+++ b/solution.py
@@ -1281,7 +1281,7 @@
         for g in range(groups)
         for x, part in ((q_heads[i], HEAD_SIZE), (kv_heads[i], kv_part))
     ]
-    mixed = along_row(jnp.concatenate(mixed, axis=0))
+    mixed = along_row(after(jnp.concatenate(mixed, axis=0), o_home))
     grad_normed_attn = merge(side, dq, dq_other, q_slots) + key_value_back(
         kv_scalars, dkv, dkv_other, kv_mine, kv_theirs
     )
@@ -1294,13 +1294,13 @@
     sums = jnp.concatenate([gain_attn_sum, gain_ffn_sum, error_col])
     for axis, mask in (("dp", 1), ("dp", 2), ("row", 1), ("row", 2)):
         sums = sums + swap(sums, axis, mask)
-    mixed, o_home, sums, grad_states, gate_up_far = lax.optimization_barrier(
-        (mixed, o_home, sums, grad_states, swap(gate_up_near, "dp", 2))
-    )
+    gate_up_far = swap(gate_up_near, "dp", 2)
     (grad_down,) = settle(place, over_cores(*down_near), 1, False)
     grad_gate, grad_up = settle(place, over_cores(gate_up_near, gate_up_far), 2, True)
     home = jnp.concatenate([mixed, o_home], axis=0)
-    home_far, grad_down, grad_gate, grad_up = lax.optimization_barrier((swap(home, "dp", 2), grad_down, grad_gate, grad_up))
+    home_far, grad_down, grad_gate, grad_up, sums = lax.optimization_barrier(
+        (swap(home, "dp", 2), grad_down, grad_gate, grad_up, sums)
+    )
     grad_query, grad_key, grad_value, grad_out = finish(place, over_cores(home, home_far))
     return (
         low(result),

time: 804 us -> 807 us (level)
    unnamed x184 -> x174, local copies, waits for them, and re-layouts: 26.3 us -> 23 us
  transfers between devices with their start and end apart: 79 -> 79, of which waited for: 48 -> 46; matrix products, arithmetic and copies ran while one was open for 13% -> 13% of each run, Pallas kernels for 19% -> 19%
where the time goes in v5:
time: 807 us; the launch traced here: 798 us
  waiting for transfers between devices  379 us (47%)
  Pallas kernels  189 us (23%)
  starting transfers between devices  71.8 us (9%)
  other arithmetic  67.6 us (8%)
  local copies, waits for them, and re-layouts  52.2 us (6%)
  between operations  27.2 us (3%)
  matrix products  11.8 us (1%)
    ppermute x70, waiting for transfers between devices, swap(): return lax.ppermute(values, axis, [(i, i ^ mask) for i in range(size)])  324 us
    pallas_call x4, Pallas kernels, feed_call(): pl.pallas_call(kernel, out_shape=tuple(shapes), grid=(blocks,), in_specs=...  74.2 us
    ppermute x70, starting transfers between devices, swap(): return lax.ppermute(values, axis, [(i, i ^ mask) for i in range(size)])  70.8 us
    pallas_call x6, Pallas kernels, local_call(): pl.pallas_call(kernel, out_shape=outs, in_specs=[pl.BlockSpec(memory_spac...  37.2 us
    pallas_call x2, Pallas kernels, outer(): pl.pallas_call(functools.partial(outer_kernel, kinds, N_ROW * part), out_...  34 us
    reduce_scatter x5, waiting for transfers between devices, along_row(): return lax.psum_scatter(x, 'row', scatter_dimension=0, tiled=True)  29.2 us
    all_gather x4, waiting for transfers between devices, gather_rows(): return lax.all_gather(values, 'row', axis=0, tiled=True)  25.8 us
    unnamed x174, local copies, waits for them, and re-layouts  23 us
  transfers between devices with their start and end apart: 79, of which 46 were waited for; matrix products, arithmetic and copies ran while one was open for 13% of the time, Pallas kernels for 19%

profile of v5, /device:TPU:0, one launch (start us, length us, event | category | flops | bytes accessed | tf_op | source)
XLA Modules:
  0.0 798.0 jit_solution(5301773181060611142)
XLA Ops:
  27.2 12.7 %collective-permute-done.2 = bf16[128,1024]{1,0:T(8,128)(2,1)S(1)} collective-permute-done((bf16[128,1024]{1,0:T(8,128)(2,1)S(1)}, bf16[128,1024]{1,0:T(8,128)(2,1)S(1)}, u32[]{:S(2)}, u32[]{:S(2)}) %collective-permute-start.2) | collective-permute-done | bytes 262176 | tf_op jit(solution)/shard_map/ppermute | solution.py:406
  45.0 4.3 collective-permute-done
  52.2 5.5 key_value.1
  79.7 23.6 %collective-permute-done.10.refs_2_ = bf16[512,1024]{1,0:T(8,128)(2,1)S(1)} collective-permute-done((bf16[512,1024]{1,0:T(8,128)(2,1)S(1)}, bf16[512,1024]{1,0:T(8,128)(2,1)S(1)}, u32[]{:S(2)}, u32[]{:S(2)}) %collective-permute-start.10) | collective-permute-done | bytes 1048608 | tf_op jit(solution)/shard_map/ppermute | solution.py:406
  107.1 6.5 project.2
  132.6 10.9 %collective-permute-done.13.refs_2_ = bf16[512,1024]{1,0:T(8,128)(2,1)S(1)} collective-permute-done((bf16[512,1024]{1,0:T(8,128)(2,1)S(1)}, bf16[512,1024]{1,0:T(8,128)(2,1)S(1)}, u32[]{:S(2)}, u32[]{:S(2)}) %collective-permute-start.13) | collective-permute-done | bytes 1048608 | tf_op jit(solution)/shard_map/ppermute | solution.py:406
  153.7 10.2 %attend.1 = (bf16[512,1024]{1,0:T(8,128)(2,1)}, f32[8,1,512]{2,1,0:T(1,128)}) custom-call(s32[8]{0:T(128)} %stack.47.flags, bf16[512,1024]{1,0:T(8,128)(2,1)} %copy-done.23, s32[1,512]{1,0:T(1,128)} %get-tuple-element.305.qseg_ref, s32[2048,1]{1,0:T(8,128)} %copy.56.kseg_ref, bf16[2048,512]{1,0:T(8,128)(2,1)} %all-gather.7.cloned.1.call-done.refs_0_.refs_1_.refs_2_.refs_3_, ...), custom_call_target="tpu_custom_call" | custom-call | flops 322122560 | bytes 838860 | tf_op jit(solution)/shard_map/attend/pallas_call | solution.py:574
  165.5 24.1 %collective-permute-done.15.other_ref = bf16[512,1024]{1,0:T(8,128)(2,1)S(1)} collective-permute-done((bf16[512,1024]{1,0:T(8,128)(2,1)}, bf16[512,1024]{1,0:T(8,128)(2,1)S(1)}, u32[]{:S(2)}, u32[]{:S(2)}) %collective-permute-start.15) | collective-permute-done | bytes 1048608 | tf_op jit(solution)/shard_map/ppermute | solution.py:406
  190.6 6.5 merge.2
  207.3 11.3 %collective-permute-done.17.refs_1_ = bf16[256,1024]{1,0:T(8,128)(2,1)S(1)} collective-permute-done((bf16[256,1024]{1,0:T(8,128)(2,1)S(1)}, bf16[256,1024]{1,0:T(8,128)(2,1)S(1)}, u32[]{:S(2)}, u32[]{:S(2)}) %collective-permute-start.17) | collective-permute-done | bytes 524320 | tf_op jit(solution)/shard_map/ppermute | solution.py:406
  218.6 22.2 %all-gather.9.cloned.1.call-done.refs_5_.refs_0_ = bf16[1408,2048]{1,0:T(8,128)(2,1)} async-done(((bf16[352,2048]{1,0:T(8,128)(2,1)}), bf16[1408,2048]{1,0:T(8,128)(2,1)}) %all-gather.9.cloned.1.call-update) | async-done | bytes 5767184 | tf_op jit(solution)/shard_map/all_gather | solution.py:67
  244.6 13.0 %collective-permute-done.18.refs_2_ = bf16[256,1024]{1,0:T(8,128)(2,1)S(1)} collective-permute-done((bf16[256,1024]{1,0:T(8,128)(2,1)}, bf16[256,1024]{1,0:T(8,128)(2,1)S(1)}, u32[]{:S(2)}, u32[]{:S(2)}) %collective-permute-start.18) | collective-permute-done | bytes 524320 | tf_op jit(solution)/shard_map/ppermute | solution.py:406
  262.6 21.2 %collective-permute-done.20.refs_4_ = bf16[256,2048]{1,0:T(8,128)(2,1)S(1)} collective-permute-done((bf16[256,2048]{1,0:T(8,128)(2,1)S(1)}, bf16[256,2048]{1,0:T(8,128)(2,1)S(1)}, u32[]{:S(2)}, u32[]{:S(2)}) %collective-permute-start.20) | collective-permute-done | bytes 1048608 | tf_op jit(solution)/shard_map/ppermute | solution.py:406
  287.7 22.5 %gate_up.1 = (f32[1024,1536]{1,0:T(8,128)}, f32[1024,1536]{1,0:T(8,128)}, bf16[1024,768]{1,0:T(8,128)(2,1)}, bf16[1024,768]{1,0:T(8,128)(2,1)}, bf16[1024,2048]{1,0:T(8,128)(2,1)}) custom-call(bf16[512,1024]{1,0:T(8,128)(2,1)} %copy-done.19, bf16[256,1024]{1,0:T(8,128)(2,1)} %copy-done.43, bf16[256,1024]{1,0:T(8,128)(2,1)} %copy-done.44, ...), custom_call_target="tpu_custom_call" | custom-call | flops 1288490240 | bytes 2097152 | tf_op jit(solution)/shard_map/gate_up/pallas_call | solution.py:879
  310.3 5.6 collective-permute-done.23.refs_1_.refs_8_
  315.9 13.6 %down.1 = (bf16[256,2048]{1,0:T(8,128)(2,1)}, bf16[256,2048]{1,0:T(8,128)(2,1)}, bf16[512,1024]{1,0:T(8,128)(2,1)}, bf16[512,1024]{1,0:T(8,128)(2,1)}) custom-call(bf16[1024,768]{1,0:T(8,128)(2,1)} %get-tuple-element.143.own_ref.left_ref, bf16[1024,768]{1,0:T(8,128)(2,1)} %get-tuple-element.126.other_ref, ...), custom_call_target="tpu_custom_call" | custom-call | flops 644245120 | bytes 2097152 | tf_op jit(solution)/shard_map/down/pallas_call | solution.py:879
  334.6 20.4 %collective-permute-done.24 = bf16[256,2048]{1,0:T(8,128)(2,1)} collective-permute-done((bf16[256,2048]{1,0:T(8,128)(2,1)}, bf16[256,2048]{1,0:T(8,128)(2,1)}, u32[]{:S(2)}, u32[]{:S(2)}) %collective-permute-start.24) | collective-permute-done | bytes 1048608 | tf_op jit(solution)/shard_map/ppermute | solution.py:406
  362.6 7.1 collective-permute-done.26
  378.8 9.4 %collective-permute-done.29.refs_2_ = bf16[256,1024]{1,0:T(8,128)(2,1)S(1)} collective-permute-done((bf16[256,1024]{1,0:T(8,128)(2,1)S(1)}, bf16[256,1024]{1,0:T(8,128)(2,1)S(1)}, u32[]{:S(2)}, u32[]{:S(2)}) %collective-permute-start.29) | collective-permute-done | bytes 524320 | tf_op jit(solution)/shard_map/ppermute | solution.py:406
  396.3 5.8 pad_maximum_fusion
  404.2 12.3 %collective-permute-done.31.refs_4_ = bf16[256,2048]{1,0:T(8,128)(2,1)S(1)} collective-permute-done((bf16[256,2048]{1,0:T(8,128)(2,1)S(1)}, bf16[256,2048]{1,0:T(8,128)(2,1)S(1)}, u32[]{:S(2)}, u32[]{:S(2)}) %collective-permute-start.31) | collective-permute-done | bytes 1048608 | tf_op jit(solution)/shard_map/ppermute | solution.py:406
  418.8 16.9 %down_back.1 = (bf16[1024,1536]{1,0:T(8,128)(2,1)}, bf16[1024,1536]{1,0:T(8,128)(2,1)}, bf16[1024,2048]{1,0:T(8,128)(2,1)}) custom-call(bf16[512,1024]{1,0:T(8,128)(2,1)} %copy-done.13, bf16[256,1024]{1,0:T(8,128)(2,1)} %copy-done.42, bf16[256,1024]{1,0:T(8,128)(2,1)} %copy-done.41, bf16[512,1024]{1,0:T(8,128)(2,1)} %copy-done.56, ...), custom_call_target="tpu_custom_call" | custom-call | flops 644245120 | bytes 2097152 | tf_op jit(solution)/shard_map/down_back/pallas_call | solution.py:879
  436.3 7.0 collective-permute-done.37.right_far_ref
  443.3 12.8 %outer.2 = bf16[704,2048]{1,0:T(8,128)(2,1)} custom-call(bf16[1024,768]{1,0:T(8,128)(2,1)} %get-tuple-element.143.own_ref.left_ref, bf16[1024,768]{1,0:T(8,128)(2,1)} %copy-done.48, bf16[1024,2048]{1,0:T(8,128)(2,1)} %get-tuple-element.145.right_ref, bf16[1024,2048]{1,0:T(8,128)(2,1)} %collective-permute-done.37.right_far_ref), custom_call_target="tpu_custom_call" | custom-call | flops 644245120 | bytes 1677721 | tf_op jit(solution)/shard_map/outer/pallas_call | solution.py:940
  456.2 21.2 %gate_up_back.1 = (bf16[256,2048]{1,0:T(8,128)(2,1)}, bf16[256,2048]{1,0:T(8,128)(2,1)}, bf16[512,1024]{1,0:T(8,128)(2,1)}, bf16[512,1024]{1,0:T(8,128)(2,1)}) custom-call(bf16[1024,1536]{1,0:T(8,128)(2,1)} %get-tuple-element.151.own_ref.left_ref, bf16[1024,1536]{1,0:T(8,128)(2,1)} %get-tuple-element.147.other_ref, ...), custom_call_target="tpu_custom_call" | custom-call | flops 1288490240 | bytes 2097152 | tf_op jit(solution)/shard_map/gate_up_back/pallas_call | solution.py:879
  479.9 21.3 %outer.3 = bf16[1408,2048]{1,0:T(8,128)(2,1)} custom-call(bf16[1024,1536]{1,0:T(8,128)(2,1)} %get-tuple-element.151.own_ref.left_ref, bf16[1024,1536]{1,0:T(8,128)(2,1)} %collective-permute-done.36.left_far_ref, bf16[1024,2048]{1,0:T(8,128)(2,1)} %get-tuple-element.153.right_ref, bf16[1024,2048]{1,0:T(8,128)(2,1)} %copy-done.25), custom_call_target="tpu_custom_call" | custom-call | flops 1288490240 | bytes 1677721 | tf_op jit(solution)/shard_map/outer/pallas_call | solution.py:940
  503.8 6.5 reduce-scatter.6.cloned.1.call-done
  516.4 9.0 %collective-permute-done.40 = bf16[256,1024]{1,0:T(8,128)(2,1)S(1)} collective-permute-done((bf16[256,1024]{1,0:T(8,128)(2,1)S(1)}, bf16[256,1024]{1,0:T(8,128)(2,1)S(1)}, u32[]{:S(2)}, u32[]{:S(2)}) %collective-permute-start.40) | collective-permute-done | bytes 524320 | tf_op jit(solution)/shard_map/ppermute | solution.py:406
  539.5 6.5 project.3
  554.5 16.3 %collective-permute-done.43 = bf16[512,1024]{1,0:T(8,128)(2,1)S(1)} collective-permute-done((bf16[512,1024]{1,0:T(8,128)(2,1)}, bf16[512,1024]{1,0:T(8,128)(2,1)S(1)}, u32[]{:S(2)}, u32[]{:S(2)}) %collective-permute-start.43) | collective-permute-done | bytes 1048608 | tf_op jit(solution)/shard_map/ppermute | solution.py:406
  570.8 5.6 collective-permute-done.45
  577.8 14.7 %attend_back.1 = (bf16[512,1024]{1,0:T(8,128)(2,1)}, bf16[2048,512]{1,0:T(8,128)(2,1)}) custom-call(s32[8]{0:T(128)} %stack.47.flags, bf16[512,1024]{1,0:T(8,128)(2,1)} %copy-done.23, bf16[512,1024]{1,0:T(8,128)(2,1)} %add_convert_fusion.1.do_ref, f32[8,1,512]{2,1,0:T(1,128)} %get-tuple-element.164.lse_ref, f32[64,512]{1,0:T(8,128)} %get-tuple-element.313.cos_ref, ...), custom_call_target="tpu_custom_call" | custom-call | flops 805306368 | bytes 1258291 | tf_op jit(solution)/shard_map/attend_back/pallas_call | solution.py:600
  592.4 22.7 %reduce-scatter.8.cloned.1.call-done = bf16[352,2048]{1,0:T(8,128)(2,1)} async-done(((bf16[1408,2048]{1,0:T(8,128)(2,1)}), bf16[352,2048]{1,0:T(8,128)(2,1)}) %reduce-scatter.8.cloned.1.call-update) | async-done | bytes 1441808 | tf_op jit(solution)/shard_map/reduce_scatter | solution.py:1208
  617.5 4.6 convolution_convert_fusion.1
  625.3 8.7 %collective-permute-done.50 = bf16[176,1024]{1,0:T(8,128)(2,1)S(1)} collective-permute-done((bf16[176,1024]{1,0:T(8,128)(2,1)S(1)}, bf16[176,1024]{1,0:T(8,128)(2,1)S(1)}, u32[]{:S(2)}, u32[]{:S(2)}) %collective-permute-start.50) | collective-permute-done | bytes 360480 | tf_op jit(solution)/shard_map/ppermute | solution.py:406
  637.2 11.1 %collective-permute-done.48 = bf16[256,2048]{1,0:T(8,128)(2,1)S(1)} collective-permute-done((bf16[256,2048]{1,0:T(8,128)(2,1)S(1)}, bf16[256,2048]{1,0:T(8,128)(2,1)S(1)}, u32[]{:S(2)}, u32[]{:S(2)}) %collective-permute-start.48) | collective-permute-done | bytes 1048608 | tf_op jit(solution)/shard_map/ppermute | solution.py:406
  650.3 13.5 %collective-permute-done.49 = bf16[256,1024]{1,0:T(8,128)(2,1)S(1)} collective-permute-done((bf16[256,1024]{1,0:T(8,128)(2,1)S(1)}, bf16[256,1024]{1,0:T(8,128)(2,1)S(1)}, u32[]{:S(2)}, u32[]{:S(2)}) %collective-permute-start.49) | collective-permute-done | bytes 524320 | tf_op jit(solution)/shard_map/ppermute | solution.py:406
  668.6 4.7 convolution_convert_fusion
  680.5 12.2 %collective-permute-done.54.other_ref = bf16[512,1024]{1,0:T(8,128)(2,1)} collective-permute-done((bf16[512,1024]{1,0:T(8,128)(2,1)S(1)}, bf16[512,1024]{1,0:T(8,128)(2,1)}, u32[]{:S(2)}, u32[]{:S(2)}) %collective-permute-start.54) | collective-permute-done | bytes 1048608 | tf_op jit(solution)/shard_map/ppermute | solution.py:406
  696.6 7.3 collective-permute-done.56.other_ref
  704.0 5.0 collective-permute-done.55
  713.2 6.5 merge.3
  719.6 5.7 key_value_back.1
  725.3 19.6 %collective-permute-done.61.refs_2_ = bf16[704,1024]{1,0:T(8,128)(2,1)} collective-permute-done((bf16[704,1024]{1,0:T(8,128)(2,1)S(1)}, bf16[704,1024]{1,0:T(8,128)(2,1)}, u32[]{:S(2)}, u32[]{:S(2)}) %collective-permute-start.61) | collective-permute-done | bytes 1441824 | tf_op jit(solution)/shard_map/ppermute | solution.py:406
  762.6 5.0 settle.2
  767.6 8.1 %settle.3 = (f32[1024,1408]{1,0:T(8,128)}, f32[1024,1408]{1,0:T(8,128)}) custom-call(s32[2]{0:T(128)} %pad_add_fusion.3.scalars, bf16[704,1024]{1,0:T(8,128)(2,1)} %copy-done.21, bf16[704,1024]{1,0:T(8,128)(2,1)} %collective-permute-done.60.refs_1_, bf16[704,1024]{1,0:T(8,128)(2,1)} %collective-permute-done.61.refs_2_, ...), custom_call_target="tpu_custom_call" | custom-call | flops 144179 | bytes 1730150 | tf_op jit(solution)/shard_map/settle/pallas_call | solution.py:974
  776.3 4.3 fusion.8
  784.8 5.2 finish.1
  (435 shorter events, 219.8 us)
Async XLA Ops:
  7.2 66.4 %all-gather.5.cloned.1.call-start = ((), (), s32[]{:S(2)}) async-start(), calls=%async_computation.5 | async-start | bytes 2621440 | tf_op jit(solution)/shard_map/all_gather | solution.py:67
  10.4 134.7 %all-gather.7.cloned.1.call-start = ((), (), s32[]{:S(2)}) async-start(), calls=%async_computation.6 | async-start | bytes 2621440 | tf_op jit(solution)/shard_map/all_gather | solution.py:67
  10.9 16.3 %collective-permute-start.1 = (bf16[128,1024]{1,0:T(8,128)(2,1)S(1)}, bf16[128,1024]{1,0:T(8,128)(2,1)S(1)}, u32[]{:S(2)}, u32[]{:S(2)}) collective-permute-start(bf16[128,1024]{1,0:T(8,128)(2,1)S(1)} %select_bitcast_fusion), channel_id=1, source_target_pairs={{0,2},{2,0},{4,6},{6,4},{1,3},{3,1},{5,7},{7,5},{8,10},{10,8},{12,... | collective-permute-start | bytes 786440 | tf_op jit(solution)/shard_map/ppermute | solution.py:406
  13.9 26.0 %collective-permute-start.2 = (bf16[128,1024]{1,0:T(8,128)(2,1)S(1)}, bf16[128,1024]{1,0:T(8,128)(2,1)S(1)}, u32[]{:S(2)}, u32[]{:S(2)}) collective-permute-start(bf16[128,1024]{1,0:T(8,128)(2,1)S(1)} %select_bitcast_fusion), channel_id=1, source_target_pairs={{0,4},{2,6},{4,0},{6,2},{1,5},{3,7},{5,1},{7,3},{8,12},{10,14},{12... | collective-permute-start | bytes 786440 | tf_op jit(solution)/shard_map/ppermute | solution.py:406
  16.5 26.4 %collective-permute-start.3 = (bf16[128,1024]{1,0:T(8,128)(2,1)S(1)}, bf16[128,1024]{1,0:T(8,128)(2,1)S(1)}, u32[]{:S(2)}, u32[]{:S(2)}) collective-permute-start(bf16[128,1024]{1,0:T(8,128)(2,1)S(1)} %select_bitcast_fusion), channel_id=1, source_target_pairs={{0,6},{2,4},{4,2},{6,0},{1,7},{3,5},{5,3},{7,1},{8,14},{10,12},{12... | collective-permute-start | bytes 786440 | tf_op jit(solution)/shard_map/ppermute | solution.py:406
  24.0 27.2 %collective-permute-start.5 = (bf16[528,1024]{1,0:T(8,128)(2,1)}, bf16[528,1024]{1,0:T(8,128)(2,1)}, u32[]{:S(2)}, u32[]{:S(2)}) collective-permute-start(bf16[528,1024]{1,0:T(8,128)(2,1)} %pad_maximum_fusion.7), channel_id=1, source_target_pairs={{0,1},{1,0},{2,3},{3,2},{4,5},{5,4},{6,7},{7,6},{8,9},{9,8},{10,11... | collective-permute-start | bytes 3244040 | tf_op jit(solution)/shard_map/ppermute | solution.py:406
  26.0 23.3 %collective-permute-start = (f32[512]{0:T(512)S(1)}, f32[512]{0:T(512)S(1)}, u32[]{:S(2)}, u32[]{:S(2)}) collective-permute-start(f32[512]{0:T(512)S(1)} %fusion.1), channel_id=1, source_target_pairs={{0,1},{1,0},{2,3},{3,2},{4,5},{5,4},{6,7},{7,6},{8,9},{9,8},{10,11... | collective-permute-start | bytes 6152 | tf_op jit(solution)/shard_map/ppermute | solution.py:406
  44.0 16.3 %collective-permute-start.7 = (f32[1]{0:T(128)}, f32[1]{0:T(128)}, u32[]{:S(2)}, u32[]{:S(2)}) collective-permute-start(f32[1]{0:T(128)} %bitcast.18), channel_id=1, source_target_pairs={{0,8},{8,0},{16,24},{24,16},{1,9},{9,1},{17,25},{25,17},{2,10},{10... | collective-permute-start | bytes 20 | tf_op jit(solution)/shard_map/ppermute | solution.py:406
  76.6 164.2 %all-gather.9.cloned.1.call-start = ((), (), s32[]{:S(2)}) async-start(), calls=%async_computation.7 | async-start | bytes 7208960 | tf_op jit(solution)/shard_map/all_gather | solution.py:67
  78.1 25.2 %collective-permute-start.10 = (bf16[512,1024]{1,0:T(8,128)(2,1)S(1)}, bf16[512,1024]{1,0:T(8,128)(2,1)S(1)}, u32[]{:S(2)}, u32[]{:S(2)}) collective-permute-start(bf16[512,1024]{1,0:T(8,128)(2,1)S(1)} %pad_maximum_fusion.10.refs_0_), channel_id=1, source_target_pairs={{0,16},{8,24},{16,0},{24,8},{1,17},{9,25},{17,1},{25,9},{2,18},{10... | collective-permute-start | bytes 3145736 | tf_op jit(solution)/shard_map/ppermute | solution.py:406
  79.7 27.4 %collective-permute-start.9 = (bf16[512,1024]{1,0:T(8,128)(2,1)S(1)}, bf16[512,1024]{1,0:T(8,128)(2,1)}, u32[]{:S(2)}, u32[]{:S(2)}) collective-permute-start(bf16[512,1024]{1,0:T(8,128)(2,1)S(1)} %pad_maximum_fusion.10.refs_0_), channel_id=1, source_target_pairs={{0,8},{8,0},{16,24},{24,16},{1,9},{9,1},{17,25},{25,17},{2,10},{10... | collective-permute-start | bytes 3145736 | tf_op jit(solution)/shard_map/ppermute | solution.py:406
  117.7 192.6 %all-gather.11.cloned.1.call-start = ((), (), s32[]{:S(2)}) async-start(), calls=%async_computation.8 | async-start | bytes 3604480 | tf_op jit(solution)/shard_map/all_gather | solution.py:67
  118.2 25.3 %collective-permute-start.13 = (bf16[512,1024]{1,0:T(8,128)(2,1)S(1)}, bf16[512,1024]{1,0:T(8,128)(2,1)S(1)}, u32[]{:S(2)}, u32[]{:S(2)}) collective-permute-start(bf16[512,1024]{1,0:T(8,128)(2,1)S(1)} %pad_maximum_fusion.11.refs_0_), channel_id=1, source_target_pairs={{0,16},{8,24},{16,0},{24,8},{1,17},{9,25},{17,1},{25,9},{2,18},{10... | collective-permute-start | bytes 3145736 | tf_op jit(solution)/shard_map/ppermute | solution.py:406
  119.7 25.4 %collective-permute-start.12 = (bf16[512,1024]{1,0:T(8,128)(2,1)}, bf16[512,1024]{1,0:T(8,128)(2,1)}, u32[]{:S(2)}, u32[]{:S(2)}) collective-permute-start(bf16[512,1024]{1,0:T(8,128)(2,1)} %get-tuple-element.109), channel_id=1, source_target_pairs={{0,1},{1,0},{2,3},{3,2},{4,5},{5,4},{6,7},{7,6},{8,9},{9,8},{10,11... | collective-permute-start | bytes 3145736 | tf_op jit(solution)/shard_map/ppermute | solution.py:406
  163.9 25.7 %collective-permute-start.15 = (bf16[512,1024]{1,0:T(8,128)(2,1)}, bf16[512,1024]{1,0:T(8,128)(2,1)S(1)}, u32[]{:S(2)}, u32[]{:S(2)}) collective-permute-start(bf16[512,1024]{1,0:T(8,128)(2,1)} %get-tuple-element.116.own_ref), channel_id=1, source_target_pairs={{0,1},{1,0},{2,3},{3,2},{4,5},{5,4},{6,7},{7,6},{8,9},{9,8},{10,11... | collective-permute-start | bytes 3145736 | tf_op jit(solution)/shard_map/ppermute | solution.py:406
  240.8 45.9 %collective-permute-start.21 = (bf16[1408,2048]{1,0:T(8,128)(2,1)}, bf16[1408,2048]{1,0:T(8,128)(2,1)}, u32[]{:S(2)}, u32[]{:S(2)}) collective-permute-start(bf16[1408,2048]{1,0:T(8,128)(2,1)} %all-gather.9.cloned.1.call-done.refs_5_.refs_0_), channel_id=1, source_target_pairs={{0,8},{8,0},{16,24},{24,16},{1,9},{9,1},{17,25},{25,17},{2,10},{10... | collective-permute-start | bytes 17301512 | tf_op jit(solution)/shard_map/ppermute | solution.py:406
  242.9 267.3 %reduce-scatter.6.cloned.1.call-start = ((), (), s32[]{:S(2)}) async-start(), calls=%async_computation.9 | async-start | bytes 3604480 | tf_op jit(solution)/shard_map/reduce_scatter | solution.py:1208
  258.9 24.9 %collective-permute-start.20 = (bf16[256,2048]{1,0:T(8,128)(2,1)S(1)}, bf16[256,2048]{1,0:T(8,128)(2,1)S(1)}, u32[]{:S(2)}, u32[]{:S(2)}) collective-permute-start(bf16[256,2048]{1,0:T(8,128)(2,1)S(1)} %pad_maximum_fusion.13), channel_id=1, source_target_pairs={{0,16},{8,24},{16,0},{24,8},{1,17},{9,25},{17,1},{25,9},{2,18},{10... | collective-permute-start | bytes 3145736 | tf_op jit(solution)/shard_map/ppermute | solution.py:406
  260.5 26.2 %collective-permute-start.19 = (bf16[512,1024]{1,0:T(8,128)(2,1)S(1)}, bf16[512,1024]{1,0:T(8,128)(2,1)S(1)}, u32[]{:S(2)}, u32[]{:S(2)}) collective-permute-start(bf16[512,1024]{1,0:T(8,128)(2,1)S(1)} %pad_maximum_fusion.12), channel_id=1, source_target_pairs={{0,1},{1,0},{2,3},{3,2},{4,5},{5,4},{6,7},{7,6},{8,9},{9,8},{10,11... | collective-permute-start | bytes 3145736 | tf_op jit(solution)/shard_map/ppermute | solution.py:406
  262.1 48.1 %collective-permute-start.22 = (bf16[512,1024]{1,0:T(8,128)(2,1)S(1)}, bf16[512,1024]{1,0:T(8,128)(2,1)}, u32[]{:S(2)}, u32[]{:S(2)}) collective-permute-start(bf16[512,1024]{1,0:T(8,128)(2,1)S(1)} %copy-done.5), channel_id=1, source_target_pairs={{0,1},{1,0},{2,3},{3,2},{4,5},{5,4},{6,7},{7,6},{8,9},{9,8},{10,11... | collective-permute-start | bytes 3145736 | tf_op jit(solution)/shard_map/ppermute | solution.py:406
  329.5 25.6 %collective-permute-start.24 = (bf16[256,2048]{1,0:T(8,128)(2,1)}, bf16[256,2048]{1,0:T(8,128)(2,1)}, u32[]{:S(2)}, u32[]{:S(2)}) collective-permute-start(bf16[256,2048]{1,0:T(8,128)(2,1)} %get-tuple-element.130), channel_id=1, source_target_pairs={{0,16},{8,24},{16,0},{24,8},{1,17},{9,25},{17,1},{25,9},{2,18},{10... | collective-permute-start | bytes 3145736 | tf_op jit(solution)/shard_map/ppermute | solution.py:406
  330.1 25.2 %collective-permute-start.25 = (bf16[512,1024]{1,0:T(8,128)(2,1)}, bf16[512,1024]{1,0:T(8,128)(2,1)}, u32[]{:S(2)}, u32[]{:S(2)}) collective-permute-start(bf16[512,1024]{1,0:T(8,128)(2,1)} %get-tuple-element.131), channel_id=1, source_target_pairs={{0,1},{1,0},{2,3},{3,2},{4,5},{5,4},{6,7},{7,6},{8,9},{9,8},{10,11... | collective-permute-start | bytes 3145736 | tf_op jit(solution)/shard_map/ppermute | solution.py:406
  334.5 67.5 %collective-permute-start.35 = (bf16[1024,2048]{1,0:T(8,128)(2,1)S(1)}, bf16[1024,2048]{1,0:T(8,128)(2,1)S(1)}, u32[]{:S(2)}, u32[]{:S(2)}) collective-permute-start(bf16[1024,2048]{1,0:T(8,128)(2,1)S(1)} %copy-done.24), channel_id=1, source_target_pairs={{0,8},{8,0},{16,24},{24,16},{1,9},{9,1},{17,25},{25,17},{2,10},{10... | collective-permute-start | bytes 12582920 | tf_op jit(solution)/shard_map/ppermute | solution.py:406
  362.5 33.8 %collective-permute-start.32 = (bf16[512,2048]{1,0:T(8,128)(2,1)S(1)}, bf16[512,2048]{1,0:T(8,128)(2,1)S(1)}, u32[]{:S(2)}, u32[]{:S(2)}) collective-permute-start(bf16[512,2048]{1,0:T(8,128)(2,1)S(1)} %pad_maximum_fusion.2), channel_id=1, source_target_pairs={{0,8},{8,0},{16,24},{24,16},{1,9},{9,1},{17,25},{25,17},{2,10},{10... | collective-permute-start | bytes 6291464 | tf_op jit(solution)/shard_map/ppermute | solution.py:406
  377.4 15.8 %collective-permute-start.33 = (bf16[512,1024]{1,0:T(8,128)(2,1)S(1)}, bf16[512,1024]{1,0:T(8,128)(2,1)S(1)}, u32[]{:S(2)}, u32[]{:S(2)}) collective-permute-start(bf16[512,1024]{1,0:T(8,128)(2,1)S(1)} %pad_maximum_fusion.16), channel_id=1, source_target_pairs={{0,8},{8,0},{16,24},{24,16},{1,9},{9,1},{17,25},{25,17},{2,10},{10... | collective-permute-start | bytes 3145736 | tf_op jit(solution)/shard_map/ppermute | solution.py:406
  391.7 24.8 %collective-permute-start.31 = (bf16[256,2048]{1,0:T(8,128)(2,1)S(1)}, bf16[256,2048]{1,0:T(8,128)(2,1)S(1)}, u32[]{:S(2)}, u32[]{:S(2)}) collective-permute-start(bf16[256,2048]{1,0:T(8,128)(2,1)S(1)} %pad_maximum_fusion.15), channel_id=1, source_target_pairs={{0,16},{8,24},{16,0},{24,8},{1,17},{9,25},{17,1},{25,9},{2,18},{10... | collective-permute-start | bytes 3145736 | tf_op jit(solution)/shard_map/ppermute | solution.py:406
  393.3 24.6 %collective-permute-start.30 = (bf16[512,1024]{1,0:T(8,128)(2,1)S(1)}, bf16[512,1024]{1,0:T(8,128)(2,1)S(1)}, u32[]{:S(2)}, u32[]{:S(2)}) collective-permute-start(bf16[512,1024]{1,0:T(8,128)(2,1)S(1)} %pad_maximum_fusion.14), channel_id=1, source_target_pairs={{0,1},{1,0},{2,3},{3,2},{4,5},{5,4},{6,7},{7,6},{8,9},{9,8},{10,11... | collective-permute-start | bytes 3145736 | tf_op jit(solution)/shard_map/ppermute | solution.py:406
  435.8 20.3 %collective-permute-start.36 = (bf16[1024,1536]{1,0:T(8,128)(2,1)}, bf16[1024,1536]{1,0:T(8,128)(2,1)}, u32[]{:S(2)}, u32[]{:S(2)}) collective-permute-start(bf16[1024,1536]{1,0:T(8,128)(2,1)} %get-tuple-element.147.other_ref), channel_id=1, source_target_pairs={{0,8},{8,0},{16,24},{24,16},{1,9},{9,1},{17,25},{25,17},{2,10},{10... | collective-permute-start | bytes 9437192 | tf_op jit(solution)/shard_map/ppermute | solution.py:406
  456.1 159.0 %reduce-scatter.8.cloned.1.call-start = ((), (), s32[]{:S(2)}) async-start(), calls=%async_computation.10 | async-start | bytes 7208960 | tf_op jit(solution)/shard_map/reduce_scatter | solution.py:1208
  477.4 25.6 %collective-permute-start.38 = (bf16[256,2048]{1,0:T(8,128)(2,1)}, bf16[256,2048]{1,0:T(8,128)(2,1)}, u32[]{:S(2)}, u32[]{:S(2)}) collective-permute-start(bf16[256,2048]{1,0:T(8,128)(2,1)} %get-tuple-element.149), channel_id=1, source_target_pairs={{0,16},{8,24},{16,0},{24,8},{1,17},{9,25},{17,1},{25,9},{2,18},{10... | collective-permute-start | bytes 3145736 | tf_op jit(solution)/shard_map/ppermute | solution.py:406
  478.6 25.2 %collective-permute-start.39 = (bf16[512,1024]{1,0:T(8,128)(2,1)}, bf16[512,1024]{1,0:T(8,128)(2,1)}, u32[]{:S(2)}, u32[]{:S(2)}) collective-permute-start(bf16[512,1024]{1,0:T(8,128)(2,1)} %get-tuple-element.150), channel_id=1, source_target_pairs={{0,1},{1,0},{2,3},{3,2},{4,5},{5,4},{6,7},{7,6},{8,9},{9,8},{10,11... | collective-permute-start | bytes 3145736 | tf_op jit(solution)/shard_map/ppermute | solution.py:406
  510.3 154.3 %reduce-scatter.10.cloned.1.call-start = ((), (), s32[]{:S(2)}) async-start(), calls=%async_computation.11 | async-start | bytes 2621440 | tf_op jit(solution)/shard_map/reduce_scatter | solution.py:1208
  546.0 24.8 %collective-permute-start.43 = (bf16[512,1024]{1,0:T(8,128)(2,1)}, bf16[512,1024]{1,0:T(8,128)(2,1)S(1)}, u32[]{:S(2)}, u32[]{:S(2)}) collective-permute-start(bf16[512,1024]{1,0:T(8,128)(2,1)} %get-tuple-element.159), channel_id=1, source_target_pairs={{0,1},{1,0},{2,3},{3,2},{4,5},{5,4},{6,7},{7,6},{8,9},{9,8},{10,11... | collective-permute-start | bytes 3145736 | tf_op jit(solution)/shard_map/ppermute | solution.py:406
  551.8 24.6 %collective-permute-start.45 = (bf16[512,1024]{1,0:T(8,128)(2,1)S(1)}, bf16[512,1024]{1,0:T(8,128)(2,1)}, u32[]{:S(2)}, u32[]{:S(2)}) collective-permute-start(bf16[512,1024]{1,0:T(8,128)(2,1)S(1)} %pad_maximum_fusion.17), channel_id=1, source_target_pairs={{0,16},{8,24},{16,0},{24,8},{1,17},{9,25},{17,1},{25,9},{2,18},{10... | collective-permute-start | bytes 3145736 | tf_op jit(solution)/shard_map/ppermute | solution.py:406
  615.1 94.1 %reduce-scatter.12.cloned.1.call-start = ((), (), s32[]{:S(2)}) async-start(), calls=%async_computation.12 | async-start | bytes 1310720 | tf_op jit(solution)/shard_map/reduce_scatter | solution.py:1208
  622.2 26.1 %collective-permute-start.48 = (bf16[256,2048]{1,0:T(8,128)(2,1)S(1)}, bf16[256,2048]{1,0:T(8,128)(2,1)S(1)}, u32[]{:S(2)}, u32[]{:S(2)}) collective-permute-start(bf16[256,2048]{1,0:T(8,128)(2,1)S(1)} %slice.519), channel_id=1, source_target_pairs={{0,16},{8,24},{16,0},{24,8},{1,17},{9,25},{17,1},{25,9},{2,18},{10... | collective-permute-start | bytes 3145736 | tf_op jit(solution)/shard_map/ppermute | solution.py:406
  634.1 29.7 %collective-permute-start.51 = (bf16[352,1024]{1,0:T(8,128)(2,1)S(1)}, bf16[352,1024]{1,0:T(8,128)(2,1)}, u32[]{:S(2)}, u32[]{:S(2)}) collective-permute-start(bf16[352,1024]{1,0:T(8,128)(2,1)S(1)} %pad_maximum_fusion.19.refs_0_), channel_id=1, source_target_pairs={{0,16},{8,24},{16,0},{24,8},{1,17},{9,25},{17,1},{25,9},{2,18},{10... | collective-permute-start | bytes 2162696 | tf_op jit(solution)/shard_map/ppermute | solution.py:406
  635.7 28.1 %collective-permute-start.46 = (bf16[352,1024]{1,0:T(8,128)(2,1)S(1)}, bf16[352,1024]{1,0:T(8,128)(2,1)}, u32[]{:S(2)}, u32[]{:S(2)}) collective-permute-start(bf16[352,1024]{1,0:T(8,128)(2,1)S(1)} %get-tuple-element.273), channel_id=1, source_target_pairs={{0,1},{1,0},{2,3},{3,2},{4,5},{5,4},{6,7},{7,6},{8,9},{9,8},{10,11... | collective-permute-start | bytes 2162696 | tf_op jit(solution)/shard_map/ppermute | solution.py:406
  648.8 15.0 %collective-permute-start.49 = (bf16[256,1024]{1,0:T(8,128)(2,1)S(1)}, bf16[256,1024]{1,0:T(8,128)(2,1)S(1)}, u32[]{:S(2)}, u32[]{:S(2)}) collective-permute-start(bf16[256,1024]{1,0:T(8,128)(2,1)S(1)} %slice.520), channel_id=1, source_target_pairs={{0,1},{1,0},{2,3},{3,2},{4,5},{5,4},{6,7},{7,6},{8,9},{9,8},{10,11... | collective-permute-start | bytes 1572872 | tf_op jit(solution)/shard_map/ppermute | solution.py:406
  666.6 26.1 %collective-permute-start.54 = (bf16[512,1024]{1,0:T(8,128)(2,1)S(1)}, bf16[512,1024]{1,0:T(8,128)(2,1)}, u32[]{:S(2)}, u32[]{:S(2)}) collective-permute-start(bf16[512,1024]{1,0:T(8,128)(2,1)S(1)} %copy-done.26), channel_id=1, source_target_pairs={{0,1},{1,0},{2,3},{3,2},{4,5},{5,4},{6,7},{7,6},{8,9},{9,8},{10,11... | collective-permute-start | bytes 3145736 | tf_op jit(solution)/shard_map/ppermute | solution.py:406
  674.3 18.5 %collective-permute-start.53 = (bf16[128,2048]{1,0:T(8,128)(2,1)}, bf16[128,2048]{1,0:T(8,128)(2,1)}, u32[]{:S(2)}, u32[]{:S(2)}) collective-permute-start(bf16[128,2048]{1,0:T(8,128)(2,1)} %bitcast.31), channel_id=1, source_target_pairs={{0,16},{8,24},{16,0},{24,8},{1,17},{9,25},{17,1},{25,9},{2,18},{10... | collective-permute-start | bytes 1572872 | tf_op jit(solution)/shard_map/ppermute | solution.py:406
  678.7 25.3 %collective-permute-start.56 = (bf16[512,512]{1,0:T(8,128)(2,1)}, bf16[512,512]{1,0:T(8,128)(2,1)}, u32[]{:S(2)}, u32[]{:S(2)}) collective-permute-start(bf16[512,512]{1,0:T(8,128)(2,1)} %copy-done.47), channel_id=1, source_target_pairs={{0,1},{1,0},{2,3},{3,2},{4,5},{5,4},{6,7},{7,6},{8,9},{9,8},{10,11... | collective-permute-start | bytes 1572872 | tf_op jit(solution)/shard_map/ppermute | solution.py:406
  680.2 73.7 %reduce-scatter.14.cloned.1.call-start = ((), (), s32[]{:S(2)}) async-start(), calls=%async_computation.13 | async-start | bytes 1966080 | tf_op jit(solution)/shard_map/reduce_scatter | solution.py:1208
  693.9 15.1 %collective-permute-start.55 = (bf16[128,1024]{1,0:T(8,128)(2,1)S(1)}, bf16[128,1024]{1,0:T(8,128)(2,1)S(1)}, u32[]{:S(2)}, u32[]{:S(2)}) collective-permute-start(bf16[128,1024]{1,0:T(8,128)(2,1)S(1)} %slice.533), channel_id=1, source_target_pairs={{0,1},{1,0},{2,3},{3,2},{4,5},{5,4},{6,7},{7,6},{8,9},{9,8},{10,11... | collective-permute-start | bytes 786440 | tf_op jit(solution)/shard_map/ppermute | solution.py:406
  711.6 33.3 %collective-permute-start.61 = (bf16[704,1024]{1,0:T(8,128)(2,1)S(1)}, bf16[704,1024]{1,0:T(8,128)(2,1)}, u32[]{:S(2)}, u32[]{:S(2)}) collective-permute-start(bf16[704,1024]{1,0:T(8,128)(2,1)S(1)} %pad_maximum_fusion.6.refs_0_), channel_id=1, source_target_pairs={{0,16},{8,24},{16,0},{24,8},{1,17},{9,25},{17,1},{25,9},{2,18},{10... | collective-permute-start | bytes 4325384 | tf_op jit(solution)/shard_map/ppermute | solution.py:406
  713.2 54.5 %collective-permute-start.60 = (bf16[704,1024]{1,0:T(8,128)(2,1)S(1)}, bf16[704,1024]{1,0:T(8,128)(2,1)}, u32[]{:S(2)}, u32[]{:S(2)}) collective-permute-start(bf16[704,1024]{1,0:T(8,128)(2,1)S(1)} %pad_maximum_fusion.6.refs_0_), channel_id=1, source_target_pairs={{0,8},{8,0},{16,24},{24,16},{1,9},{9,1},{17,25},{25,17},{2,10},{10... | collective-permute-start | bytes 4325384 | tf_op jit(solution)/shard_map/ppermute | solution.py:406
  744.9 22.7 %collective-permute-start.62 = (bf16[704,1024]{1,0:T(8,128)(2,1)}, bf16[704,1024]{1,0:T(8,128)(2,1)}, u32[]{:S(2)}, u32[]{:S(2)}) collective-permute-start(bf16[704,1024]{1,0:T(8,128)(2,1)} %collective-permute-done.61.refs_2_), channel_id=1, source_target_pairs={{0,8},{8,0},{16,24},{24,16},{1,9},{9,1},{17,25},{25,17},{2,10},{10... | collective-permute-start | bytes 4325384 | tf_op jit(solution)/shard_map/ppermute | solution.py:406
  756.4 19.3 %collective-permute-start.57 = (bf16[320,1024]{1,0:T(8,128)(2,1)}, bf16[320,1024]{1,0:T(8,128)(2,1)}, u32[]{:S(2)}, u32[]{:S(2)}) collective-permute-start(bf16[320,1024]{1,0:T(8,128)(2,1)} %constant_dynamic-update-slice_fusion.2.refs_0_), channel_id=1, source_target_pairs={{0,16},{8,24},{16,0},{24,8},{1,17},{9,25},{17,1},{25,9},{2,18},{10... | collective-permute-start | bytes 1966088 | tf_op jit(solution)/shard_map/ppermute | solution.py:406
  (110 other events, 1022.9 us)
Sparse Core Ops, SparseCore 0:
  10.6 62.9 all-gather.4
  76.8 56.4 all-gather.6
  135.4 105.4 all-gather.8
  243.1 57.5 all-gather.10
  456.2 53.9 reduce-scatter.5
  513.0 102.0 reduce-scatter.7
  618.0 44.3 reduce-scatter.9
  680.3 26.4 reduce-scatter.11
  710.5 36.1 reduce-scatter.13
